TPU v7x, 512 devices: a whole 4x4x16 slice. The times are simulated.
512 devices in a mesh: blk: 64 (over z, y_lo, core), head: 8 (over y_hi, x).
Axes of the slice: x: 4, y: 4 (y_hi: 2, y_lo: 2; y = y_hi * 2 + y_lo), z: 16, core: 2. Of those that a mesh axis runs over, the one named last changes fastest.
Arguments:
- queries: bfloat16 [12288, 4096], P(('blk', 'head'))
- key_rows: bfloat16 [12288, 1024], P(('blk', 'head'))
- value_rows: bfloat16 [12288, 1024], P(('blk', 'head')), may hold values from -6 to 6
- visit_ids: int32 [12288], replicated, may hold values from 0 to 3, as said below
- span_order: int32 [64], replicated, may hold values from 0 to 63, each once
Outputs:
- attended: bfloat16 [12288, 4096], P(('blk', 'head'))
Inputs may be any that keep to these rules, and one draw needn't show every extreme that they name: `visit_ids`: visit ids never fall along time; every one of the 4 visits has events and begins at an even position. `span_order`: each block index holds a different block of 192 consecutive events.
All inputs are finite; a program needn't handle non-finite values.
Results may differ from a plain program's by a relative error of at most 0.0049.
Values may be sent and summed in bfloat16 or wider, within the bound.
No kernel may reach another device: no remote copies, remote signals or barrier semaphores. Data moves between devices by JAX's collectives and lax.ppermute only.
A program may use at most 64 MiB of HBM per device.

v0:
```python
import jax
import jax.numpy as jnp
from jax import lax
from jax.experimental import pallas as pl
from jax.experimental.pallas import tpu as pltpu
from jax.sharding import Mesh, PartitionSpec as P

HEADS = 32
KV_HEADS = 8
HEAD_DIM = 128
GROUP = HEADS // KV_HEADS
SPAN_ROWS = 192
PIECE = 24
PARTS = SPAN_ROWS // PIECE
VISITS = 4
SPANS = 64
HALF = SPANS // 2
KEYS = HALF * SPAN_ROWS
PER_TILE = 4
TILE = PER_TILE * SPAN_ROWS
TILES = KEYS // TILE
SOURCES = 8
ROWS = GROUP * PIECE
SCALE_LOG2 = HEAD_DIM ** (-0.5) * 1.4426950408889634
NOTHING = -3e38

ORDER = 0
COUNT = 64
SORTED = COUNT + 65
START = SORTED + HALF
YLO = START + VISITS
CORE = YLO + 1
ZLO = YLO + 2
FIRST = YLO + 3


def gather_keys(info, own_ref, other_ref, k_buf, v_buf, sems):
    core, zlo = info[CORE], info[ZLO]
    k_pieces = k_buf.reshape(HALF * PARTS, PIECE, HEAD_DIM)
    v_pieces = v_buf.reshape(HALF * PARTS, PIECE, HEAD_DIM)

    def each(act):
        def step(i, carry):
            k, half = i // 2, i % 2
            for src, side in ((own_ref, core), (other_ref, 1 - core)):
                span = info[ORDER + (k * 2 + zlo) * 4 + half * 2 + side]
                rank = info[COUNT + span]
                for which, buf in ((0, k_pieces), (1, v_pieces)):
                    act(
                        pltpu.make_async_copy(
                            src.at[pl.ds(half * PARTS, PARTS), k, which],
                            buf.at[pl.ds(rank * PARTS, PARTS)],
                            sems.at[which, (k * 2 + half) * 2 + side],
                        )
                    )
            return carry

        lax.fori_loop(0, 2 * SOURCES, step, 0)

    each(lambda c: c.start())
    each(lambda c: c.wait())


def attend_sources(info, side, q_ref, k_buf, v_buf, s_buf, put):
    ylo, core, first = info[YLO], info[CORE], info[FIRST]
    inside = lax.rem(lax.broadcasted_iota(jnp.int32, (ROWS, HEAD_DIM), 0), PIECE)
    lane = lax.broadcasted_iota(jnp.int32, (1, HEAD_DIM), 1)

    def start_of(pos):
        low = jnp.zeros_like(pos)
        for v in range(1, VISITS):
            low = jnp.where(info[START + v] <= pos, info[START + v], low)
        return low

    def one_source(n, carry):
        span = info[ORDER + (n * 2 + side) * 4 + ylo * 2 + core]
        p0 = span * SPAN_ROWS + first
        pos = p0 + inside
        low = start_of(pos)
        low0 = start_of(p0)
        tile_a = info[COUNT + low0 // SPAN_ROWS] // PER_TILE
        tile_b = (info[COUNT + span + 1] + PER_TILE - 1) // PER_TILE
        q = q_ref[n].astype(jnp.float32).reshape(ROWS, HEAD_DIM).astype(jnp.bfloat16)

        def scores(j, best):
            base = pl.multiple_of(j * TILE, TILE)
            s = lax.dot_general(
                q,
                k_buf[pl.ds(base, TILE), :],
                (((1,), (1,)), ((), ())),
                preferred_element_type=jnp.float32,
            )
            at = [
                info[SORTED + j * PER_TILE + u] * SPAN_ROWS - u * SPAN_ROWS
                for u in range(PER_TILE)
            ]
            for c in range(TILE // HEAD_DIM):
                lo_u = c * HEAD_DIM // SPAN_ROWS
                hi_u = (c * HEAD_DIM + HEAD_DIM - 1) // SPAN_ROWS
                key = lane + c * HEAD_DIM
                if lo_u == hi_u:
                    key = key + at[lo_u]
                else:
                    key = key + jnp.where(key < hi_u * SPAN_ROWS, at[lo_u], at[hi_u])
                part = jnp.where(
                    (key >= low) & (key <= pos),
                    s[:, c * HEAD_DIM : (c + 1) * HEAD_DIM],
                    -jnp.inf,
                )
                s_buf[j, :, c * HEAD_DIM : (c + 1) * HEAD_DIM] = part
                best = jnp.maximum(best, part)
            return best

        best = lax.fori_loop(
            tile_a, tile_b, scores, jnp.full((ROWS, HEAD_DIM), -jnp.inf, jnp.float32)
        )
        top = jnp.max(best, axis=1, keepdims=True)
        some = top > -jnp.inf
        top = jnp.where(some, top, 0.0)

        def mix(j, state):
            total, acc = state
            base = pl.multiple_of(j * TILE, TILE)
            w = jnp.exp2((s_buf[j] - top) * SCALE_LOG2)
            for c in range(TILE // HEAD_DIM):
                total = total + w[:, c * HEAD_DIM : (c + 1) * HEAD_DIM]
            acc = acc + jnp.dot(
                w.astype(jnp.bfloat16),
                v_buf[pl.ds(base, TILE), :],
                preferred_element_type=jnp.float32,
            )
            return total, acc

        zero = jnp.zeros((ROWS, HEAD_DIM), jnp.float32)
        total, acc = lax.fori_loop(tile_a, tile_b, mix, (zero, zero))
        total = jnp.sum(total, axis=1, keepdims=True)
        safe = jnp.where(some, total, 1.0)
        mass = jnp.where(some, top * SCALE_LOG2 + jnp.log2(safe), NOTHING)
        put(n, (acc / safe).reshape(GROUP, PIECE, HEAD_DIM), mass)
        return carry

    lax.fori_loop(0, SOURCES, one_source, 0)


def far_kernel(info, q_ref, own_ref, other_ref, o_ref, k_buf, v_buf, s_buf, sems):
    gather_keys(info, own_ref, other_ref, k_buf, v_buf, sems)
    lane = lax.broadcasted_iota(jnp.int32, (PIECE, HEAD_DIM), 1)

    def put(n, out, mass):
        o_ref[n, :GROUP] = out.astype(jnp.bfloat16)
        packed = jnp.zeros((PIECE, HEAD_DIM), jnp.float32)
        high = mass.astype(jnp.bfloat16).astype(jnp.float32)
        rest = mass - high
        middle = rest.astype(jnp.bfloat16).astype(jnp.float32)
        pieces = (high, middle, rest - middle)
        for g in range(GROUP):
            for i, piece in enumerate(pieces):
                packed = jnp.where(
                    lane == 3 * g + i, piece[g * PIECE : (g + 1) * PIECE], packed
                )
        o_ref[n, GROUP] = packed.astype(jnp.bfloat16)

    attend_sources(info, 1 - info[ZLO], q_ref, k_buf, v_buf, s_buf, put)


def near_kernel(info, q_ref, k_buf, v_buf, o_ref, m_ref, s_buf):
    def put(n, out, mass):
        o_ref[n] = out
        m_ref[n] = jnp.broadcast_to(mass, (ROWS, HEAD_DIM)).reshape(
            GROUP, PIECE, HEAD_DIM
        )

    attend_sources(info, info[ZLO], q_ref, k_buf, v_buf, s_buf, put)


def merge_kernel(near_ref, mass_ref, far_ref, o_ref):
    for n in range(SOURCES):
        packed = far_ref[n, GROUP].astype(jnp.float32)
        for g in range(GROUP):
            a = mass_ref[n, g]
            b = (
                packed[:, 3 * g : 3 * g + 1]
                + packed[:, 3 * g + 1 : 3 * g + 2]
                + packed[:, 3 * g + 2 : 3 * g + 3]
            )
            m = jnp.maximum(a, b)
            wa, wb = jnp.exp2(a - m), jnp.exp2(b - m)
            out = (wa * near_ref[n, g] + wb * far_ref[n, g].astype(jnp.float32)) / (wa + wb)
            o_ref[n, :, g * HEAD_DIM : (g + 1) * HEAD_DIM] = out.astype(jnp.bfloat16)


def pack_kernel(q_ref, k_ref, v_ref, o_ref):
    for h in range(KV_HEADS):
        o_ref[h, 0] = k_ref[:, h * HEAD_DIM : (h + 1) * HEAD_DIM]
        o_ref[h, 1] = v_ref[:, h * HEAD_DIM : (h + 1) * HEAD_DIM]
        for g in range(GROUP):
            c = (h * GROUP + g) * HEAD_DIM
            o_ref[h, 2 + g] = q_ref[:, c : c + HEAD_DIM]


SMEM = pl.BlockSpec(memory_space=pltpu.SMEM)
VMEM = pl.BlockSpec(memory_space=pltpu.VMEM)
ANY = pl.BlockSpec(memory_space=pl.ANY)
COST = pl.CostEstimate(flops=6_000_000_000, bytes_accessed=4_000_000, transcendentals=4_000_000)


def shape(*sizes, kind=jnp.bfloat16):
    return jax.ShapeDtypeStruct(sizes, kind)


SCORES = pltpu.VMEM((TILES, ROWS, TILE), jnp.float32)
SMALL = pltpu.CompilerParams(vmem_limit_bytes=8 << 20)
LIMIT = pltpu.CompilerParams(vmem_limit_bytes=32 << 20)


def far_part(info, q, own, other):
    return pl.pallas_call(
        far_kernel,
        out_shape=(
            shape(SOURCES, GROUP + 1, PIECE, HEAD_DIM),
            shape(KEYS, HEAD_DIM),
            shape(KEYS, HEAD_DIM),
        ),
        in_specs=[SMEM, VMEM, ANY, ANY],
        out_specs=(VMEM, VMEM, VMEM),
        scratch_shapes=[SCORES, pltpu.SemaphoreType.DMA((2, HALF))],
        compiler_params=LIMIT,
        cost_estimate=COST,
        name="far",
    )(info, q, own, other)


def near_part(info, q, k, v):
    return pl.pallas_call(
        near_kernel,
        out_shape=(
            shape(SOURCES, GROUP, PIECE, HEAD_DIM, kind=jnp.float32),
            shape(SOURCES, GROUP, PIECE, HEAD_DIM, kind=jnp.float32),
        ),
        in_specs=[SMEM, VMEM, VMEM, VMEM],
        out_specs=(VMEM, VMEM),
        scratch_shapes=[SCORES],
        compiler_params=LIMIT,
        cost_estimate=COST,
        name="near",
    )(info, q, k, v)


def merge(near, mass, far):
    return pl.pallas_call(
        merge_kernel,
        out_shape=shape(SOURCES, PIECE, GROUP * HEAD_DIM),
        in_specs=[VMEM, VMEM, VMEM],
        out_specs=VMEM,
        compiler_params=SMALL,
        name="merge",
    )(near, mass, far)


def pack(q, k, v):
    return pl.pallas_call(
        pack_kernel,
        out_shape=shape(KV_HEADS, GROUP + 2, PIECE, HEAD_DIM),
        in_specs=[VMEM, VMEM, VMEM],
        out_specs=VMEM,
        compiler_params=SMALL,
        name="pack",
    )(q, k, v)


PLANE = ("ylo", "yhi", "x")
SWAP = [(0, 1), (1, 0)]


def table(visit_ids, span_order):
    zlo = lax.axis_index("zlo").astype(jnp.int32)
    block = jnp.arange(SPANS, dtype=jnp.int32)
    mine = (block // 4) % 2 == zlo
    upto = jnp.arange(SPANS + 1, dtype=jnp.int32)
    count = jnp.sum(
        (mine[None, :] & (span_order[None, :] < upto[:, None])).astype(jnp.int32), axis=1
    )
    ranks = jnp.arange(HALF, dtype=jnp.int32)
    ordered = jnp.sum((count[None, 1:] <= ranks[:, None]).astype(jnp.int32), axis=1)
    starts = jnp.sum(
        (visit_ids[None, :] < jnp.arange(VISITS, dtype=jnp.int32)[:, None]).astype(jnp.int32),
        axis=1,
    )
    place = jnp.stack(
        [
            lax.axis_index("ylo"),
            lax.axis_index("core"),
            lax.axis_index("zlo"),
            (lax.axis_index("yhi") * 4 + lax.axis_index("x")) * PIECE,
        ]
    ).astype(jnp.int32)
    return jnp.concatenate([span_order, count, ordered, starts, place])


def body(queries, key_rows, value_rows, visit_ids, span_order):
    info = table(visit_ids, span_order)
    packed = lax.all_to_all(pack(queries, key_rows, value_rows), "zhi", 0, 0, tiled=True)
    near_q = packed[:, 2:]
    far_q = lax.ppermute(near_q, "zlo", SWAP)
    kv = packed[:, :2]
    spread = jnp.broadcast_to(kv[None], (16,) + kv.shape)
    own = lax.all_to_all(spread, PLANE, 0, 0, tiled=True)
    other = lax.ppermute(own, "core", SWAP)

    far_out, k, v = far_part(info, far_q, own, other)
    sent = lax.ppermute(far_out, "zlo", SWAP)
    near_out, mass = near_part(info, near_q, k, v)
    out = merge(near_out, mass, sent)
    out = lax.all_to_all(out, "zhi", 0, 0, tiled=True)
    return jnp.transpose(out, (1, 0, 2)).reshape(PIECE, HEADS * HEAD_DIM)


def solution(mesh):
    fine = Mesh(
        mesh.devices.reshape(8, 2, 2, 2, 2, 4), ("zhi", "zlo", "ylo", "core", "yhi", "x")
    )
    rows = P(("zhi", "zlo", "ylo", "core", "yhi", "x"), None)
    return jax.shard_map(
        body,
        mesh=fine,
        in_specs=(rows, rows, rows, P(), P()),
        out_specs=rows,
        check_vma=False,
    )
```

profile of v0, /device:TPU:1, one launch (start us, length us, event | category | flops | bytes accessed | tf_op | source)
XLA Modules:
  0.0 130.6 jit_solution(10579944970778475439)
XLA Ops:
  0.0 0.0 copy-start
  0.0 0.9 copy-done
  0.9 0.0 copy-start.1
  0.9 0.8 copy-done.1
  1.7 0.0 copy-start.2
  1.7 0.8 copy-done.2
  2.5 0.1 pack.1
  2.6 33.0 %all_to_all.15 = bf16[8,6,24,128]{3,2,1,0:T(8,128)(2,1)S(1)} all-to-all(bf16[8,6,24,128]{3,2,1,0:T(8,128)(2,1)S(1)} %pack.1), channel_id=1, replica_groups=mesh['zhi'=8,'zlo'=2,'ylo'=2,'core'=2,'yhi'=2,'x'=4] {'zhi'}, dimensions={0} | all-to-all | bytes 589824 | tf_op jit(solution)/shard_map/all_to_all | solution.py:302
  35.5 0.0 copy-start.3
  35.6 0.7 copy-done.3
  36.2 0.3 broadcast_in_dim.2
  36.5 0.0 copy-start.4
  36.6 22.6 %all_to_all.16.own_ref = bf16[16,8,2,24,128]{4,3,2,1,0:T(8,128)(2,1)S(1)} all-to-all(bf16[16,8,2,24,128]{4,3,2,1,0:T(8,128)(2,1)S(1)} %broadcast_in_dim.2), channel_id=1, replica_groups=mesh['zhi'=8,'zlo'=2,'ylo'=2,'core'=2,'yhi'=2,'x'=4] {'ylo','yhi','x'}, dimensions={0} | all-to-all | bytes 3145728 | tf_op jit(solution)/shard_map/all_to_all | solution.py:307
  59.2 9.7 %collective-permute-start.1 = (bf16[16,8,2,24,128]{4,3,2,1,0:T(8,128)(2,1)S(1)}, bf16[16,8,2,24,128]{4,3,2,1,0:T(8,128)(2,1)S(1)}, u32[]{:S(2)}, u32[]{:S(2)}) collective-permute-start(bf16[16,8,2,24,128]{4,3,2,1,0:T(8,128)(2,1)S(1)} %all_to_all.16.own_ref), channel_id=1, source_target_pairs={{0,8},{8,0},{1,9},{9,1},{2,10},{10,2},{3,11},{11,3},{4,12},{12,4},... | collective-permute-start | bytes 4718600 | tf_op jit(solution)/shard_map/ppermute | solution.py:308
  68.9 0.0 copy-done.4
  69.0 0.1 convert_reduce_fusion.1
  69.1 0.1 slice.9
  69.1 1.0 slice.12.q_ref
  70.1 4.3 %collective-permute-start = (bf16[8,4,24,128]{3,2,1,0:T(8,128)(2,1)S(1)}, bf16[8,4,24,128]{3,2,1,0:T(8,128)(2,1)S(1)}, u32[]{:S(2)}, u32[]{:S(2)}) collective-permute-start(bf16[8,4,24,128]{3,2,1,0:T(8,128)(2,1)S(1)} %slice.12.q_ref), channel_id=1, source_target_pairs={{0,32},{32,0},{1,33},{33,1},{2,34},{34,2},{3,35},{35,3},{4,36},{36... | collective-permute-start | bytes 589832 | tf_op jit(solution)/shard_map/ppermute | solution.py:304
  74.4 0.7 convert_reduce_fusion.2
  75.1 1.0 convert_reduce_fusion
  76.1 0.7 concatenate.3.info
  76.8 2.9 %collective-permute-done.q_ref = bf16[8,4,24,128]{3,2,1,0:T(8,128)(2,1)S(1)} collective-permute-done((bf16[8,4,24,128]{3,2,1,0:T(8,128)(2,1)S(1)}, bf16[8,4,24,128]{3,2,1,0:T(8,128)(2,1)S(1)}, u32[]{:S(2)}, u32[]{:S(2)}) %collective-permute-start) | collective-permute-done | bytes 196640 | tf_op jit(solution)/shard_map/ppermute | solution.py:304
  79.7 0.0 collective-permute-done.1.other_ref
  79.7 12.6 %far.1 = (bf16[8,5,24,128]{3,2,1,0:T(8,128)(2,1)S(1)}, bf16[6144,128]{1,0:T(8,128)(2,1)S(1)}, bf16[6144,128]{1,0:T(8,128)(2,1)S(1)}) custom-call(s32[169]{0:T(256)S(1)} %concatenate.3.info, bf16[8,4,24,128]{3,2,1,0:T(8,128)(2,1)S(1)} %collective-permute-done.q_ref, bf16[16,8,2,24,128]{4,3,2,1,0:T(8,128)(2,1)S(1)} %all_to_all.16.own_ref, ...), custom_call_target="tpu_custom_call" | custom-call | flops 6000000000 | bytes 4000000 | tf_op jit(solution)/shard_map/far/pallas_call | solution.py:217
  92.3 3.1 %collective-permute-start.2 = (bf16[8,5,24,128]{3,2,1,0:T(8,128)(2,1)S(1)}, bf16[8,5,24,128]{3,2,1,0:T(8,128)(2,1)S(1)}, u32[]{:S(2)}, u32[]{:S(2)}) collective-permute-start(bf16[8,5,24,128]{3,2,1,0:T(8,128)(2,1)S(1)} %get-tuple-element.14), channel_id=1, source_target_pairs={{0,32},{32,0},{1,33},{33,1},{2,34},{34,2},{3,35},{35,3},{4,36},{36... | collective-permute-start | bytes 737288 | tf_op jit(solution)/shard_map/ppermute | solution.py:311
  95.4 10.2 %near.1 = (f32[8,4,24,128]{3,2,1,0:T(8,128)S(1)}, f32[8,4,24,128]{3,2,1,0:T(8,128)S(1)}) custom-call(s32[169]{0:T(256)S(1)} %concatenate.3.info, bf16[8,4,24,128]{3,2,1,0:T(8,128)(2,1)S(1)} %slice.12.q_ref, bf16[6144,128]{1,0:T(8,128)(2,1)S(1)} %get-tuple-element.10.k_buf, bf16[6144,128]{1,0:T(8,128)(2,1)S(1)} %get-tuple-element.11.v_buf), custom_call_target="tpu_custom_call" | custom-call | flops 6000000000 | bytes 4000000 | tf_op jit(solution)/shard_map/near/pallas_call | solution.py:234
  105.6 0.0 collective-permute-done.2.far_ref
  105.6 0.5 merge.1
  106.0 23.9 %all_to_all.17 = bf16[8,24,512]{2,1,0:T(8,128)(2,1)S(1)} all-to-all(bf16[8,24,512]{2,1,0:T(8,128)(2,1)S(1)} %merge.1), channel_id=1, replica_groups=mesh['zhi'=8,'zlo'=2,'ylo'=2,'core'=2,'yhi'=2,'x'=4] {'zhi'}, dimensions={0} | all-to-all | bytes 393216 | tf_op jit(solution)/shard_map/all_to_all | solution.py:314
  129.9 0.7 copy.8
  (2 shorter events, 0.0 us)
Async XLA Ops:
  0.0 0.9 copy-start
  0.9 0.8 copy-start.1
  1.7 0.8 copy-start.2
  35.5 0.7 copy-start.3
  36.5 32.4 %copy-start.4 = (s32[64]{0:T(128)S(1)}, s32[64]{0:T(128)}, u32[]{:S(2)}) copy-start(s32[64]{0:T(128)} %param.9) | copy-start | bytes 772
  59.2 20.5 %collective-permute-start.1 = (bf16[16,8,2,24,128]{4,3,2,1,0:T(8,128)(2,1)S(1)}, bf16[16,8,2,24,128]{4,3,2,1,0:T(8,128)(2,1)S(1)}, u32[]{:S(2)}, u32[]{:S(2)}) collective-permute-start(bf16[16,8,2,24,128]{4,3,2,1,0:T(8,128)(2,1)S(1)} %all_to_all.16.own_ref), channel_id=1, source_target_pairs={{0,8},{8,0},{1,9},{9,1},{2,10},{10,2},{3,11},{11,3},{4,12},{12,4},... | collective-permute-start | bytes 4718600 | tf_op jit(solution)/shard_map/ppermute | solution.py:308
  70.1 9.6 %collective-permute-start = (bf16[8,4,24,128]{3,2,1,0:T(8,128)(2,1)S(1)}, bf16[8,4,24,128]{3,2,1,0:T(8,128)(2,1)S(1)}, u32[]{:S(2)}, u32[]{:S(2)}) collective-permute-start(bf16[8,4,24,128]{3,2,1,0:T(8,128)(2,1)S(1)} %slice.12.q_ref), channel_id=1, source_target_pairs={{0,32},{32,0},{1,33},{33,1},{2,34},{34,2},{3,35},{35,3},{4,36},{36... | collective-permute-start | bytes 589832 | tf_op jit(solution)/shard_map/ppermute | solution.py:304
  92.3 13.3 %collective-permute-start.2 = (bf16[8,5,24,128]{3,2,1,0:T(8,128)(2,1)S(1)}, bf16[8,5,24,128]{3,2,1,0:T(8,128)(2,1)S(1)}, u32[]{:S(2)}, u32[]{:S(2)}) collective-permute-start(bf16[8,5,24,128]{3,2,1,0:T(8,128)(2,1)S(1)} %get-tuple-element.14), channel_id=1, source_target_pairs={{0,32},{32,0},{1,33},{33,1},{2,34},{34,2},{3,35},{35,3},{4,36},{36... | collective-permute-start | bytes 737288 | tf_op jit(solution)/shard_map/ppermute | solution.py:311
where the time goes:
time: 131 us
  blocking collectives  79.5 us (61%)
  Pallas kernels  23.3 us (18%)
  starting transfers between devices  17.1 us (13%)
  local copies, waits for them, and re-layouts  5.94 us (5%)
  waiting for transfers between devices  2.88 us (2%)
  other arithmetic  1.77 us (1%)
    all_to_all x1, blocking collectives, body(): lax.all_to_all(pack(queries, key_rows, value_rows), 'zhi', 0, 0, tiled=True)  33 us
    all_to_all x1, blocking collectives, body(): out = lax.all_to_all(out, 'zhi', 0, 0, tiled=True)  23.9 us
    all_to_all x1, blocking collectives, body(): own = lax.all_to_all(spread, PLANE, 0, 0, tiled=True)  22.6 us
    pallas_call x1, Pallas kernels, far_part(): pl.pallas_call(far_kernel, out_shape=(shape(SOURCES, GROUP + 1, PIECE, HE...  12.6 us
    pallas_call x1, Pallas kernels, near_part(): pl.pallas_call(near_kernel, out_shape=(shape(SOURCES, GROUP, PIECE, HEAD_...  10.2 us
    ppermute x1, starting transfers between devices, body(): other = lax.ppermute(own, 'core', SWAP)  9.71 us
    ppermute x1, starting transfers between devices, body(): far_q = lax.ppermute(near_q, 'zlo', SWAP)  4.32 us
    unnamed x10, local copies, waits for them, and re-layouts  3.21 us
  transfers between devices with their start and end apart: 3, of which 1 were waited for; matrix products, arithmetic and copies ran while one was open for 3% of the time, Pallas kernels for 8%

commit v1 on v0

v1 whole, which is shorter than its diff:
```python
import jax
import jax.numpy as jnp
from jax import lax
from jax.experimental import pallas as pl
from jax.experimental.pallas import tpu as pltpu
from jax.sharding import Mesh, PartitionSpec as P

HEADS = 32
KV_HEADS = 8
HEAD_DIM = 128
GROUP = HEADS // KV_HEADS
SPAN_ROWS = 192
PIECE = 24
PARTS = SPAN_ROWS // PIECE
VISITS = 4
SPANS = 64
HALF = SPANS // 2
KEYS = HALF * SPAN_ROWS
PER_TILE = 4
UNROLL = 2
TILE = PER_TILE * SPAN_ROWS
TILES = KEYS // TILE
SOURCES = 8
ROWS = GROUP * PIECE
SCALE_LOG2 = HEAD_DIM ** (-0.5) * 1.4426950408889634
NOTHING = -3e38

ORDER = 0
COUNT = 64
SORTED = COUNT + 65
START = SORTED + HALF
YLO = START + VISITS
CORE = YLO + 1
ZLO = YLO + 2
FIRST = YLO + 3


def gather_keys(info, own_ref, other_ref, buf, which, sems):
    core, zlo = info[CORE], info[ZLO]
    pieces = buf.reshape(HALF * PARTS, PIECE, HEAD_DIM)

    def each(act):
        def step(i, carry):
            k, half = i // 2, i % 2
            for src, side in ((own_ref, core), (other_ref, 1 - core)):
                span = info[ORDER + (k * 2 + zlo) * 4 + half * 2 + side]
                rank = info[COUNT + span]
                act(
                    pltpu.make_async_copy(
                        src.at[pl.ds(half * PARTS, PARTS), k, which],
                        pieces.at[pl.ds(rank * PARTS, PARTS)],
                        sems.at[which, (k * 2 + half) * 2 + side],
                    )
                )
            return carry

        lax.fori_loop(0, 2 * SOURCES, step, 0)

    return lambda: each(lambda c: c.start()), lambda: each(lambda c: c.wait())


def attend_sources(info, side, q_ref, k_buf, v_buf, scratch, put, k_ready, v_ready):
    s_buf, q_buf, low_buf, pos_buf, best, top_buf, total, acc, item_n, item_j = scratch
    ylo, core, first = info[YLO], info[CORE], info[FIRST]
    inside = lax.broadcasted_iota(jnp.int32, (PIECE, HEAD_DIM), 0)
    lane = lax.broadcasted_iota(jnp.int32, (1, HEAD_DIM), 1)

    def start_of(pos):
        low = jnp.zeros_like(pos)
        for v in range(1, VISITS):
            low = jnp.where(info[START + v] <= pos, info[START + v], low)
        return low

    count = jnp.int32(0)
    for n in range(SOURCES):
        span = info[ORDER + (n * 2 + side) * 4 + ylo * 2 + core]
        p0 = span * SPAN_ROWS + first
        pos = p0 + inside
        pos_buf[n] = pos
        low_buf[n] = start_of(pos)
        q_buf[n] = (
            q_ref[n, 2:].astype(jnp.float32).reshape(ROWS, HEAD_DIM).astype(jnp.bfloat16)
        )
        tile_a = info[COUNT + start_of(p0) // SPAN_ROWS] // PER_TILE
        tile_b = (info[COUNT + span + 1] + PER_TILE - 1) // PER_TILE

        def note(j, at, n=n):
            item_n[at] = n
            item_j[at] = j
            return at + 1

        count = lax.fori_loop(tile_a, tile_b, note, count)
    for u in range(UNROLL - 1):
        item_n[count + u] = SOURCES
        item_j[count + u] = 0
    steps = (count + UNROLL - 1) // UNROLL

    for n in range(SOURCES):
        for u in range(UNROLL):
            best[u, n] = jnp.full((ROWS, HEAD_DIM), -jnp.inf, jnp.float32)
            total[u, n] = jnp.zeros((ROWS, HEAD_DIM), jnp.float32)
            acc[u, n] = jnp.zeros((ROWS, HEAD_DIM), jnp.float32)

    k_ready()

    def scores(i, carry):
        for u in range(UNROLL):
            at = i * UNROLL + u
            slot, j = item_n[at], item_j[at]
            n = jnp.minimum(slot, SOURCES - 1)
            s = lax.dot_general(
                q_buf[n],
                k_buf[pl.ds(pl.multiple_of(j * TILE, TILE), TILE), :],
                (((1,), (1,)), ((), ())),
                preferred_element_type=jnp.float32,
            )
            s = s.reshape(GROUP, PIECE, TILE)
            low, pos = low_buf[n], pos_buf[n]
            base = [
                (info[SORTED + j * PER_TILE + w] - w) * SPAN_ROWS for w in range(PER_TILE)
            ]
            high = best[u, slot].reshape(GROUP, PIECE, HEAD_DIM)
            for c in range(TILE // HEAD_DIM):
                left = c * HEAD_DIM // SPAN_ROWS
                right = (c * HEAD_DIM + HEAD_DIM - 1) // SPAN_ROWS
                key = lane + c * HEAD_DIM
                if left == right:
                    key = key + base[left]
                else:
                    key = key + jnp.where(key < right * SPAN_ROWS, base[left], base[right])
                keep = (key >= low) & (key <= pos)
                part = jnp.where(
                    keep[None], s[:, :, c * HEAD_DIM : (c + 1) * HEAD_DIM], -jnp.inf
                )
                s_buf[at, :, c * HEAD_DIM : (c + 1) * HEAD_DIM] = part.reshape(ROWS, HEAD_DIM)
                high = jnp.maximum(high, part)
            best[u, slot] = high.reshape(ROWS, HEAD_DIM)
        return carry

    lax.fori_loop(0, steps, scores, 0)

    for n in range(SOURCES):
        high = best[0, n]
        for u in range(1, UNROLL):
            high = jnp.maximum(high, best[u, n])
        top = jnp.max(high, axis=1, keepdims=True)
        top_buf[n] = jnp.broadcast_to(top, (ROWS, HEAD_DIM))

    v_ready()

    def mix(i, carry):
        for u in range(UNROLL):
            at = i * UNROLL + u
            slot, j = item_n[at], item_j[at]
            n = jnp.minimum(slot, SOURCES - 1)
            top = top_buf[n]
            top = jnp.where(top > -jnp.inf, top, 0.0)
            part_sum = total[u, slot]
            parts = []
            for c in range(TILE // HEAD_DIM):
                w = jnp.exp2(
                    (s_buf[at, :, c * HEAD_DIM : (c + 1) * HEAD_DIM] - top) * SCALE_LOG2
                )
                part_sum = part_sum + w
                parts.append(w.astype(jnp.bfloat16))
            total[u, slot] = part_sum
            acc[u, slot] = acc[u, slot] + jnp.dot(
                jnp.concatenate(parts, axis=1),
                v_buf[pl.ds(pl.multiple_of(j * TILE, TILE), TILE), :],
                preferred_element_type=jnp.float32,
            )
        return carry

    lax.fori_loop(0, steps, mix, 0)

    for n in range(SOURCES):
        top = top_buf[n]
        whole, out = total[0, n], acc[0, n]
        for u in range(1, UNROLL):
            whole, out = whole + total[u, n], out + acc[u, n]
        whole = jnp.sum(whole, axis=1, keepdims=True)
        some = top > -jnp.inf
        safe = jnp.where(some, whole, 1.0)
        mass = jnp.where(some, top * SCALE_LOG2 + jnp.log2(safe), NOTHING)
        put(
            n,
            (out / safe).reshape(GROUP, PIECE, HEAD_DIM),
            mass.reshape(GROUP, PIECE, HEAD_DIM),
        )


def far_kernel(info, q_ref, own_ref, other_ref, o_ref, k_buf, v_buf, sems, *scratch):
    k_start, k_ready = gather_keys(info, own_ref, other_ref, k_buf, 0, sems)
    v_start, v_ready = gather_keys(info, own_ref, other_ref, v_buf, 1, sems)
    k_start()
    v_start()
    lane = lax.broadcasted_iota(jnp.int32, (PIECE, HEAD_DIM), 1)

    def put(n, out, mass):
        o_ref[n, :GROUP] = out.astype(jnp.bfloat16)
        high = mass.astype(jnp.bfloat16).astype(jnp.float32)
        rest = mass - high
        middle = rest.astype(jnp.bfloat16).astype(jnp.float32)
        pieces = (high, middle, rest - middle)
        packed = jnp.zeros((PIECE, HEAD_DIM), jnp.float32)
        for g in range(GROUP):
            for i, piece in enumerate(pieces):
                packed = jnp.where(lane == 3 * g + i, piece[g], packed)
        o_ref[n, GROUP] = packed.astype(jnp.bfloat16)

    attend_sources(
        info, 1 - info[ZLO], q_ref, k_buf, v_buf, scratch, put, k_ready, v_ready
    )


def near_kernel(info, q_ref, k_buf, v_buf, o_ref, m_ref, *scratch):
    def put(n, out, mass):
        o_ref[n] = out
        m_ref[n] = mass

    nothing = lambda: None
    attend_sources(info, info[ZLO], q_ref, k_buf, v_buf, scratch, put, nothing, nothing)


def merge_kernel(near_ref, mass_ref, far_ref, o_ref):
    for n in range(SOURCES):
        packed = far_ref[n, GROUP].astype(jnp.float32)
        for g in range(GROUP):
            a = mass_ref[n, g]
            b = (
                packed[:, 3 * g : 3 * g + 1]
                + packed[:, 3 * g + 1 : 3 * g + 2]
                + packed[:, 3 * g + 2 : 3 * g + 3]
            )
            m = jnp.maximum(a, b)
            wa, wb = jnp.exp2(a - m), jnp.exp2(b - m)
            out = (wa * near_ref[n, g] + wb * far_ref[n, g].astype(jnp.float32)) / (wa + wb)
            o_ref[n, :, g * HEAD_DIM : (g + 1) * HEAD_DIM] = out.astype(jnp.bfloat16)


def pack_kernel(q_ref, k_ref, v_ref, o_ref, sems):
    copies = []
    for h in range(KV_HEADS):
        for i in range(GROUP + 2):
            src, c = ((k_ref, h), (v_ref, h))[i] if i < 2 else (q_ref, h * GROUP + i - 2)
            copies.append(
                pltpu.make_async_copy(
                    src.at[:, c * HEAD_DIM : (c + 1) * HEAD_DIM], o_ref.at[h, i], sems.at[h, i]
                )
            )
    for c in copies:
        c.start()
    for c in copies:
        c.wait()


def fan_kernel(packed_ref, o_ref):
    for i in range(16):
        o_ref[i] = packed_ref[:, :2]


SMEM = pl.BlockSpec(memory_space=pltpu.SMEM)
VMEM = pl.BlockSpec(memory_space=pltpu.VMEM)
ANY = pl.BlockSpec(memory_space=pl.ANY)
HBM = pl.BlockSpec(memory_space=pltpu.HBM)
COST = pl.CostEstimate(flops=6_000_000_000, bytes_accessed=4_000_000, transcendentals=4_000_000)


def shape(*sizes, kind=jnp.bfloat16):
    return jax.ShapeDtypeStruct(sizes, kind)


ITEMS = SOURCES * TILES + UNROLL
SCRATCH = [
    pltpu.VMEM((ITEMS, ROWS, TILE), jnp.float32),
    pltpu.VMEM((SOURCES, ROWS, HEAD_DIM), jnp.bfloat16),
    pltpu.VMEM((SOURCES, PIECE, HEAD_DIM), jnp.int32),
    pltpu.VMEM((SOURCES, PIECE, HEAD_DIM), jnp.int32),
    pltpu.VMEM((UNROLL, SOURCES + 1, ROWS, HEAD_DIM), jnp.float32),
    pltpu.VMEM((SOURCES, ROWS, HEAD_DIM), jnp.float32),
    pltpu.VMEM((UNROLL, SOURCES + 1, ROWS, HEAD_DIM), jnp.float32),
    pltpu.VMEM((UNROLL, SOURCES + 1, ROWS, HEAD_DIM), jnp.float32),
    pltpu.SMEM((ITEMS,), jnp.int32),
    pltpu.SMEM((ITEMS,), jnp.int32),
]
SMALL = pltpu.CompilerParams(vmem_limit_bytes=8 << 20)
LIMIT = pltpu.CompilerParams(vmem_limit_bytes=40 << 20)


def far_part(info, q, own, other):
    return pl.pallas_call(
        far_kernel,
        out_shape=(
            shape(SOURCES, GROUP + 1, PIECE, HEAD_DIM),
            shape(KEYS, HEAD_DIM),
            shape(KEYS, HEAD_DIM),
        ),
        in_specs=[SMEM, VMEM, ANY, ANY],
        out_specs=(VMEM, VMEM, VMEM),
        scratch_shapes=[pltpu.SemaphoreType.DMA((2, HALF))] + SCRATCH,
        compiler_params=LIMIT,
        cost_estimate=COST,
        name="far",
    )(info, q, own, other)


def near_part(info, q, k, v):
    return pl.pallas_call(
        near_kernel,
        out_shape=(
            shape(SOURCES, GROUP, PIECE, HEAD_DIM, kind=jnp.float32),
            shape(SOURCES, GROUP, PIECE, HEAD_DIM, kind=jnp.float32),
        ),
        in_specs=[SMEM, VMEM, VMEM, VMEM],
        out_specs=(VMEM, VMEM),
        scratch_shapes=SCRATCH,
        compiler_params=LIMIT,
        cost_estimate=COST,
        name="near",
    )(info, q, k, v)


def merge(near, mass, far):
    return pl.pallas_call(
        merge_kernel,
        out_shape=shape(SOURCES, PIECE, GROUP * HEAD_DIM),
        in_specs=[VMEM, VMEM, VMEM],
        out_specs=VMEM,
        compiler_params=SMALL,
        name="merge",
    )(near, mass, far)


def pack(q, k, v):
    return pl.pallas_call(
        pack_kernel,
        out_shape=shape(KV_HEADS, GROUP + 2, PIECE, HEAD_DIM),
        in_specs=[HBM, HBM, HBM],
        out_specs=VMEM,
        scratch_shapes=[pltpu.SemaphoreType.DMA((KV_HEADS, GROUP + 2))],
        name="pack",
    )(q, k, v)


def fan(packed):
    return pl.pallas_call(
        fan_kernel,
        out_shape=shape(16, SOURCES, 2, PIECE, HEAD_DIM),
        in_specs=[VMEM],
        out_specs=VMEM,
        compiler_params=SMALL,
        name="fan",
    )(packed)


PLANE = ("ylo", "yhi", "x")
SWAP = [(0, 1), (1, 0)]


def table(visit_ids, span_order):
    zlo = lax.axis_index("zlo").astype(jnp.int32)
    block = jnp.arange(SPANS, dtype=jnp.int32)
    mine = (block // 4) % 2 == zlo
    upto = jnp.arange(SPANS + 1, dtype=jnp.int32)
    count = jnp.sum(
        (mine[None, :] & (span_order[None, :] < upto[:, None])).astype(jnp.int32), axis=1
    )
    ranks = jnp.arange(HALF, dtype=jnp.int32)
    ordered = jnp.sum((count[None, 1:] <= ranks[:, None]).astype(jnp.int32), axis=1)
    starts = jnp.sum(
        (visit_ids[None, :] < jnp.arange(VISITS, dtype=jnp.int32)[:, None]).astype(jnp.int32),
        axis=1,
    )
    place = jnp.stack(
        [
            lax.axis_index("ylo"),
            lax.axis_index("core"),
            lax.axis_index("zlo"),
            (lax.axis_index("yhi") * 4 + lax.axis_index("x")) * PIECE,
        ]
    ).astype(jnp.int32)
    return jnp.concatenate([span_order, count, ordered, starts, place])


def body(queries, key_rows, value_rows, visit_ids, span_order):
    info = table(visit_ids, span_order)
    packed = lax.all_to_all(pack(queries, key_rows, value_rows), "zhi", 0, 0, tiled=True)
    far_q = lax.ppermute(packed, "zlo", SWAP)
    spread = fan(packed)
    own = lax.all_to_all(spread, PLANE, 0, 0, tiled=True)
    other = lax.ppermute(own, "core", SWAP)

    far_out, k, v = far_part(info, far_q, own, other)
    sent = lax.ppermute(far_out, "zlo", SWAP)
    near_out, mass = near_part(info, packed, k, v)
    out = merge(near_out, mass, sent)
    out = lax.all_to_all(out, "zhi", 0, 0, tiled=True)
    return jnp.transpose(out, (1, 0, 2)).reshape(PIECE, HEADS * HEAD_DIM)


def solution(mesh):
    fine = Mesh(
        mesh.devices.reshape(8, 2, 2, 2, 2, 4), ("zhi", "zlo", "ylo", "core", "yhi", "x")
    )
    rows = P(("zhi", "zlo", "ylo", "core", "yhi", "x"), None)
    return jax.shard_map(
        body,
        mesh=fine,
        in_specs=(rows, rows, rows, P(), P()),
        out_specs=rows,
        check_vma=False,
    )
```

time: 131 us -> 123 us (0.939)
  Pallas kernels: 23.3 us -> 16.1 us
  local copies, waits for them, and re-layouts: 5.94 us -> 0.86 us
  waiting for transfers between devices: 2.88 us -> 6.88 us
  starting transfers between devices: 17.1 us -> 19.8 us
  other arithmetic: 1.77 us -> 0.44 us
    pallas_call x1, Pallas kernels: 12.6 us -> 7.67 us  [far_part(): pl.pallas_call(far_kernel, out_shape=(shape(SOURCES, GROUP + 1, PIECE, HE...]
    pallas_call x1, Pallas kernels: 10.2 us -> 5.61 us  [near_part(): pl.pallas_call(near_kernel, out_shape=(shape(SOURCES, GROUP, PIECE, HEAD_...]
    ppermute x1, waiting for transfers between devices: 2.88 us -> 6.85 us  [body(): far_q = lax.ppermute(packed, 'zlo', SWAP)]
    unnamed x10 -> x4, local copies, waits for them, and re-layouts: 3.21 us -> 0.01 us
    ppermute x1, starting transfers between devices: 3.07 us -> 5.76 us  [body(): sent = lax.ppermute(far_out, 'zlo', SWAP)]
    pallas_call x1, Pallas kernels: 0.05 us -> 2.12 us  [pack(): pl.pallas_call(pack_kernel, out_shape=shape(KV_HEADS, GROUP + 2, PIECE, H...]
    all_to_all x1, blocking collectives: 23.9 us -> 22.3 us  [body(): out = lax.all_to_all(out, 'zhi', 0, 0, tiled=True)]
  transfers between devices with their start and end apart: 3 -> 3, of which waited for: 1 -> 1; matrix products, arithmetic and copies ran while one was open for 3% -> 0% of each run, Pallas kernels for 8% -> 5%
where the time goes in v1:
time: 123 us; the launch traced here: 122 us
  blocking collectives  78.3 us (64%)
  starting transfers between devices  19.8 us (16%)
  Pallas kernels  16.1 us (13%)
  waiting for transfers between devices  6.88 us (6%)
    all_to_all x1, blocking collectives, body(): lax.all_to_all(pack(queries, key_rows, value_rows), 'zhi', 0, 0, tiled=True)  33.2 us
    all_to_all x1, blocking collectives, body(): own = lax.all_to_all(spread, PLANE, 0, 0, tiled=True)  22.8 us
    all_to_all x1, blocking collectives, body(): out = lax.all_to_all(out, 'zhi', 0, 0, tiled=True)  22.3 us
    ppermute x1, starting transfers between devices, body(): other = lax.ppermute(own, 'core', SWAP)  9.71 us
    pallas_call x1, Pallas kernels, far_part(): pl.pallas_call(far_kernel, out_shape=(shape(SOURCES, GROUP + 1, PIECE, HE...  7.67 us
    ppermute x1, waiting for transfers between devices, body(): far_q = lax.ppermute(packed, 'zlo', SWAP)  6.85 us
    ppermute x1, starting transfers between devices, body(): sent = lax.ppermute(far_out, 'zlo', SWAP)  5.76 us
    pallas_call x1, Pallas kernels, near_part(): pl.pallas_call(near_kernel, out_shape=(shape(SOURCES, GROUP, PIECE, HEAD_...  5.61 us
  transfers between devices with their start and end apart: 3, of which 1 were waited for; matrix products, arithmetic and copies ran while one was open for 0% of the time, Pallas kernels for 5%

profile of v1, /device:TPU:1, one launch (start us, length us, event | category | flops | bytes accessed | tf_op | source)
XLA Modules:
  0.0 122.4 jit_solution(15276711580864140102)
XLA Ops:
  0.0 2.1 %pack.1 = bf16[8,6,24,128]{3,2,1,0:T(8,128)(2,1)} custom-call(bf16[24,4096]{1,0:T(8,128)(2,1)} %q_ref.1, bf16[24,1024]{1,0:T(8,128)(2,1)} %k_ref.1, bf16[24,1024]{1,0:T(8,128)(2,1)} %v_ref.1), custom_call_target="tpu_custom_call" | custom-call | tf_op jit(solution)/shard_map/pack/pallas_call | solution.py:335
  2.1 33.2 %all_to_all.15.packed_ref.q_ref = bf16[8,6,24,128]{3,2,1,0:T(8,128)(2,1)S(1)} all-to-all(bf16[8,6,24,128]{3,2,1,0:T(8,128)(2,1)} %pack.1), channel_id=1, replica_groups=mesh['zhi'=8,'zlo'=2,'ylo'=2,'core'=2,'yhi'=2,'x'=4] {'zhi'}, dimensions={0} | all-to-all | bytes 589824 | tf_op jit(solution)/shard_map/all_to_all | solution.py:387
  35.3 0.2 fan.1
  35.5 0.0 copy-start.1
  35.5 0.0 copy-start
  35.5 22.8 %all_to_all.16.own_ref = bf16[16,8,2,24,128]{4,3,2,1,0:T(8,128)(2,1)S(1)} all-to-all(bf16[16,8,2,24,128]{4,3,2,1,0:T(8,128)(2,1)S(1)} %fan.1), channel_id=1, replica_groups=mesh['zhi'=8,'zlo'=2,'ylo'=2,'core'=2,'yhi'=2,'x'=4] {'ylo','yhi','x'}, dimensions={0} | all-to-all | bytes 3145728 | tf_op jit(solution)/shard_map/all_to_all | solution.py:390
  58.3 9.7 %collective-permute-start.1 = (bf16[16,8,2,24,128]{4,3,2,1,0:T(8,128)(2,1)S(1)}, bf16[16,8,2,24,128]{4,3,2,1,0:T(8,128)(2,1)S(1)}, u32[]{:S(2)}, u32[]{:S(2)}) collective-permute-start(bf16[16,8,2,24,128]{4,3,2,1,0:T(8,128)(2,1)S(1)} %all_to_all.16.own_ref), channel_id=1, source_target_pairs={{0,8},{8,0},{1,9},{9,1},{2,10},{10,2},{3,11},{11,3},{4,12},{12,4},... | collective-permute-start | bytes 4718600 | tf_op jit(solution)/shard_map/ppermute | solution.py:391
  68.1 4.3 %collective-permute-start = (bf16[8,6,24,128]{3,2,1,0:T(8,128)(2,1)S(1)}, bf16[8,6,24,128]{3,2,1,0:T(8,128)(2,1)}, u32[]{:S(2)}, u32[]{:S(2)}) collective-permute-start(bf16[8,6,24,128]{3,2,1,0:T(8,128)(2,1)S(1)} %all_to_all.15.packed_ref.q_ref), channel_id=1, source_target_pairs={{0,32},{32,0},{1,33},{33,1},{2,34},{34,2},{3,35},{35,3},{4,36},{36... | collective-permute-start | bytes 884744 | tf_op jit(solution)/shard_map/ppermute | solution.py:388
  72.4 0.0 copy-done.1
  72.4 0.1 convert_reduce_fusion.1
  72.5 0.1 slice.3
  72.6 0.1 convert_reduce_fusion.2
  72.7 0.0 copy-done
  72.7 0.2 convert_reduce_fusion
  72.9 0.1 concatenate.3.info
  73.0 6.8 %collective-permute-done.q_ref = bf16[8,6,24,128]{3,2,1,0:T(8,128)(2,1)} collective-permute-done((bf16[8,6,24,128]{3,2,1,0:T(8,128)(2,1)S(1)}, bf16[8,6,24,128]{3,2,1,0:T(8,128)(2,1)}, u32[]{:S(2)}, u32[]{:S(2)}) %collective-permute-start) | collective-permute-done | bytes 294944 | tf_op jit(solution)/shard_map/ppermute | solution.py:388
  79.8 0.0 collective-permute-done.1.other_ref
  79.8 7.7 %far.1 = (bf16[8,5,24,128]{3,2,1,0:T(8,128)(2,1)S(1)}, bf16[6144,128]{1,0:T(8,128)(2,1)S(1)}, bf16[6144,128]{1,0:T(8,128)(2,1)S(1)}) custom-call(s32[169]{0:T(256)S(1)} %concatenate.3.info, bf16[8,6,24,128]{3,2,1,0:T(8,128)(2,1)} %collective-permute-done.q_ref, bf16[16,8,2,24,128]{4,3,2,1,0:T(8,128)(2,1)S(1)} %all_to_all.16.own_ref, ...), custom_call_target="tpu_custom_call" | custom-call | flops 6000000000 | bytes 4000000 | tf_op jit(solution)/shard_map/far/pallas_call | solution.py:291
  87.5 5.8 %collective-permute-start.2 = (bf16[8,5,24,128]{3,2,1,0:T(8,128)(2,1)S(1)}, bf16[8,5,24,128]{3,2,1,0:T(8,128)(2,1)S(1)}, u32[]{:S(2)}, u32[]{:S(2)}) collective-permute-start(bf16[8,5,24,128]{3,2,1,0:T(8,128)(2,1)S(1)} %get-tuple-element.14), channel_id=1, source_target_pairs={{0,32},{32,0},{1,33},{33,1},{2,34},{34,2},{3,35},{35,3},{4,36},{36... | collective-permute-start | bytes 737288 | tf_op jit(solution)/shard_map/ppermute | solution.py:394
  93.3 5.6 %near.1 = (f32[8,4,24,128]{3,2,1,0:T(8,128)S(1)}, f32[8,4,24,128]{3,2,1,0:T(8,128)S(1)}) custom-call(s32[169]{0:T(256)S(1)} %concatenate.3.info, bf16[8,6,24,128]{3,2,1,0:T(8,128)(2,1)S(1)} %all_to_all.15.packed_ref.q_ref, bf16[6144,128]{1,0:T(8,128)(2,1)S(1)} %get-tuple-element.10.k_buf, bf16[6144,128]{1,0:T(8,128)(2,1)S(1)} %get-tuple-element.11.v_buf), custom_call_target="tpu_custom_call" | custom-call | flops 6000000000 | bytes 4000000 | tf_op jit(solution)/shard_map/near/pallas_call | solution.py:308
  98.9 0.0 collective-permute-done.2.far_ref
  98.9 0.5 merge.1
  99.4 22.3 %all_to_all.17 = bf16[8,24,512]{2,1,0:T(8,128)(2,1)S(1)} all-to-all(bf16[8,24,512]{2,1,0:T(8,128)(2,1)S(1)} %merge.1), channel_id=1, replica_groups=mesh['zhi'=8,'zlo'=2,'ylo'=2,'core'=2,'yhi'=2,'x'=4] {'zhi'}, dimensions={0} | all-to-all | bytes 393216 | tf_op jit(solution)/shard_map/all_to_all | solution.py:397
  121.7 0.7 copy.8
  (1 shorter events, 0.0 us)
Async XLA Ops:
  35.5 36.9 %copy-start.1 = (s32[64]{0:T(128)S(1)}, s32[64]{0:T(128)}, u32[]{:S(2)}) copy-start(s32[64]{0:T(128)} %param.9) | copy-start | bytes 772
  35.5 37.2 %copy-start = (s32[12288]{0:T(1024)S(1)}, s32[12288]{0:T(1024)}, u32[]{:S(2)}) copy-start(s32[12288]{0:T(1024)} %param.8) | copy-start | bytes 147460
  58.3 21.5 %collective-permute-start.1 = (bf16[16,8,2,24,128]{4,3,2,1,0:T(8,128)(2,1)S(1)}, bf16[16,8,2,24,128]{4,3,2,1,0:T(8,128)(2,1)S(1)}, u32[]{:S(2)}, u32[]{:S(2)}) collective-permute-start(bf16[16,8,2,24,128]{4,3,2,1,0:T(8,128)(2,1)S(1)} %all_to_all.16.own_ref), channel_id=1, source_target_pairs={{0,8},{8,0},{1,9},{9,1},{2,10},{10,2},{3,11},{11,3},{4,12},{12,4},... | collective-permute-start | bytes 4718600 | tf_op jit(solution)/shard_map/ppermute | solution.py:391
  68.1 11.8 %collective-permute-start = (bf16[8,6,24,128]{3,2,1,0:T(8,128)(2,1)S(1)}, bf16[8,6,24,128]{3,2,1,0:T(8,128)(2,1)}, u32[]{:S(2)}, u32[]{:S(2)}) collective-permute-start(bf16[8,6,24,128]{3,2,1,0:T(8,128)(2,1)S(1)} %all_to_all.15.packed_ref.q_ref), channel_id=1, source_target_pairs={{0,32},{32,0},{1,33},{33,1},{2,34},{34,2},{3,35},{35,3},{4,36},{36... | collective-permute-start | bytes 884744 | tf_op jit(solution)/shard_map/ppermute | solution.py:388
  87.5 11.4 %collective-permute-start.2 = (bf16[8,5,24,128]{3,2,1,0:T(8,128)(2,1)S(1)}, bf16[8,5,24,128]{3,2,1,0:T(8,128)(2,1)S(1)}, u32[]{:S(2)}, u32[]{:S(2)}) collective-permute-start(bf16[8,5,24,128]{3,2,1,0:T(8,128)(2,1)S(1)} %get-tuple-element.14), channel_id=1, source_target_pairs={{0,32},{32,0},{1,33},{33,1},{2,34},{34,2},{3,35},{35,3},{4,36},{36... | collective-permute-start | bytes 737288 | tf_op jit(solution)/shard_map/ppermute | solution.py:394

commit v2 on v1

--- a/solution.py
+++ b/solution.py
@@ -17,7 +17,7 @@
 HALF = SPANS // 2
 KEYS = HALF * SPAN_ROWS
 PER_TILE = 4
-UNROLL = 2
+UNROLL = 4
 TILE = PER_TILE * SPAN_ROWS
 TILES = KEYS // TILE
 SOURCES = 8
@@ -35,28 +35,36 @@
 FIRST = YLO + 3
 
 
-def gather_keys(info, own_ref, other_ref, buf, which, sems):
-    core, zlo = info[CORE], info[ZLO]
+def key_copies(info, src, side, buf, which, sems):
+    zlo = info[ZLO]
     pieces = buf.reshape(HALF * PARTS, PIECE, HEAD_DIM)
 
-    def each(act):
+    def each(act, by_y):
         def step(i, carry):
             k, half = i // 2, i % 2
-            for src, side in ((own_ref, core), (other_ref, 1 - core)):
-                span = info[ORDER + (k * 2 + zlo) * 4 + half * 2 + side]
-                rank = info[COUNT + span]
+            span = info[ORDER + (k * 2 + zlo) * 4 + half * 2 + side]
+            rank = info[COUNT + span]
+            for yhi in range(2):
+                y = half * 2 + yhi
+                rows = src.at[y, :, k, which] if by_y else src.at[:, y, k, which]
                 act(
                     pltpu.make_async_copy(
-                        src.at[pl.ds(half * PARTS, PARTS), k, which],
-                        pieces.at[pl.ds(rank * PARTS, PARTS)],
-                        sems.at[which, (k * 2 + half) * 2 + side],
+                        rows,
+                        pieces.at[pl.ds(rank * PARTS + yhi * 4, 4)],
+                        sems.at[which, i, yhi],
                     )
                 )
             return carry
 
         lax.fori_loop(0, 2 * SOURCES, step, 0)
 
-    return lambda: each(lambda c: c.start()), lambda: each(lambda c: c.wait())
+    def start():
+        for by_y in (True, False):
+            pl.when(side == (0 if by_y else 1))(
+                lambda by_y=by_y: each(lambda c: c.start(), by_y)
+            )
+
+    return start, lambda: each(lambda c: c.wait(), True)
 
 
 def attend_sources(info, side, q_ref, k_buf, v_buf, scratch, put, k_ready, v_ready):
@@ -189,9 +197,23 @@
         )
 
 
-def far_kernel(info, q_ref, own_ref, other_ref, o_ref, k_buf, v_buf, sems, *scratch):
-    k_start, k_ready = gather_keys(info, own_ref, other_ref, k_buf, 0, sems)
-    v_start, v_ready = gather_keys(info, own_ref, other_ref, v_buf, 1, sems)
+def order_kernel(info, own_ref, k_buf, v_buf, sems):
+    parts = [
+        key_copies(info, own_ref, info[CORE], buf, which, sems)
+        for which, buf in ((0, k_buf), (1, v_buf))
+    ]
+    for start, _ in parts:
+        start()
+    for _, ready in parts:
+        ready()
+
+
+def far_kernel(
+    info, q_ref, other_ref, k_half, v_half, o_ref, k_buf, v_buf, sems, *scratch
+):
+    side = 1 - info[CORE]
+    k_start, k_ready = key_copies(info, other_ref, side, k_buf, 0, sems)
+    v_start, v_ready = key_copies(info, other_ref, side, v_buf, 1, sems)
     k_start()
     v_start()
     lane = lax.broadcasted_iota(jnp.int32, (PIECE, HEAD_DIM), 1)
@@ -254,9 +276,14 @@
         c.wait()
 
 
-def fan_kernel(packed_ref, o_ref):
-    for i in range(16):
+def fan_first_kernel(packed_ref, o_ref):
+    for i in range(4):
         o_ref[i] = packed_ref[:, :2]
+
+
+def fan_second_kernel(line_ref, o_ref):
+    for i in range(4):
+        o_ref[i] = line_ref[...]
 
 
 SMEM = pl.BlockSpec(memory_space=pltpu.SMEM)
@@ -287,7 +314,23 @@
 LIMIT = pltpu.CompilerParams(vmem_limit_bytes=40 << 20)
 
 
-def far_part(info, q, own, other):
+SEMS = pltpu.SemaphoreType.DMA((2, 2 * SOURCES, 2))
+
+
+def order_part(info, own):
+    return pl.pallas_call(
+        order_kernel,
+        out_shape=(shape(KEYS, HEAD_DIM), shape(KEYS, HEAD_DIM)),
+        in_specs=[SMEM, ANY],
+        out_specs=(VMEM, VMEM),
+        scratch_shapes=[SEMS],
+        compiler_params=SMALL,
+        cost_estimate=pl.CostEstimate(flops=0, bytes_accessed=6_000_000, transcendentals=0),
+        name="order",
+    )(info, own)
+
+
+def far_part(info, q, other, k, v):
     return pl.pallas_call(
         far_kernel,
         out_shape=(
@@ -295,13 +338,14 @@
             shape(KEYS, HEAD_DIM),
             shape(KEYS, HEAD_DIM),
         ),
-        in_specs=[SMEM, VMEM, ANY, ANY],
+        in_specs=[SMEM, VMEM, ANY, VMEM, VMEM],
         out_specs=(VMEM, VMEM, VMEM),
-        scratch_shapes=[pltpu.SemaphoreType.DMA((2, HALF))] + SCRATCH,
+        scratch_shapes=[SEMS] + SCRATCH,
+        input_output_aliases={3: 1, 4: 2},
         compiler_params=LIMIT,
         cost_estimate=COST,
         name="far",
-    )(info, q, own, other)
+    )(info, q, other, k, v)
 
 
 def near_part(info, q, k, v):
@@ -342,19 +386,40 @@
     )(q, k, v)
 
 
-def fan(packed):
-    return pl.pallas_call(
-        fan_kernel,
-        out_shape=shape(16, SOURCES, 2, PIECE, HEAD_DIM),
+def fan(kernel, source, *sizes):
+    return pl.pallas_call(
+        kernel,
+        out_shape=shape(*sizes, SOURCES, 2, PIECE, HEAD_DIM),
         in_specs=[VMEM],
         out_specs=VMEM,
         compiler_params=SMALL,
         name="fan",
-    )(packed)
-
-
-PLANE = ("ylo", "yhi", "x")
+    )(source)
+
+
 SWAP = [(0, 1), (1, 0)]
+
+
+def place_of(ylo, core, yhi, x):
+    return ((ylo * 2 + core) * 2 + yhi) * 4 + x
+
+
+def lines(core, along_x):
+    ys = [(ylo, yhi) for ylo in range(2) for yhi in range(2)]
+    if along_x:
+        return [[place_of(ylo, core, yhi, x) for x in range(4)] for ylo, yhi in ys]
+    return [[place_of(ylo, core, yhi, x) for ylo, yhi in ys] for x in range(4)]
+
+
+def spread(rows, along_x):
+    return lax.all_to_all(
+        rows,
+        "plane",
+        0,
+        0,
+        axis_index_groups=lines(0, along_x) + lines(1, not along_x),
+        tiled=True,
+    )
 
 
 def table(visit_ids, span_order):
@@ -371,26 +436,24 @@
         (visit_ids[None, :] < jnp.arange(VISITS, dtype=jnp.int32)[:, None]).astype(jnp.int32),
         axis=1,
     )
-    place = jnp.stack(
-        [
-            lax.axis_index("ylo"),
-            lax.axis_index("core"),
-            lax.axis_index("zlo"),
-            (lax.axis_index("yhi") * 4 + lax.axis_index("x")) * PIECE,
-        ]
-    ).astype(jnp.int32)
+    at = lax.axis_index("plane")
+    place = jnp.stack([at // 16, at // 8 % 2, zlo, at % 8 * PIECE]).astype(jnp.int32)
     return jnp.concatenate([span_order, count, ordered, starts, place])
 
 
 def body(queries, key_rows, value_rows, visit_ids, span_order):
     info = table(visit_ids, span_order)
-    packed = lax.all_to_all(pack(queries, key_rows, value_rows), "zhi", 0, 0, tiled=True)
+    packed = pack(queries, key_rows, value_rows)
+    packed = lax.all_to_all(packed, "zhi", 0, 0, tiled=True)
     far_q = lax.ppermute(packed, "zlo", SWAP)
-    spread = fan(packed)
-    own = lax.all_to_all(spread, PLANE, 0, 0, tiled=True)
-    other = lax.ppermute(own, "core", SWAP)
-
-    far_out, k, v = far_part(info, far_q, own, other)
+    line = fan(fan_first_kernel, packed, 4)
+    line = spread(line, True)
+    own = fan(fan_second_kernel, line, 4, 4)
+    own = spread(own, False)
+    other = lax.ppermute(own, "plane", [(i, i ^ 8) for i in range(32)])
+    k, v = order_part(info, own)
+
+    far_out, k, v = far_part(info, far_q, other, k, v)
     sent = lax.ppermute(far_out, "zlo", SWAP)
     near_out, mass = near_part(info, packed, k, v)
     out = merge(near_out, mass, sent)
@@ -399,10 +462,8 @@
 
 
 def solution(mesh):
-    fine = Mesh(
-        mesh.devices.reshape(8, 2, 2, 2, 2, 4), ("zhi", "zlo", "ylo", "core", "yhi", "x")
-    )
-    rows = P(("zhi", "zlo", "ylo", "core", "yhi", "x"), None)
+    fine = Mesh(mesh.devices.reshape(8, 2, 32), ("zhi", "zlo", "plane"))
+    rows = P(("zhi", "zlo", "plane"), None)
     return jax.shard_map(
         body,
         mesh=fine,

time: 123 us -> 123 us (level)
  starting transfers between devices: 19.8 us -> 18.5 us
    all_to_all x2 -> x3, blocking collectives: 56 us -> 59.6 us  [the longest x1 33.2 us: body(): packed = lax.all_to_all(packed, 'zhi', 0, 0, tiled=True)]
    all_to_all x1, blocking collectives: 22.3 us -> 18.8 us  [body(): out = lax.all_to_all(out, 'zhi', 0, 0, tiled=True)]
    pallas_call x1 -> x3, Pallas kernels: 0.2 us -> 2.75 us  [the longest x1 2.5 us: order_part(): pl.pallas_call(order_kernel, out_shape=(shape(KEYS, HEAD_DIM), shape(KEYS...]
    ppermute x1, starting transfers between devices: 4.32 us -> 1.92 us  [body(): far_q = lax.ppermute(packed, 'zlo', SWAP)]
    ppermute x1, starting transfers between devices: 9.71 us -> 12 us  [body(): other = lax.ppermute(own, 'plane', [(i, i ^ 8) for i in range(32)])]
    ppermute x1, waiting for transfers between devices: 0.03 us -> 1.72 us  [body(): sent = lax.ppermute(far_out, 'zlo', SWAP)]
    pallas_call x1, Pallas kernels: 7.67 us -> 6.32 us  [far_part(): pl.pallas_call(far_kernel, out_shape=(shape(SOURCES, GROUP + 1, PIECE, HE...]
    ppermute x1, waiting for transfers between devices: 6.85 us -> 5.51 us  [body(): far_q = lax.ppermute(packed, 'zlo', SWAP)]
  transfers between devices with their start and end apart: 3 -> 3, of which waited for: 1 -> 2; matrix products, arithmetic and copies ran while one was open for 0% -> 0% of each run, Pallas kernels for 5% -> 6%
where the time goes in v2:
time: 123 us; the launch traced here: 122 us
  blocking collectives  78.4 us (64%)
  starting transfers between devices  18.5 us (15%)
  Pallas kernels  16.3 us (13%)
  waiting for transfers between devices  7.22 us (6%)
    all_to_all x1, blocking collectives, body(): packed = lax.all_to_all(packed, 'zhi', 0, 0, tiled=True)  33.2 us
    all_to_all x2, blocking collectives, spread(): lax.all_to_all(rows, 'plane', 0, 0, axis_index_groups=lines(0, along_x) +...  26.4 us
    all_to_all x1, blocking collectives, body(): out = lax.all_to_all(out, 'zhi', 0, 0, tiled=True)  18.8 us
    ppermute x1, starting transfers between devices, body(): other = lax.ppermute(own, 'plane', [(i, i ^ 8) for i in range(32)])  12 us
    pallas_call x1, Pallas kernels, far_part(): pl.pallas_call(far_kernel, out_shape=(shape(SOURCES, GROUP + 1, PIECE, HE...  6.32 us
    ppermute x1, waiting for transfers between devices, body(): far_q = lax.ppermute(packed, 'zlo', SWAP)  5.51 us
    pallas_call x1, Pallas kernels, near_part(): pl.pallas_call(near_kernel, out_shape=(shape(SOURCES, GROUP, PIECE, HEAD_...  4.62 us
    ppermute x1, starting transfers between devices, body(): sent = lax.ppermute(far_out, 'zlo', SWAP)  4.52 us
  transfers between devices with their start and end apart: 3, of which 2 were waited for; matrix products, arithmetic and copies ran while one was open for 0% of the time, Pallas kernels for 6%

profile of v2, /device:TPU:1, one launch (start us, length us, event | category | flops | bytes accessed | tf_op | source)
XLA Modules:
  0.0 121.8 jit_solution(15555585705838909514)
XLA Ops:
  0.0 2.1 %pack.1 = bf16[8,6,24,128]{3,2,1,0:T(8,128)(2,1)} custom-call(bf16[24,4096]{1,0:T(8,128)(2,1)} %q_ref.1, bf16[24,1024]{1,0:T(8,128)(2,1)} %k_ref.1, bf16[24,1024]{1,0:T(8,128)(2,1)} %v_ref.1), custom_call_target="tpu_custom_call" | custom-call | tf_op jit(solution)/shard_map/pack/pallas_call | solution.py:379
  2.1 33.2 %all_to_all.20.packed_ref.q_ref = bf16[8,6,24,128]{3,2,1,0:T(8,128)(2,1)S(1)} all-to-all(bf16[8,6,24,128]{3,2,1,0:T(8,128)(2,1)} %pack.1), channel_id=1, replica_groups=mesh['zhi'=8,'zlo'=2,'plane'=32] {'zhi'}, dimensions={0} | all-to-all | bytes 589824 | tf_op jit(solution)/shard_map/all_to_all | solution.py:447
  35.3 0.1 fan.2
  35.4 9.9 %all_to_all.21.line_ref = bf16[4,8,2,24,128]{4,3,2,1,0:T(8,128)(2,1)S(1)} all-to-all(bf16[4,8,2,24,128]{4,3,2,1,0:T(8,128)(2,1)S(1)} %fan.2), channel_id=1, replica_groups={{0,1,2,3},{4,5,6,7},{16,17,18,19},{20,21,22,23},{8,12,24,28},{9,13,25,2..., dimensions={0} | all-to-all | bytes 786432 | tf_op jit(solution)/shard_map/all_to_all | solution.py:415
  45.3 0.2 fan.3
  45.5 0.0 copy-start.1
  45.5 0.0 copy-start
  45.5 16.5 %all_to_all.22.own_ref = bf16[4,4,8,2,24,128]{5,4,3,2,1,0:T(8,128)(2,1)S(1)} all-to-all(bf16[4,4,8,2,24,128]{5,4,3,2,1,0:T(8,128)(2,1)S(1)} %fan.3), channel_id=1, replica_groups={{0,4,16,20},{1,5,17,21},{2,6,18,22},{3,7,19,23},{8,9,10,11},{12,13,14,1..., dimensions={0} | all-to-all | bytes 3145728 | tf_op jit(solution)/shard_map/all_to_all | solution.py:415
  62.0 12.0 %collective-permute-start.1 = (bf16[4,4,8,2,24,128]{5,4,3,2,1,0:T(8,128)(2,1)S(1)}, bf16[4,4,8,2,24,128]{5,4,3,2,1,0:T(8,128)(2,1)S(1)}, u32[]{:S(2)}, u32[]{:S(2)}) collective-permute-start(bf16[4,4,8,2,24,128]{5,4,3,2,1,0:T(8,128)(2,1)S(1)} %all_to_all.22.own_ref), channel_id=1, source_target_pairs={{0,8},{1,9},{2,10},{3,11},{4,12},{5,13},{6,14},{7,15},{8,0},{9,1},... | collective-permute-start | bytes 4718600 | tf_op jit(solution)/shard_map/ppermute | solution.py:453
  74.1 1.9 %collective-permute-start = (bf16[8,6,24,128]{3,2,1,0:T(8,128)(2,1)S(1)}, bf16[8,6,24,128]{3,2,1,0:T(8,128)(2,1)}, u32[]{:S(2)}, u32[]{:S(2)}) collective-permute-start(bf16[8,6,24,128]{3,2,1,0:T(8,128)(2,1)S(1)} %all_to_all.20.packed_ref.q_ref), channel_id=1, source_target_pairs={{0,32},{32,0},{1,33},{33,1},{2,34},{34,2},{3,35},{35,3},{4,36},{36... | collective-permute-start | bytes 884744 | tf_op jit(solution)/shard_map/ppermute | solution.py:448
  76.0 0.0 copy-done.1
  76.1 0.1 convert_reduce_fusion.1
  76.2 0.1 slice.3
  76.2 0.1 convert_reduce_fusion.2
  76.3 0.0 copy-done
  76.4 0.2 convert_reduce_fusion
  76.6 0.1 concatenate.3.info
  76.7 2.5 %order.1 = (bf16[6144,128]{1,0:T(8,128)(2,1)S(1)}, bf16[6144,128]{1,0:T(8,128)(2,1)S(1)}) custom-call(s32[169]{0:T(256)S(1)} %concatenate.3.info, bf16[4,4,8,2,24,128]{5,4,3,2,1,0:T(8,128)(2,1)S(1)} %all_to_all.22.own_ref), custom_call_target="tpu_custom_call" | custom-call | bytes 6000000 | tf_op jit(solution)/shard_map/order/pallas_call | solution.py:321
  79.2 5.5 %collective-permute-done.q_ref = bf16[8,6,24,128]{3,2,1,0:T(8,128)(2,1)} collective-permute-done((bf16[8,6,24,128]{3,2,1,0:T(8,128)(2,1)S(1)}, bf16[8,6,24,128]{3,2,1,0:T(8,128)(2,1)}, u32[]{:S(2)}, u32[]{:S(2)}) %collective-permute-start) | collective-permute-done | bytes 294944 | tf_op jit(solution)/shard_map/ppermute | solution.py:448
  84.7 0.0 collective-permute-done.1.other_ref
  84.7 6.3 %far.1 = (bf16[8,5,24,128]{3,2,1,0:T(8,128)(2,1)S(1)}, bf16[6144,128]{1,0:T(8,128)(2,1)S(1)}, bf16[6144,128]{1,0:T(8,128)(2,1)S(1)}) custom-call(s32[169]{0:T(256)S(1)} %concatenate.3.info, bf16[8,6,24,128]{3,2,1,0:T(8,128)(2,1)} %collective-permute-done.q_ref, ...), custom_call_target="tpu_custom_call", output_to_operand_aliasing={{1}: (3, {}), {2}: (4, {})} | custom-call | flops 6000000000 | bytes 4000000 | tf_op jit(solution)/shard_map/far/pallas_call | solution.py:334
  91.0 4.5 %collective-permute-start.2 = (bf16[8,5,24,128]{3,2,1,0:T(8,128)(2,1)S(1)}, bf16[8,5,24,128]{3,2,1,0:T(8,128)(2,1)S(1)}, u32[]{:S(2)}, u32[]{:S(2)}) collective-permute-start(bf16[8,5,24,128]{3,2,1,0:T(8,128)(2,1)S(1)} %get-tuple-element.18), channel_id=1, source_target_pairs={{0,32},{32,0},{1,33},{33,1},{2,34},{34,2},{3,35},{35,3},{4,36},{36... | collective-permute-start | bytes 737288 | tf_op jit(solution)/shard_map/ppermute | solution.py:457
  95.5 4.6 %near.1 = (f32[8,4,24,128]{3,2,1,0:T(8,128)S(1)}, f32[8,4,24,128]{3,2,1,0:T(8,128)S(1)}) custom-call(s32[169]{0:T(256)S(1)} %concatenate.3.info, bf16[8,6,24,128]{3,2,1,0:T(8,128)(2,1)S(1)} %all_to_all.20.packed_ref.q_ref, bf16[6144,128]{1,0:T(8,128)(2,1)S(1)} %get-tuple-element.14.k_buf, bf16[6144,128]{1,0:T(8,128)(2,1)S(1)} %get-tuple-element.15.v_buf), custom_call_target="tpu_custom_call" | custom-call | flops 6000000000 | bytes 4000000 | tf_op jit(solution)/shard_map/near/pallas_call | solution.py:352
  100.1 1.7 %collective-permute-done.2.far_ref = bf16[8,5,24,128]{3,2,1,0:T(8,128)(2,1)S(1)} collective-permute-done((bf16[8,5,24,128]{3,2,1,0:T(8,128)(2,1)S(1)}, bf16[8,5,24,128]{3,2,1,0:T(8,128)(2,1)S(1)}, u32[]{:S(2)}, u32[]{:S(2)}) %collective-permute-start.2) | collective-permute-done | bytes 245792 | tf_op jit(solution)/shard_map/ppermute | solution.py:457
  101.9 0.5 merge.1
  102.3 18.8 %all_to_all.23 = bf16[8,24,512]{2,1,0:T(8,128)(2,1)S(1)} all-to-all(bf16[8,24,512]{2,1,0:T(8,128)(2,1)S(1)} %merge.1), channel_id=1, replica_groups=mesh['zhi'=8,'zlo'=2,'plane'=32] {'zhi'}, dimensions={0} | all-to-all | bytes 393216 | tf_op jit(solution)/shard_map/all_to_all | solution.py:460
  121.2 0.7 copy.10
  (1 shorter events, 0.0 us)
Async XLA Ops:
  45.5 30.6 %copy-start.1 = (s32[64]{0:T(128)S(1)}, s32[64]{0:T(128)}, u32[]{:S(2)}) copy-start(s32[64]{0:T(128)} %param.9) | copy-start | bytes 772
  45.5 30.8 %copy-start = (s32[12288]{0:T(1024)S(1)}, s32[12288]{0:T(1024)}, u32[]{:S(2)}) copy-start(s32[12288]{0:T(1024)} %param.8) | copy-start | bytes 147460
  62.0 22.7 %collective-permute-start.1 = (bf16[4,4,8,2,24,128]{5,4,3,2,1,0:T(8,128)(2,1)S(1)}, bf16[4,4,8,2,24,128]{5,4,3,2,1,0:T(8,128)(2,1)S(1)}, u32[]{:S(2)}, u32[]{:S(2)}) collective-permute-start(bf16[4,4,8,2,24,128]{5,4,3,2,1,0:T(8,128)(2,1)S(1)} %all_to_all.22.own_ref), channel_id=1, source_target_pairs={{0,8},{1,9},{2,10},{3,11},{4,12},{5,13},{6,14},{7,15},{8,0},{9,1},... | collective-permute-start | bytes 4718600 | tf_op jit(solution)/shard_map/ppermute | solution.py:453
  74.1 10.6 %collective-permute-start = (bf16[8,6,24,128]{3,2,1,0:T(8,128)(2,1)S(1)}, bf16[8,6,24,128]{3,2,1,0:T(8,128)(2,1)}, u32[]{:S(2)}, u32[]{:S(2)}) collective-permute-start(bf16[8,6,24,128]{3,2,1,0:T(8,128)(2,1)S(1)} %all_to_all.20.packed_ref.q_ref), channel_id=1, source_target_pairs={{0,32},{32,0},{1,33},{33,1},{2,34},{34,2},{3,35},{35,3},{4,36},{36... | collective-permute-start | bytes 884744 | tf_op jit(solution)/shard_map/ppermute | solution.py:448
  91.0 10.9 %collective-permute-start.2 = (bf16[8,5,24,128]{3,2,1,0:T(8,128)(2,1)S(1)}, bf16[8,5,24,128]{3,2,1,0:T(8,128)(2,1)S(1)}, u32[]{:S(2)}, u32[]{:S(2)}) collective-permute-start(bf16[8,5,24,128]{3,2,1,0:T(8,128)(2,1)S(1)} %get-tuple-element.18), channel_id=1, source_target_pairs={{0,32},{32,0},{1,33},{33,1},{2,34},{34,2},{3,35},{35,3},{4,36},{36... | collective-permute-start | bytes 737288 | tf_op jit(solution)/shard_map/ppermute | solution.py:457

commit v3 on v2

--- a/solution.py
+++ b/solution.py
@@ -39,32 +39,23 @@
     zlo = info[ZLO]
     pieces = buf.reshape(HALF * PARTS, PIECE, HEAD_DIM)
 
-    def each(act, by_y):
+    def each(act):
         def step(i, carry):
             k, half = i // 2, i % 2
             span = info[ORDER + (k * 2 + zlo) * 4 + half * 2 + side]
             rank = info[COUNT + span]
-            for yhi in range(2):
-                y = half * 2 + yhi
-                rows = src.at[y, :, k, which] if by_y else src.at[:, y, k, which]
-                act(
-                    pltpu.make_async_copy(
-                        rows,
-                        pieces.at[pl.ds(rank * PARTS + yhi * 4, 4)],
-                        sems.at[which, i, yhi],
-                    )
+            act(
+                pltpu.make_async_copy(
+                    src.at[pl.ds(half * PARTS, PARTS), k, which],
+                    pieces.at[pl.ds(rank * PARTS, PARTS)],
+                    sems.at[which, i],
                 )
+            )
             return carry
 
         lax.fori_loop(0, 2 * SOURCES, step, 0)
 
-    def start():
-        for by_y in (True, False):
-            pl.when(side == (0 if by_y else 1))(
-                lambda by_y=by_y: each(lambda c: c.start(), by_y)
-            )
-
-    return start, lambda: each(lambda c: c.wait(), True)
+    return lambda: each(lambda c: c.start()), lambda: each(lambda c: c.wait())
 
 
 def attend_sources(info, side, q_ref, k_buf, v_buf, scratch, put, k_ready, v_ready):
@@ -276,14 +267,9 @@
         c.wait()
 
 
-def fan_first_kernel(packed_ref, o_ref):
-    for i in range(4):
+def fan_kernel(packed_ref, o_ref):
+    for i in range(16):
         o_ref[i] = packed_ref[:, :2]
-
-
-def fan_second_kernel(line_ref, o_ref):
-    for i in range(4):
-        o_ref[i] = line_ref[...]
 
 
 SMEM = pl.BlockSpec(memory_space=pltpu.SMEM)
@@ -314,7 +300,7 @@
 LIMIT = pltpu.CompilerParams(vmem_limit_bytes=40 << 20)
 
 
-SEMS = pltpu.SemaphoreType.DMA((2, 2 * SOURCES, 2))
+SEMS = pltpu.SemaphoreType.DMA((2, 2 * SOURCES))
 
 
 def order_part(info, own):
@@ -386,40 +372,22 @@
     )(q, k, v)
 
 
-def fan(kernel, source, *sizes):
-    return pl.pallas_call(
-        kernel,
-        out_shape=shape(*sizes, SOURCES, 2, PIECE, HEAD_DIM),
+def fan(packed):
+    return pl.pallas_call(
+        fan_kernel,
+        out_shape=shape(16, SOURCES, 2, PIECE, HEAD_DIM),
         in_specs=[VMEM],
         out_specs=VMEM,
         compiler_params=SMALL,
         name="fan",
-    )(source)
+    )(packed)
 
 
 SWAP = [(0, 1), (1, 0)]
-
-
-def place_of(ylo, core, yhi, x):
-    return ((ylo * 2 + core) * 2 + yhi) * 4 + x
-
-
-def lines(core, along_x):
-    ys = [(ylo, yhi) for ylo in range(2) for yhi in range(2)]
-    if along_x:
-        return [[place_of(ylo, core, yhi, x) for x in range(4)] for ylo, yhi in ys]
-    return [[place_of(ylo, core, yhi, x) for ylo, yhi in ys] for x in range(4)]
-
-
-def spread(rows, along_x):
-    return lax.all_to_all(
-        rows,
-        "plane",
-        0,
-        0,
-        axis_index_groups=lines(0, along_x) + lines(1, not along_x),
-        tiled=True,
-    )
+PLANE = [
+    [((ylo * 2 + core) * 2 + yhi) * 4 + x for ylo in range(2) for yhi in range(2) for x in range(4)]
+    for core in range(2)
+]
 
 
 def table(visit_ids, span_order):
@@ -446,10 +414,10 @@
     packed = pack(queries, key_rows, value_rows)
     packed = lax.all_to_all(packed, "zhi", 0, 0, tiled=True)
     far_q = lax.ppermute(packed, "zlo", SWAP)
-    line = fan(fan_first_kernel, packed, 4)
-    line = spread(line, True)
-    own = fan(fan_second_kernel, line, 4, 4)
-    own = spread(own, False)
+    spread = fan(packed)
+    own = lax.all_to_all(
+        spread, "plane", 0, 0, axis_index_groups=PLANE, tiled=True
+    )
     other = lax.ppermute(own, "plane", [(i, i ^ 8) for i in range(32)])
     k, v = order_part(info, own)
 

time: 123 us -> 121 us (0.984)
  waiting for transfers between devices: 7.22 us -> 5.9 us
    all_to_all x2 -> x1, blocking collectives: 26.4 us -> 22.8 us  [body(): lax.all_to_all(spread, 'plane', 0, 0, axis_index_groups=PLANE, tiled=True)]
    all_to_all x1, blocking collectives: 18.8 us -> 22.2 us  [body(): out = lax.all_to_all(out, 'zhi', 0, 0, tiled=True)]
    ppermute x1, starting transfers between devices: 1.92 us -> 4.32 us  [body(): far_q = lax.ppermute(packed, 'zlo', SWAP)]
    ppermute x1, starting transfers between devices: 12 us -> 9.71 us  [body(): other = lax.ppermute(own, 'plane', [(i, i ^ 8) for i in range(32)])]
where the time goes in v3:
time: 121 us; the launch traced here: 120 us
  blocking collectives  78.2 us (65%)
  starting transfers between devices  19.4 us (16%)
  Pallas kernels  15.3 us (13%)
  waiting for transfers between devices  5.9 us (5%)
    all_to_all x1, blocking collectives, body(): packed = lax.all_to_all(packed, 'zhi', 0, 0, tiled=True)  33.2 us
    all_to_all x1, blocking collectives, body(): lax.all_to_all(spread, 'plane', 0, 0, axis_index_groups=PLANE, tiled=True)  22.8 us
    all_to_all x1, blocking collectives, body(): out = lax.all_to_all(out, 'zhi', 0, 0, tiled=True)  22.2 us
    ppermute x1, starting transfers between devices, body(): other = lax.ppermute(own, 'plane', [(i, i ^ 8) for i in range(32)])  9.71 us
    pallas_call x1, Pallas kernels, far_part(): pl.pallas_call(far_kernel, out_shape=(shape(SOURCES, GROUP + 1, PIECE, HE...  5.84 us
    ppermute x1, starting transfers between devices, body(): sent = lax.ppermute(far_out, 'zlo', SWAP)  5.41 us
    ppermute x1, waiting for transfers between devices, body(): far_q = lax.ppermute(packed, 'zlo', SWAP)  4.81 us
    pallas_call x1, Pallas kernels, near_part(): pl.pallas_call(near_kernel, out_shape=(shape(SOURCES, GROUP, PIECE, HEAD_...  4.62 us
  transfers between devices with their start and end apart: 3, of which 2 were waited for; matrix products, arithmetic and copies ran while one was open for 0% of the time, Pallas kernels for 6%

profile of v3, /device:TPU:1, one launch (start us, length us, event | category | flops | bytes accessed | tf_op | source)
XLA Modules:
  0.0 120.3 jit_solution(17842048134670025269)
XLA Ops:
  0.0 2.1 %pack.1 = bf16[8,6,24,128]{3,2,1,0:T(8,128)(2,1)} custom-call(bf16[24,4096]{1,0:T(8,128)(2,1)} %q_ref.1, bf16[24,1024]{1,0:T(8,128)(2,1)} %k_ref.1, bf16[24,1024]{1,0:T(8,128)(2,1)} %v_ref.1), custom_call_target="tpu_custom_call" | custom-call | tf_op jit(solution)/shard_map/pack/pallas_call | solution.py:365
  2.1 33.2 %all_to_all.15.packed_ref.q_ref = bf16[8,6,24,128]{3,2,1,0:T(8,128)(2,1)S(1)} all-to-all(bf16[8,6,24,128]{3,2,1,0:T(8,128)(2,1)} %pack.1), channel_id=1, replica_groups=mesh['zhi'=8,'zlo'=2,'plane'=32] {'zhi'}, dimensions={0} | all-to-all | bytes 589824 | tf_op jit(solution)/shard_map/all_to_all | solution.py:415
  35.3 0.2 fan.1
  35.5 0.0 copy-start.1
  35.5 0.0 copy-start
  35.5 22.8 %all_to_all.16.own_ref = bf16[16,8,2,24,128]{4,3,2,1,0:T(8,128)(2,1)S(1)} all-to-all(bf16[16,8,2,24,128]{4,3,2,1,0:T(8,128)(2,1)S(1)} %fan.1), channel_id=1, replica_groups={{0,1,2,3,4,5,6,7,16,17,18,19,20,21,22,23},{8,9,10,11,12,13,14,15,24,25,..., dimensions={0} | all-to-all | bytes 3145728 | tf_op jit(solution)/shard_map/all_to_all | solution.py:418
  58.3 9.7 %collective-permute-start.1 = (bf16[16,8,2,24,128]{4,3,2,1,0:T(8,128)(2,1)S(1)}, bf16[16,8,2,24,128]{4,3,2,1,0:T(8,128)(2,1)S(1)}, u32[]{:S(2)}, u32[]{:S(2)}) collective-permute-start(bf16[16,8,2,24,128]{4,3,2,1,0:T(8,128)(2,1)S(1)} %all_to_all.16.own_ref), channel_id=1, source_target_pairs={{0,8},{1,9},{2,10},{3,11},{4,12},{5,13},{6,14},{7,15},{8,0},{9,1},... | collective-permute-start | bytes 4718600 | tf_op jit(solution)/shard_map/ppermute | solution.py:421
  68.1 4.3 %collective-permute-start = (bf16[8,6,24,128]{3,2,1,0:T(8,128)(2,1)S(1)}, bf16[8,6,24,128]{3,2,1,0:T(8,128)(2,1)}, u32[]{:S(2)}, u32[]{:S(2)}) collective-permute-start(bf16[8,6,24,128]{3,2,1,0:T(8,128)(2,1)S(1)} %all_to_all.15.packed_ref.q_ref), channel_id=1, source_target_pairs={{0,32},{32,0},{1,33},{33,1},{2,34},{34,2},{3,35},{35,3},{4,36},{36... | collective-permute-start | bytes 884744 | tf_op jit(solution)/shard_map/ppermute | solution.py:416
  72.4 0.0 copy-done.1
  72.4 0.1 convert_reduce_fusion.1
  72.5 0.1 slice.3
  72.6 0.1 convert_reduce_fusion.2
  72.7 0.0 copy-done
  72.7 0.2 convert_reduce_fusion
  72.9 0.1 concatenate.3.info
  73.0 2.0 %order.1 = (bf16[6144,128]{1,0:T(8,128)(2,1)S(1)}, bf16[6144,128]{1,0:T(8,128)(2,1)S(1)}) custom-call(s32[169]{0:T(256)S(1)} %concatenate.3.info, bf16[16,8,2,24,128]{4,3,2,1,0:T(8,128)(2,1)S(1)} %all_to_all.16.own_ref), custom_call_target="tpu_custom_call" | custom-call | bytes 6000000 | tf_op jit(solution)/shard_map/order/pallas_call | solution.py:307
  75.1 4.8 %collective-permute-done.q_ref = bf16[8,6,24,128]{3,2,1,0:T(8,128)(2,1)} collective-permute-done((bf16[8,6,24,128]{3,2,1,0:T(8,128)(2,1)S(1)}, bf16[8,6,24,128]{3,2,1,0:T(8,128)(2,1)}, u32[]{:S(2)}, u32[]{:S(2)}) %collective-permute-start) | collective-permute-done | bytes 294944 | tf_op jit(solution)/shard_map/ppermute | solution.py:416
  79.9 0.0 collective-permute-done.1.other_ref
  79.9 5.8 %far.1 = (bf16[8,5,24,128]{3,2,1,0:T(8,128)(2,1)S(1)}, bf16[6144,128]{1,0:T(8,128)(2,1)S(1)}, bf16[6144,128]{1,0:T(8,128)(2,1)S(1)}) custom-call(s32[169]{0:T(256)S(1)} %concatenate.3.info, bf16[8,6,24,128]{3,2,1,0:T(8,128)(2,1)} %collective-permute-done.q_ref, ...), custom_call_target="tpu_custom_call", output_to_operand_aliasing={{1}: (3, {}), {2}: (4, {})} | custom-call | flops 6000000000 | bytes 4000000 | tf_op jit(solution)/shard_map/far/pallas_call | solution.py:320
  85.7 5.4 %collective-permute-start.2 = (bf16[8,5,24,128]{3,2,1,0:T(8,128)(2,1)S(1)}, bf16[8,5,24,128]{3,2,1,0:T(8,128)(2,1)S(1)}, u32[]{:S(2)}, u32[]{:S(2)}) collective-permute-start(bf16[8,5,24,128]{3,2,1,0:T(8,128)(2,1)S(1)} %get-tuple-element.18), channel_id=1, source_target_pairs={{0,32},{32,0},{1,33},{33,1},{2,34},{34,2},{3,35},{35,3},{4,36},{36... | collective-permute-start | bytes 737288 | tf_op jit(solution)/shard_map/ppermute | solution.py:425
  91.1 4.6 %near.1 = (f32[8,4,24,128]{3,2,1,0:T(8,128)S(1)}, f32[8,4,24,128]{3,2,1,0:T(8,128)S(1)}) custom-call(s32[169]{0:T(256)S(1)} %concatenate.3.info, bf16[8,6,24,128]{3,2,1,0:T(8,128)(2,1)S(1)} %all_to_all.15.packed_ref.q_ref, bf16[6144,128]{1,0:T(8,128)(2,1)S(1)} %get-tuple-element.14.k_buf, bf16[6144,128]{1,0:T(8,128)(2,1)S(1)} %get-tuple-element.15.v_buf), custom_call_target="tpu_custom_call" | custom-call | flops 6000000000 | bytes 4000000 | tf_op jit(solution)/shard_map/near/pallas_call | solution.py:338
  95.8 1.1 collective-permute-done.2.far_ref
  96.9 0.5 merge.1
  97.3 22.2 %all_to_all.17 = bf16[8,24,512]{2,1,0:T(8,128)(2,1)S(1)} all-to-all(bf16[8,24,512]{2,1,0:T(8,128)(2,1)S(1)} %merge.1), channel_id=1, replica_groups=mesh['zhi'=8,'zlo'=2,'plane'=32] {'zhi'}, dimensions={0} | all-to-all | bytes 393216 | tf_op jit(solution)/shard_map/all_to_all | solution.py:428
  119.6 0.7 copy.10
  (1 shorter events, 0.0 us)
Async XLA Ops:
  35.5 36.9 %copy-start.1 = (s32[64]{0:T(128)S(1)}, s32[64]{0:T(128)}, u32[]{:S(2)}) copy-start(s32[64]{0:T(128)} %param.9) | copy-start | bytes 772
  35.5 37.2 %copy-start = (s32[12288]{0:T(1024)S(1)}, s32[12288]{0:T(1024)}, u32[]{:S(2)}) copy-start(s32[12288]{0:T(1024)} %param.8) | copy-start | bytes 147460
  58.3 21.6 %collective-permute-start.1 = (bf16[16,8,2,24,128]{4,3,2,1,0:T(8,128)(2,1)S(1)}, bf16[16,8,2,24,128]{4,3,2,1,0:T(8,128)(2,1)S(1)}, u32[]{:S(2)}, u32[]{:S(2)}) collective-permute-start(bf16[16,8,2,24,128]{4,3,2,1,0:T(8,128)(2,1)S(1)} %all_to_all.16.own_ref), channel_id=1, source_target_pairs={{0,8},{1,9},{2,10},{3,11},{4,12},{5,13},{6,14},{7,15},{8,0},{9,1},... | collective-permute-start | bytes 4718600 | tf_op jit(solution)/shard_map/ppermute | solution.py:421
  68.1 11.8 %collective-permute-start = (bf16[8,6,24,128]{3,2,1,0:T(8,128)(2,1)S(1)}, bf16[8,6,24,128]{3,2,1,0:T(8,128)(2,1)}, u32[]{:S(2)}, u32[]{:S(2)}) collective-permute-start(bf16[8,6,24,128]{3,2,1,0:T(8,128)(2,1)S(1)} %all_to_all.15.packed_ref.q_ref), channel_id=1, source_target_pairs={{0,32},{32,0},{1,33},{33,1},{2,34},{34,2},{3,35},{35,3},{4,36},{36... | collective-permute-start | bytes 884744 | tf_op jit(solution)/shard_map/ppermute | solution.py:416
  85.7 11.1 %collective-permute-start.2 = (bf16[8,5,24,128]{3,2,1,0:T(8,128)(2,1)S(1)}, bf16[8,5,24,128]{3,2,1,0:T(8,128)(2,1)S(1)}, u32[]{:S(2)}, u32[]{:S(2)}) collective-permute-start(bf16[8,5,24,128]{3,2,1,0:T(8,128)(2,1)S(1)} %get-tuple-element.18), channel_id=1, source_target_pairs={{0,32},{32,0},{1,33},{33,1},{2,34},{34,2},{3,35},{35,3},{4,36},{36... | collective-permute-start | bytes 737288 | tf_op jit(solution)/shard_map/ppermute | solution.py:425

commit v4 on v3

--- a/solution.py
+++ b/solution.py
@@ -33,33 +33,29 @@
 CORE = YLO + 1
 ZLO = YLO + 2
 FIRST = YLO + 3
-
-
-def key_copies(info, src, side, buf, which, sems):
+TOTAL = YLO + 4
+LIST = TOTAL + 2
+ITEMS = SOURCES * TILES + UNROLL
+
+
+def take_keys(info, src, side, k_buf, v_buf):
     zlo = info[ZLO]
-    pieces = buf.reshape(HALF * PARTS, PIECE, HEAD_DIM)
-
-    def each(act):
-        def step(i, carry):
-            k, half = i // 2, i % 2
-            span = info[ORDER + (k * 2 + zlo) * 4 + half * 2 + side]
-            rank = info[COUNT + span]
-            act(
-                pltpu.make_async_copy(
-                    src.at[pl.ds(half * PARTS, PARTS), k, which],
-                    pieces.at[pl.ds(rank * PARTS, PARTS)],
-                    sems.at[which, i],
-                )
-            )
-            return carry
-
-        lax.fori_loop(0, 2 * SOURCES, step, 0)
-
-    return lambda: each(lambda c: c.start()), lambda: each(lambda c: c.wait())
-
-
-def attend_sources(info, side, q_ref, k_buf, v_buf, scratch, put, k_ready, v_ready):
-    s_buf, q_buf, low_buf, pos_buf, best, top_buf, total, acc, item_n, item_j = scratch
+    pieces = [buf.reshape(HALF * PARTS, PIECE, HEAD_DIM) for buf in (k_buf, v_buf)]
+
+    def step(i, carry):
+        k, half = i // 2, i % 2
+        span = info[ORDER + (k * 2 + zlo) * 4 + half * 2 + side]
+        rank = info[COUNT + span]
+        for part in range(PARTS):
+            for which, buf in enumerate(pieces):
+                buf[rank * PARTS + part] = src[half * PARTS + part, k, which]
+        return carry
+
+    lax.fori_loop(0, 2 * SOURCES, step, 0)
+
+
+def attend_sources(info, side, q_ref, k_buf, v_buf, scratch, put):
+    s_buf, q_buf, low_buf, pos_buf, best, top_buf, total, acc = scratch
     ylo, core, first = info[YLO], info[CORE], info[FIRST]
     inside = lax.broadcasted_iota(jnp.int32, (PIECE, HEAD_DIM), 0)
     lane = lax.broadcasted_iota(jnp.int32, (1, HEAD_DIM), 1)
@@ -70,42 +66,29 @@
             low = jnp.where(info[START + v] <= pos, info[START + v], low)
         return low
 
-    count = jnp.int32(0)
     for n in range(SOURCES):
         span = info[ORDER + (n * 2 + side) * 4 + ylo * 2 + core]
-        p0 = span * SPAN_ROWS + first
-        pos = p0 + inside
+        pos = span * SPAN_ROWS + first + inside
         pos_buf[n] = pos
         low_buf[n] = start_of(pos)
         q_buf[n] = (
             q_ref[n, 2:].astype(jnp.float32).reshape(ROWS, HEAD_DIM).astype(jnp.bfloat16)
         )
-        tile_a = info[COUNT + start_of(p0) // SPAN_ROWS] // PER_TILE
-        tile_b = (info[COUNT + span + 1] + PER_TILE - 1) // PER_TILE
-
-        def note(j, at, n=n):
-            item_n[at] = n
-            item_j[at] = j
-            return at + 1
-
-        count = lax.fori_loop(tile_a, tile_b, note, count)
-    for u in range(UNROLL - 1):
-        item_n[count + u] = SOURCES
-        item_j[count + u] = 0
-    steps = (count + UNROLL - 1) // UNROLL
-
-    for n in range(SOURCES):
-        for u in range(UNROLL):
-            best[u, n] = jnp.full((ROWS, HEAD_DIM), -jnp.inf, jnp.float32)
-            total[u, n] = jnp.zeros((ROWS, HEAD_DIM), jnp.float32)
-            acc[u, n] = jnp.zeros((ROWS, HEAD_DIM), jnp.float32)
-
-    k_ready()
+        best[n] = jnp.full((ROWS, HEAD_DIM), -jnp.inf, jnp.float32)
+        total[n] = jnp.zeros((ROWS, HEAD_DIM), jnp.float32)
+        acc[n] = jnp.zeros((ROWS, HEAD_DIM), jnp.float32)
+    far = jnp.where(side == info[ZLO], 0, 1)
+    steps = (info[TOTAL + far] + UNROLL - 1) // UNROLL
+    listed = LIST + far * ITEMS
+
+    def item(at):
+        entry = info[listed + at]
+        return entry // 16, entry % 16
 
     def scores(i, carry):
         for u in range(UNROLL):
             at = i * UNROLL + u
-            slot, j = item_n[at], item_j[at]
+            slot, j = item(at)
             n = jnp.minimum(slot, SOURCES - 1)
             s = lax.dot_general(
                 q_buf[n],
@@ -118,7 +101,7 @@
             base = [
                 (info[SORTED + j * PER_TILE + w] - w) * SPAN_ROWS for w in range(PER_TILE)
             ]
-            high = best[u, slot].reshape(GROUP, PIECE, HEAD_DIM)
+            high = best[slot].reshape(GROUP, PIECE, HEAD_DIM)
             for c in range(TILE // HEAD_DIM):
                 left = c * HEAD_DIM // SPAN_ROWS
                 right = (c * HEAD_DIM + HEAD_DIM - 1) // SPAN_ROWS
@@ -133,28 +116,23 @@
                 )
                 s_buf[at, :, c * HEAD_DIM : (c + 1) * HEAD_DIM] = part.reshape(ROWS, HEAD_DIM)
                 high = jnp.maximum(high, part)
-            best[u, slot] = high.reshape(ROWS, HEAD_DIM)
+            best[slot] = high.reshape(ROWS, HEAD_DIM)
         return carry
 
     lax.fori_loop(0, steps, scores, 0)
 
     for n in range(SOURCES):
-        high = best[0, n]
-        for u in range(1, UNROLL):
-            high = jnp.maximum(high, best[u, n])
-        top = jnp.max(high, axis=1, keepdims=True)
+        top = jnp.max(best[n], axis=1, keepdims=True)
         top_buf[n] = jnp.broadcast_to(top, (ROWS, HEAD_DIM))
-
-    v_ready()
 
     def mix(i, carry):
         for u in range(UNROLL):
             at = i * UNROLL + u
-            slot, j = item_n[at], item_j[at]
+            slot, j = item(at)
             n = jnp.minimum(slot, SOURCES - 1)
             top = top_buf[n]
             top = jnp.where(top > -jnp.inf, top, 0.0)
-            part_sum = total[u, slot]
+            part_sum = total[slot]
             parts = []
             for c in range(TILE // HEAD_DIM):
                 w = jnp.exp2(
@@ -162,8 +140,8 @@
                 )
                 part_sum = part_sum + w
                 parts.append(w.astype(jnp.bfloat16))
-            total[u, slot] = part_sum
-            acc[u, slot] = acc[u, slot] + jnp.dot(
+            total[slot] = part_sum
+            acc[slot] = acc[slot] + jnp.dot(
                 jnp.concatenate(parts, axis=1),
                 v_buf[pl.ds(pl.multiple_of(j * TILE, TILE), TILE), :],
                 preferred_element_type=jnp.float32,
@@ -174,10 +152,7 @@
 
     for n in range(SOURCES):
         top = top_buf[n]
-        whole, out = total[0, n], acc[0, n]
-        for u in range(1, UNROLL):
-            whole, out = whole + total[u, n], out + acc[u, n]
-        whole = jnp.sum(whole, axis=1, keepdims=True)
+        whole, out = jnp.sum(total[n], axis=1, keepdims=True), acc[n]
         some = top > -jnp.inf
         safe = jnp.where(some, whole, 1.0)
         mass = jnp.where(some, top * SCALE_LOG2 + jnp.log2(safe), NOTHING)
@@ -188,25 +163,12 @@
         )
 
 
-def order_kernel(info, own_ref, k_buf, v_buf, sems):
-    parts = [
-        key_copies(info, own_ref, info[CORE], buf, which, sems)
-        for which, buf in ((0, k_buf), (1, v_buf))
-    ]
-    for start, _ in parts:
-        start()
-    for _, ready in parts:
-        ready()
-
-
-def far_kernel(
-    info, q_ref, other_ref, k_half, v_half, o_ref, k_buf, v_buf, sems, *scratch
-):
-    side = 1 - info[CORE]
-    k_start, k_ready = key_copies(info, other_ref, side, k_buf, 0, sems)
-    v_start, v_ready = key_copies(info, other_ref, side, v_buf, 1, sems)
-    k_start()
-    v_start()
+def order_kernel(info, own_ref, k_buf, v_buf):
+    take_keys(info, own_ref, info[CORE], k_buf, v_buf)
+
+
+def far_kernel(info, q_ref, other_ref, k_half, v_half, o_ref, k_buf, v_buf, *scratch):
+    take_keys(info, other_ref, 1 - info[CORE], k_buf, v_buf)
     lane = lax.broadcasted_iota(jnp.int32, (PIECE, HEAD_DIM), 1)
 
     def put(n, out, mass):
@@ -221,9 +183,7 @@
                 packed = jnp.where(lane == 3 * g + i, piece[g], packed)
         o_ref[n, GROUP] = packed.astype(jnp.bfloat16)
 
-    attend_sources(
-        info, 1 - info[ZLO], q_ref, k_buf, v_buf, scratch, put, k_ready, v_ready
-    )
+    attend_sources(info, 1 - info[ZLO], q_ref, k_buf, v_buf, scratch, put)
 
 
 def near_kernel(info, q_ref, k_buf, v_buf, o_ref, m_ref, *scratch):
@@ -231,8 +191,7 @@
         o_ref[n] = out
         m_ref[n] = mass
 
-    nothing = lambda: None
-    attend_sources(info, info[ZLO], q_ref, k_buf, v_buf, scratch, put, nothing, nothing)
+    attend_sources(info, info[ZLO], q_ref, k_buf, v_buf, scratch, put)
 
 
 def merge_kernel(near_ref, mass_ref, far_ref, o_ref):
@@ -274,7 +233,6 @@
 
 SMEM = pl.BlockSpec(memory_space=pltpu.SMEM)
 VMEM = pl.BlockSpec(memory_space=pltpu.VMEM)
-ANY = pl.BlockSpec(memory_space=pl.ANY)
 HBM = pl.BlockSpec(memory_space=pltpu.HBM)
 COST = pl.CostEstimate(flops=6_000_000_000, bytes_accessed=4_000_000, transcendentals=4_000_000)
 
@@ -283,33 +241,26 @@
     return jax.ShapeDtypeStruct(sizes, kind)
 
 
-ITEMS = SOURCES * TILES + UNROLL
 SCRATCH = [
     pltpu.VMEM((ITEMS, ROWS, TILE), jnp.float32),
     pltpu.VMEM((SOURCES, ROWS, HEAD_DIM), jnp.bfloat16),
     pltpu.VMEM((SOURCES, PIECE, HEAD_DIM), jnp.int32),
     pltpu.VMEM((SOURCES, PIECE, HEAD_DIM), jnp.int32),
-    pltpu.VMEM((UNROLL, SOURCES + 1, ROWS, HEAD_DIM), jnp.float32),
+    pltpu.VMEM((SOURCES + 1, ROWS, HEAD_DIM), jnp.float32),
     pltpu.VMEM((SOURCES, ROWS, HEAD_DIM), jnp.float32),
-    pltpu.VMEM((UNROLL, SOURCES + 1, ROWS, HEAD_DIM), jnp.float32),
-    pltpu.VMEM((UNROLL, SOURCES + 1, ROWS, HEAD_DIM), jnp.float32),
-    pltpu.SMEM((ITEMS,), jnp.int32),
-    pltpu.SMEM((ITEMS,), jnp.int32),
+    pltpu.VMEM((SOURCES + 1, ROWS, HEAD_DIM), jnp.float32),
+    pltpu.VMEM((SOURCES + 1, ROWS, HEAD_DIM), jnp.float32),
 ]
 SMALL = pltpu.CompilerParams(vmem_limit_bytes=8 << 20)
 LIMIT = pltpu.CompilerParams(vmem_limit_bytes=40 << 20)
 
 
-SEMS = pltpu.SemaphoreType.DMA((2, 2 * SOURCES))
-
-
 def order_part(info, own):
     return pl.pallas_call(
         order_kernel,
         out_shape=(shape(KEYS, HEAD_DIM), shape(KEYS, HEAD_DIM)),
-        in_specs=[SMEM, ANY],
+        in_specs=[SMEM, VMEM],
         out_specs=(VMEM, VMEM),
-        scratch_shapes=[SEMS],
         compiler_params=SMALL,
         cost_estimate=pl.CostEstimate(flops=0, bytes_accessed=6_000_000, transcendentals=0),
         name="order",
@@ -324,9 +275,9 @@
             shape(KEYS, HEAD_DIM),
             shape(KEYS, HEAD_DIM),
         ),
-        in_specs=[SMEM, VMEM, ANY, VMEM, VMEM],
+        in_specs=[SMEM, VMEM, VMEM, VMEM, VMEM],
         out_specs=(VMEM, VMEM, VMEM),
-        scratch_shapes=[SEMS] + SCRATCH,
+        scratch_shapes=SCRATCH,
         input_output_aliases={3: 1, 4: 2},
         compiler_params=LIMIT,
         cost_estimate=COST,
@@ -388,6 +339,11 @@
     [((ylo * 2 + core) * 2 + yhi) * 4 + x for ylo in range(2) for yhi in range(2) for x in range(4)]
     for core in range(2)
 ]
+
+
+def look(values, at):
+    index = jnp.arange(values.shape[0], dtype=jnp.int32)
+    return jnp.sum(jnp.where(at[:, None] == index[None, :], values[None, :], 0), axis=1)
 
 
 def table(visit_ids, span_order):
@@ -406,7 +362,23 @@
     )
     at = lax.axis_index("plane")
     place = jnp.stack([at // 16, at // 8 % 2, zlo, at % 8 * PIECE]).astype(jnp.int32)
-    return jnp.concatenate([span_order, count, ordered, starts, place])
+    lists, totals = [], []
+    for side in (zlo, 1 - zlo):
+        source = (jnp.arange(SOURCES, dtype=jnp.int32) * 2 + side) * 4 + place[0] * 2 + place[1]
+        span = look(span_order, source)
+        p0 = span * SPAN_ROWS + place[3]
+        low = jnp.max(jnp.where(starts[None, :] <= p0[:, None], starts[None, :], 0), axis=1)
+        tile_a = look(count, low // SPAN_ROWS) // PER_TILE
+        tile_b = (look(count, span + 1) + PER_TILE - 1) // PER_TILE
+        size = jnp.maximum(tile_b - tile_a, 0)
+        order = jnp.arange(SOURCES)
+        ends = jnp.sum(jnp.where(order[None, :] <= order[:, None], size[None, :], 0), axis=1)
+        at = jnp.arange(ITEMS, dtype=jnp.int32)
+        slot = jnp.sum((ends[None, :] <= at[:, None]).astype(jnp.int32), axis=1)
+        tile = at + look(tile_a - ends + size, slot)
+        lists.append(slot * 16 + jnp.where(slot < SOURCES, tile, 0))
+        totals.append(jnp.sum(size)[None])
+    return jnp.concatenate([span_order, count, ordered, starts, place] + totals + lists)
 
 
 def body(queries, key_rows, value_rows, visit_ids, span_order):

time: 121 us -> 124 us (1.025)
  blocking collectives: 78.2 us -> 23.6 us
  waiting for transfers between devices: 5.9 us -> 40.5 us
  starting transfers between devices: 19.4 us -> 39.2 us
  other arithmetic: 0.44 us -> 3.78 us
  Pallas kernels: 15.3 us -> 13.2 us
    all_to_all x2 -> x0, blocking collectives: 56 us -> none  [the longest x1 33.2 us: body(): packed = lax.all_to_all(packed, 'zhi', 0, 0, tiled=True)]
    all_to_all x0 -> x2, waiting for transfers between devices: none -> 33.8 us  [the longest x1 18 us: body(): lax.all_to_all(spread, 'plane', 0, 0, axis_index_groups=PLANE, tiled=True)]
    all_to_all x0 -> x2, starting transfers between devices: none -> 22.5 us  [the longest x1 15.6 us: body(): packed = lax.all_to_all(packed, 'zhi', 0, 0, tiled=True)]
    reduce_sum x0 -> x9, other arithmetic: none -> 2.38 us  [the longest x4 1.26 us: look(): jnp.sum(jnp.where(at[:, None] == index[None, :], values[None, :], 0), axi...]
    ppermute x1, starting transfers between devices: 9.71 us -> 8.12 us  [body(): other = lax.ppermute(own, 'plane', [(i, i ^ 8) for i in range(32)])]
    pallas_call x1, Pallas kernels: 5.84 us -> 4.25 us  [far_part(): pl.pallas_call(far_kernel, out_shape=(shape(SOURCES, GROUP + 1, PIECE, HE...]
    all_to_all x1, blocking collectives: 22.2 us -> 23.6 us  [body(): out = lax.all_to_all(out, 'zhi', 0, 0, tiled=True)]
  transfers between devices with their start and end apart: 3 -> 5, of which waited for: 2 -> 4; matrix products, arithmetic and copies ran while one was open for 0% -> 4% of each run, Pallas kernels for 6% -> 4%
where the time goes in v4:
time: 124 us; the launch traced here: 122 us
  waiting for transfers between devices  40.5 us (33%)
  starting transfers between devices  39.2 us (32%)
  blocking collectives  23.6 us (19%)
  Pallas kernels  13.2 us (11%)
  other arithmetic  3.78 us (3%)
  local copies, waits for them, and re-layouts  2.03 us (2%)
    all_to_all x1, blocking collectives, body(): out = lax.all_to_all(out, 'zhi', 0, 0, tiled=True)  23.6 us
    all_to_all x1, waiting for transfers between devices, body(): lax.all_to_all(spread, 'plane', 0, 0, axis_index_groups=PLANE, tiled=True)  18 us
    all_to_all x1, waiting for transfers between devices, body(): packed = lax.all_to_all(packed, 'zhi', 0, 0, tiled=True)  15.8 us
    all_to_all x1, starting transfers between devices, body(): packed = lax.all_to_all(packed, 'zhi', 0, 0, tiled=True)  15.6 us
    ppermute x1, starting transfers between devices, body(): other = lax.ppermute(own, 'plane', [(i, i ^ 8) for i in range(32)])  8.12 us
    all_to_all x1, starting transfers between devices, body(): lax.all_to_all(spread, 'plane', 0, 0, axis_index_groups=PLANE, tiled=True)  6.89 us
    ppermute x1, starting transfers between devices, body(): sent = lax.ppermute(far_out, 'zlo', SWAP)  5.44 us
    ppermute x1, waiting for transfers between devices, body(): far_q = lax.ppermute(packed, 'zlo', SWAP)  5.02 us
  transfers between devices with their start and end apart: 5, of which 4 were waited for; matrix products, arithmetic and copies ran while one was open for 4% of the time, Pallas kernels for 4%

profile of v4, /device:TPU:1, one launch (start us, length us, event | category | flops | bytes accessed | tf_op | source)
XLA Modules:
  0.0 122.5 jit_solution(7478135887882685046)
XLA Ops:
  0.0 2.1 %pack.1 = bf16[8,6,24,128]{3,2,1,0:T(8,128)(2,1)} custom-call(bf16[24,4096]{1,0:T(8,128)(2,1)} %q_ref.1, bf16[24,1024]{1,0:T(8,128)(2,1)} %k_ref.1, bf16[24,1024]{1,0:T(8,128)(2,1)} %v_ref.1), custom_call_target="tpu_custom_call" | custom-call | tf_op jit(solution)/shard_map/pack/pallas_call | solution.py:316
  2.1 15.6 %all-to-all-start = ((bf16[8,6,24,128]{3,2,1,0:T(8,128)(2,1)}), bf16[8,6,24,128]{3,2,1,0:T(8,128)(2,1)S(1)}, u32[]{:S(2)}, u32[]{:S(2)}) async-start(bf16[8,6,24,128]{3,2,1,0:T(8,128)(2,1)} %pack.1), calls=%async_computation | async-start | bytes 589824 | tf_op jit(solution)/shard_map/all_to_all | solution.py:387
  17.8 0.9 select_reduce_fusion.6
  18.7 1.0 convert_reduce_fusion
  19.7 15.8 %all-to-all-done.packed_ref.q_ref = bf16[8,6,24,128]{3,2,1,0:T(8,128)(2,1)S(1)} async-done(((bf16[8,6,24,128]{3,2,1,0:T(8,128)(2,1)}), bf16[8,6,24,128]{3,2,1,0:T(8,128)(2,1)S(1)}, u32[]{:S(2)}, u32[]{:S(2)}) %all-to-all-start) | async-done | bytes 294944 | tf_op jit(solution)/shard_map/all_to_all | solution.py:387
  35.5 1.4 %fan.1 = bf16[16,8,2,24,128]{4,3,2,1,0:T(8,128)(2,1)} custom-call(bf16[8,6,24,128]{3,2,1,0:T(8,128)(2,1)S(1)} %all-to-all-done.packed_ref.q_ref), custom_call_target="tpu_custom_call" | custom-call | tf_op jit(solution)/shard_map/fan/pallas_call | solution.py:327
  36.9 0.0 copy-start
  36.9 6.9 %all-to-all-start.1 = ((bf16[16,8,2,24,128]{4,3,2,1,0:T(8,128)(2,1)}), bf16[16,8,2,24,128]{4,3,2,1,0:T(8,128)(2,1)S(1)}, u32[]{:S(2)}, u32[]{:S(2)}) async-start(bf16[16,8,2,24,128]{4,3,2,1,0:T(8,128)(2,1)} %fan.1), calls=%async_computation.1 | async-start | bytes 3145728 | tf_op jit(solution)/shard_map/all_to_all | solution.py:390
  43.8 0.0 copy-done
  43.8 0.1 convert_reduce_fusion.1
  43.9 0.1 slice.3
  44.0 0.1 select_reduce_fusion.10
  44.1 0.2 select_reduce_fusion.5
  44.3 0.7 fusion.5
  45.0 0.1 select_reduce_fusion.1
  45.2 18.0 %all-to-all-done.1.own_ref = bf16[16,8,2,24,128]{4,3,2,1,0:T(8,128)(2,1)S(1)} async-done(((bf16[16,8,2,24,128]{4,3,2,1,0:T(8,128)(2,1)}), bf16[16,8,2,24,128]{4,3,2,1,0:T(8,128)(2,1)S(1)}, u32[]{:S(2)}, u32[]{:S(2)}) %all-to-all-start.1) | async-done | bytes 1572896 | tf_op jit(solution)/shard_map/all_to_all | solution.py:390
  63.1 8.1 %collective-permute-start.1 = (bf16[16,8,2,24,128]{4,3,2,1,0:T(8,128)(2,1)S(1)}, bf16[16,8,2,24,128]{4,3,2,1,0:T(8,128)(2,1)S(1)}, u32[]{:S(2)}, u32[]{:S(2)}) collective-permute-start(bf16[16,8,2,24,128]{4,3,2,1,0:T(8,128)(2,1)S(1)} %all-to-all-done.1.own_ref), channel_id=1, source_target_pairs={{0,8},{1,9},{2,10},{3,11},{4,12},{5,13},{6,14},{7,15},{8,0},{9,1},... | collective-permute-start | bytes 4718600 | tf_op jit(solution)/shard_map/ppermute | solution.py:393
  71.2 0.1 select_reduce_fusion.3
  71.3 0.1 convert_reduce_fusion.3
  71.4 0.1 convert_reduce_fusion.4
  71.5 0.1 select_reduce_fusion
  71.6 0.1 select_reduce_fusion.2
  71.7 3.2 %collective-permute-start = (bf16[8,6,24,128]{3,2,1,0:T(8,128)(2,1)S(1)}, bf16[8,6,24,128]{3,2,1,0:T(8,128)(2,1)}, u32[]{:S(2)}, u32[]{:S(2)}) collective-permute-start(bf16[8,6,24,128]{3,2,1,0:T(8,128)(2,1)S(1)} %all-to-all-done.packed_ref.q_ref), channel_id=1, source_target_pairs={{0,32},{32,0},{1,33},{33,1},{2,34},{34,2},{3,35},{35,3},{4,36},{36... | collective-permute-start | bytes 884744 | tf_op jit(solution)/shard_map/ppermute | solution.py:388
  74.9 0.1 convert_reduce_fusion.2
  75.0 1.3 %concatenate.3.info = s32[307]{0:T(512)S(1)} concatenate(s32[64]{0:T(128)S(1)} %copy-done, s32[65]{0:T(128)S(1)} %convert_reduce_fusion.1, s32[32]{0:T(128)S(1)} %convert_reduce_fusion.2, s32[4]{0:T(128)S(1)} %convert_reduce_fusion, s32[1]{0:T(128)} %bitcast, s32[1]{0:T(128)} %bitcast.1, s32[1]{0:T(128)} %bitcast.2, s32[1]{0:T(128)} %bitcast.3, s32[1]{0:T(128)} %bitcast.4, ...), dimensions={0} | concatenate | bytes 2456 | tf_op jit(solution)/shard_map/concatenate | solution.py:381
  76.3 1.0 order.1
  77.2 5.0 %collective-permute-done.q_ref = bf16[8,6,24,128]{3,2,1,0:T(8,128)(2,1)} collective-permute-done((bf16[8,6,24,128]{3,2,1,0:T(8,128)(2,1)S(1)}, bf16[8,6,24,128]{3,2,1,0:T(8,128)(2,1)}, u32[]{:S(2)}, u32[]{:S(2)}) %collective-permute-start) | collective-permute-done | bytes 294944 | tf_op jit(solution)/shard_map/ppermute | solution.py:388
  82.3 0.0 collective-permute-done.1.other_ref
  82.3 4.3 %far.1 = (bf16[8,5,24,128]{3,2,1,0:T(8,128)(2,1)S(1)}, bf16[6144,128]{1,0:T(8,128)(2,1)S(1)}, bf16[6144,128]{1,0:T(8,128)(2,1)S(1)}) custom-call(s32[307]{0:T(512)S(1)} %concatenate.3.info, bf16[8,6,24,128]{3,2,1,0:T(8,128)(2,1)} %collective-permute-done.q_ref, ...), custom_call_target="tpu_custom_call", output_to_operand_aliasing={{1}: (3, {}), {2}: (4, {})} | custom-call | flops 6000000000 | bytes 4000000 | tf_op jit(solution)/shard_map/far/pallas_call | solution.py:271
  86.5 5.4 %collective-permute-start.2 = (bf16[8,5,24,128]{3,2,1,0:T(8,128)(2,1)S(1)}, bf16[8,5,24,128]{3,2,1,0:T(8,128)(2,1)S(1)}, u32[]{:S(2)}, u32[]{:S(2)}) collective-permute-start(bf16[8,5,24,128]{3,2,1,0:T(8,128)(2,1)S(1)} %get-tuple-element.18), channel_id=1, source_target_pairs={{0,32},{32,0},{1,33},{33,1},{2,34},{34,2},{3,35},{35,3},{4,36},{36... | collective-permute-start | bytes 737288 | tf_op jit(solution)/shard_map/ppermute | solution.py:397
  92.0 4.1 %near.1 = (f32[8,4,24,128]{3,2,1,0:T(8,128)S(1)}, f32[8,4,24,128]{3,2,1,0:T(8,128)S(1)}) custom-call(s32[307]{0:T(512)S(1)} %concatenate.3.info, bf16[8,6,24,128]{3,2,1,0:T(8,128)(2,1)S(1)} %all-to-all-done.packed_ref.q_ref, bf16[6144,128]{1,0:T(8,128)(2,1)S(1)} %get-tuple-element.14.k_buf, bf16[6144,128]{1,0:T(8,128)(2,1)S(1)} %get-tuple-element.15.v_buf), custom_call_target="tpu_custom_call" | custom-call | flops 6000000000 | bytes 4000000 | tf_op jit(solution)/shard_map/near/pallas_call | solution.py:289
  96.0 1.7 %collective-permute-done.2.far_ref = bf16[8,5,24,128]{3,2,1,0:T(8,128)(2,1)S(1)} collective-permute-done((bf16[8,5,24,128]{3,2,1,0:T(8,128)(2,1)S(1)}, bf16[8,5,24,128]{3,2,1,0:T(8,128)(2,1)S(1)}, u32[]{:S(2)}, u32[]{:S(2)}) %collective-permute-start.2) | collective-permute-done | bytes 245792 | tf_op jit(solution)/shard_map/ppermute | solution.py:397
  97.7 0.5 merge.1
  98.2 23.6 %all_to_all.15 = bf16[8,24,512]{2,1,0:T(8,128)(2,1)S(1)} all-to-all(bf16[8,24,512]{2,1,0:T(8,128)(2,1)S(1)} %merge.1), channel_id=1, replica_groups=mesh['zhi'=8,'zlo'=2,'plane'=32] {'zhi'}, dimensions={0} | all-to-all | bytes 393216 | tf_op jit(solution)/shard_map/all_to_all | solution.py:400
  121.8 0.7 copy.10
  (11 shorter events, 0.1 us)
Async XLA Ops:
  2.1 33.4 %all-to-all-start = ((bf16[8,6,24,128]{3,2,1,0:T(8,128)(2,1)}), bf16[8,6,24,128]{3,2,1,0:T(8,128)(2,1)S(1)}, u32[]{:S(2)}, u32[]{:S(2)}) async-start(bf16[8,6,24,128]{3,2,1,0:T(8,128)(2,1)} %pack.1), calls=%async_computation | async-start | bytes 589824 | tf_op jit(solution)/shard_map/all_to_all | solution.py:387
  36.9 6.9 %copy-start = (s32[64]{0:T(128)S(1)}, s32[64]{0:T(128)}, u32[]{:S(2)}) copy-start(s32[64]{0:T(128)} %param.9) | copy-start | bytes 772
  36.9 26.2 %all-to-all-start.1 = ((bf16[16,8,2,24,128]{4,3,2,1,0:T(8,128)(2,1)}), bf16[16,8,2,24,128]{4,3,2,1,0:T(8,128)(2,1)S(1)}, u32[]{:S(2)}, u32[]{:S(2)}) async-start(bf16[16,8,2,24,128]{4,3,2,1,0:T(8,128)(2,1)} %fan.1), calls=%async_computation.1 | async-start | bytes 3145728 | tf_op jit(solution)/shard_map/all_to_all | solution.py:390
  63.1 19.2 %collective-permute-start.1 = (bf16[16,8,2,24,128]{4,3,2,1,0:T(8,128)(2,1)S(1)}, bf16[16,8,2,24,128]{4,3,2,1,0:T(8,128)(2,1)S(1)}, u32[]{:S(2)}, u32[]{:S(2)}) collective-permute-start(bf16[16,8,2,24,128]{4,3,2,1,0:T(8,128)(2,1)S(1)} %all-to-all-done.1.own_ref), channel_id=1, source_target_pairs={{0,8},{1,9},{2,10},{3,11},{4,12},{5,13},{6,14},{7,15},{8,0},{9,1},... | collective-permute-start | bytes 4718600 | tf_op jit(solution)/shard_map/ppermute | solution.py:393
  71.7 10.5 %collective-permute-start = (bf16[8,6,24,128]{3,2,1,0:T(8,128)(2,1)S(1)}, bf16[8,6,24,128]{3,2,1,0:T(8,128)(2,1)}, u32[]{:S(2)}, u32[]{:S(2)}) collective-permute-start(bf16[8,6,24,128]{3,2,1,0:T(8,128)(2,1)S(1)} %all-to-all-done.packed_ref.q_ref), channel_id=1, source_target_pairs={{0,32},{32,0},{1,33},{33,1},{2,34},{34,2},{3,35},{35,3},{4,36},{36... | collective-permute-start | bytes 884744 | tf_op jit(solution)/shard_map/ppermute | solution.py:388
  86.5 11.2 %collective-permute-start.2 = (bf16[8,5,24,128]{3,2,1,0:T(8,128)(2,1)S(1)}, bf16[8,5,24,128]{3,2,1,0:T(8,128)(2,1)S(1)}, u32[]{:S(2)}, u32[]{:S(2)}) collective-permute-start(bf16[8,5,24,128]{3,2,1,0:T(8,128)(2,1)S(1)} %get-tuple-element.18), channel_id=1, source_target_pairs={{0,32},{32,0},{1,33},{33,1},{2,34},{34,2},{3,35},{35,3},{4,36},{36... | collective-permute-start | bytes 737288 | tf_op jit(solution)/shard_map/ppermute | solution.py:397

commit v5 on v4

--- a/solution.py
+++ b/solution.py
@@ -17,7 +17,7 @@
 HALF = SPANS // 2
 KEYS = HALF * SPAN_ROWS
 PER_TILE = 4
-UNROLL = 4
+UNROLL = 3
 TILE = PER_TILE * SPAN_ROWS
 TILES = KEYS // TILE
 SOURCES = 8
@@ -35,7 +35,7 @@
 FIRST = YLO + 3
 TOTAL = YLO + 4
 LIST = TOTAL + 2
-ITEMS = SOURCES * TILES + UNROLL
+ITEMS = SOURCES // 2 * TILES + UNROLL
 
 
 def take_keys(info, src, side, k_buf, v_buf):
@@ -72,7 +72,7 @@
         pos_buf[n] = pos
         low_buf[n] = start_of(pos)
         q_buf[n] = (
-            q_ref[n, 2:].astype(jnp.float32).reshape(ROWS, HEAD_DIM).astype(jnp.bfloat16)
+            q_ref[n].astype(jnp.float32).reshape(ROWS, HEAD_DIM).astype(jnp.bfloat16)
         )
         best[n] = jnp.full((ROWS, HEAD_DIM), -jnp.inf, jnp.float32)
         total[n] = jnp.zeros((ROWS, HEAD_DIM), jnp.float32)
@@ -83,25 +83,23 @@
 
     def item(at):
         entry = info[listed + at]
-        return entry // 16, entry % 16
+        return (entry // 256, entry // 16 % 16), entry % 16
 
     def scores(i, carry):
         for u in range(UNROLL):
             at = i * UNROLL + u
-            slot, j = item(at)
-            n = jnp.minimum(slot, SOURCES - 1)
-            s = lax.dot_general(
-                q_buf[n],
+            slots, j = item(at)
+            sources = [jnp.minimum(slot, SOURCES - 1) for slot in slots]
+            both = lax.dot_general(
+                jnp.concatenate([q_buf[n] for n in sources], axis=0),
                 k_buf[pl.ds(pl.multiple_of(j * TILE, TILE), TILE), :],
                 (((1,), (1,)), ((), ())),
                 preferred_element_type=jnp.float32,
             )
-            s = s.reshape(GROUP, PIECE, TILE)
-            low, pos = low_buf[n], pos_buf[n]
             base = [
                 (info[SORTED + j * PER_TILE + w] - w) * SPAN_ROWS for w in range(PER_TILE)
             ]
-            high = best[slot].reshape(GROUP, PIECE, HEAD_DIM)
+            keys = []
             for c in range(TILE // HEAD_DIM):
                 left = c * HEAD_DIM // SPAN_ROWS
                 right = (c * HEAD_DIM + HEAD_DIM - 1) // SPAN_ROWS
@@ -110,13 +108,23 @@
                     key = key + base[left]
                 else:
                     key = key + jnp.where(key < right * SPAN_ROWS, base[left], base[right])
-                keep = (key >= low) & (key <= pos)
-                part = jnp.where(
-                    keep[None], s[:, :, c * HEAD_DIM : (c + 1) * HEAD_DIM], -jnp.inf
-                )
-                s_buf[at, :, c * HEAD_DIM : (c + 1) * HEAD_DIM] = part.reshape(ROWS, HEAD_DIM)
-                high = jnp.maximum(high, part)
-            best[slot] = high.reshape(ROWS, HEAD_DIM)
+                keys.append(key)
+            for e in range(2):
+                s = both[e * ROWS : (e + 1) * ROWS].reshape(GROUP, PIECE, TILE)
+                low, pos = low_buf[sources[e]], pos_buf[sources[e]]
+                high = best[slots[e]].reshape(GROUP, PIECE, HEAD_DIM)
+                for c, key in enumerate(keys):
+                    keep = (key >= low) & (key <= pos)
+                    part = jnp.where(
+                        keep[None], s[:, :, c * HEAD_DIM : (c + 1) * HEAD_DIM], -jnp.inf
+                    )
+                    s_buf[
+                        at,
+                        e * ROWS : (e + 1) * ROWS,
+                        c * HEAD_DIM : (c + 1) * HEAD_DIM,
+                    ] = part.reshape(ROWS, HEAD_DIM)
+                    high = jnp.maximum(high, part)
+                best[slots[e]] = high.reshape(ROWS, HEAD_DIM)
         return carry
 
     lax.fori_loop(0, steps, scores, 0)
@@ -128,24 +136,31 @@
     def mix(i, carry):
         for u in range(UNROLL):
             at = i * UNROLL + u
-            slot, j = item(at)
-            n = jnp.minimum(slot, SOURCES - 1)
-            top = top_buf[n]
-            top = jnp.where(top > -jnp.inf, top, 0.0)
-            part_sum = total[slot]
-            parts = []
-            for c in range(TILE // HEAD_DIM):
-                w = jnp.exp2(
-                    (s_buf[at, :, c * HEAD_DIM : (c + 1) * HEAD_DIM] - top) * SCALE_LOG2
-                )
-                part_sum = part_sum + w
-                parts.append(w.astype(jnp.bfloat16))
-            total[slot] = part_sum
-            acc[slot] = acc[slot] + jnp.dot(
-                jnp.concatenate(parts, axis=1),
+            slots, j = item(at)
+            rows = []
+            for e in range(2):
+                top = top_buf[jnp.minimum(slots[e], SOURCES - 1)]
+                top = jnp.where(top > -jnp.inf, top, 0.0)
+                part_sum = total[slots[e]]
+                parts = []
+                for c in range(TILE // HEAD_DIM):
+                    part = s_buf[
+                        at,
+                        e * ROWS : (e + 1) * ROWS,
+                        c * HEAD_DIM : (c + 1) * HEAD_DIM,
+                    ]
+                    w = jnp.exp2((part - top) * SCALE_LOG2)
+                    part_sum = part_sum + w
+                    parts.append(w.astype(jnp.bfloat16))
+                total[slots[e]] = part_sum
+                rows.append(jnp.concatenate(parts, axis=1))
+            mixed = jnp.dot(
+                jnp.concatenate(rows, axis=0),
                 v_buf[pl.ds(pl.multiple_of(j * TILE, TILE), TILE), :],
                 preferred_element_type=jnp.float32,
             )
+            for e in range(2):
+                acc[slots[e]] = acc[slots[e]] + mixed[e * ROWS : (e + 1) * ROWS]
         return carry
 
     lax.fori_loop(0, steps, mix, 0)
@@ -210,30 +225,23 @@
             o_ref[n, :, g * HEAD_DIM : (g + 1) * HEAD_DIM] = out.astype(jnp.bfloat16)
 
 
-def pack_kernel(q_ref, k_ref, v_ref, o_ref, sems):
-    copies = []
+def pack_kernel(q_ref, k_ref, v_ref, o_ref):
     for h in range(KV_HEADS):
-        for i in range(GROUP + 2):
-            src, c = ((k_ref, h), (v_ref, h))[i] if i < 2 else (q_ref, h * GROUP + i - 2)
-            copies.append(
-                pltpu.make_async_copy(
-                    src.at[:, c * HEAD_DIM : (c + 1) * HEAD_DIM], o_ref.at[h, i], sems.at[h, i]
-                )
-            )
-    for c in copies:
-        c.start()
-    for c in copies:
-        c.wait()
-
-
-def fan_kernel(packed_ref, o_ref):
+        o_ref[h, 0] = k_ref[:, h * HEAD_DIM : (h + 1) * HEAD_DIM]
+        o_ref[h, 1] = v_ref[:, h * HEAD_DIM : (h + 1) * HEAD_DIM]
+        for g in range(GROUP):
+            c = (h * GROUP + g) * HEAD_DIM
+            o_ref[h, 2 + g] = q_ref[:, c : c + HEAD_DIM]
+
+
+def fan_kernel(packed_ref, o_ref, q_ref):
     for i in range(16):
         o_ref[i] = packed_ref[:, :2]
+    q_ref[...] = packed_ref[:, 2:]
 
 
 SMEM = pl.BlockSpec(memory_space=pltpu.SMEM)
 VMEM = pl.BlockSpec(memory_space=pltpu.VMEM)
-HBM = pl.BlockSpec(memory_space=pltpu.HBM)
 COST = pl.CostEstimate(flops=6_000_000_000, bytes_accessed=4_000_000, transcendentals=4_000_000)
 
 
@@ -242,7 +250,7 @@
 
 
 SCRATCH = [
-    pltpu.VMEM((ITEMS, ROWS, TILE), jnp.float32),
+    pltpu.VMEM((ITEMS, 2 * ROWS, TILE), jnp.float32),
     pltpu.VMEM((SOURCES, ROWS, HEAD_DIM), jnp.bfloat16),
     pltpu.VMEM((SOURCES, PIECE, HEAD_DIM), jnp.int32),
     pltpu.VMEM((SOURCES, PIECE, HEAD_DIM), jnp.int32),
@@ -316,9 +324,8 @@
     return pl.pallas_call(
         pack_kernel,
         out_shape=shape(KV_HEADS, GROUP + 2, PIECE, HEAD_DIM),
-        in_specs=[HBM, HBM, HBM],
+        in_specs=[VMEM, VMEM, VMEM],
         out_specs=VMEM,
-        scratch_shapes=[pltpu.SemaphoreType.DMA((KV_HEADS, GROUP + 2))],
         name="pack",
     )(q, k, v)
 
@@ -326,9 +333,12 @@
 def fan(packed):
     return pl.pallas_call(
         fan_kernel,
-        out_shape=shape(16, SOURCES, 2, PIECE, HEAD_DIM),
+        out_shape=(
+            shape(16, SOURCES, 2, PIECE, HEAD_DIM),
+            shape(SOURCES, GROUP, PIECE, HEAD_DIM),
+        ),
         in_specs=[VMEM],
-        out_specs=VMEM,
+        out_specs=(VMEM, VMEM),
         compiler_params=SMALL,
         name="fan",
     )(packed)
@@ -362,40 +372,54 @@
     )
     at = lax.axis_index("plane")
     place = jnp.stack([at // 16, at // 8 % 2, zlo, at % 8 * PIECE]).astype(jnp.int32)
-    lists, totals = [], []
-    for side in (zlo, 1 - zlo):
-        source = (jnp.arange(SOURCES, dtype=jnp.int32) * 2 + side) * 4 + place[0] * 2 + place[1]
-        span = look(span_order, source)
-        p0 = span * SPAN_ROWS + place[3]
-        low = jnp.max(jnp.where(starts[None, :] <= p0[:, None], starts[None, :], 0), axis=1)
-        tile_a = look(count, low // SPAN_ROWS) // PER_TILE
-        tile_b = (look(count, span + 1) + PER_TILE - 1) // PER_TILE
-        size = jnp.maximum(tile_b - tile_a, 0)
-        order = jnp.arange(SOURCES)
-        ends = jnp.sum(jnp.where(order[None, :] <= order[:, None], size[None, :], 0), axis=1)
-        at = jnp.arange(ITEMS, dtype=jnp.int32)
-        slot = jnp.sum((ends[None, :] <= at[:, None]).astype(jnp.int32), axis=1)
-        tile = at + look(tile_a - ends + size, slot)
-        lists.append(slot * 16 + jnp.where(slot < SOURCES, tile, 0))
-        totals.append(jnp.sum(size)[None])
-    return jnp.concatenate([span_order, count, ordered, starts, place] + totals + lists)
+    side = jnp.stack([zlo, 1 - zlo])[:, None]
+    source = (jnp.arange(SOURCES, dtype=jnp.int32)[None] * 2 + side) * 4
+    span = look(span_order, source.reshape(-1) + place[0] * 2 + place[1])
+    p0 = span * SPAN_ROWS + place[3]
+    low = jnp.max(jnp.where(starts[None, :] <= p0[:, None], starts[None, :], 0), axis=1)
+    tile_a = look(count, low // SPAN_ROWS) // PER_TILE
+    tile_b = (look(count, span + 1) + PER_TILE - 1) // PER_TILE
+    tiles = jnp.arange(TILES, dtype=jnp.int32)
+    active = (tile_a[:, None] <= tiles) & (tiles < tile_b[:, None])
+    active = active.reshape(2, SOURCES, TILES).astype(jnp.int32)
+    n = jnp.arange(SOURCES, dtype=jnp.int32)
+    before = (n[None, :] < n[:, None]).astype(jnp.int32)
+    rank = jnp.sum(before[None, :, :, None] * active[:, None], axis=2)
+    pairs = (jnp.sum(active, axis=1) + 1) // 2
+    earlier = (tiles[None, :] < tiles[:, None]).astype(jnp.int32)
+    offset = jnp.sum(earlier[None] * pairs[:, None, :], axis=2)
+    at = jnp.arange(ITEMS, dtype=jnp.int32)
+    where = jnp.where(active == 1, offset[:, None, :] * 2 + rank, -1)
+    where = where.reshape(2, 1, SOURCES * TILES)
+    owner = jnp.repeat(n, TILES)[None, None] - SOURCES
+
+    def owners(half):
+        hit = where == (at * 2 + half)[None, :, None]
+        return SOURCES + jnp.sum(jnp.where(hit, owner, 0), axis=2)
+
+    done = (offset + pairs)[:, None, :] <= at[None, :, None]
+    tile = jnp.minimum(jnp.sum(done.astype(jnp.int32), axis=2), TILES - 1)
+    listed = owners(0) * 256 + owners(1) * 16 + tile
+    return jnp.concatenate(
+        [span_order, count, ordered, starts, place, jnp.sum(pairs, axis=1), listed.reshape(-1)]
+    )
 
 
 def body(queries, key_rows, value_rows, visit_ids, span_order):
     info = table(visit_ids, span_order)
     packed = pack(queries, key_rows, value_rows)
     packed = lax.all_to_all(packed, "zhi", 0, 0, tiled=True)
-    far_q = lax.ppermute(packed, "zlo", SWAP)
-    spread = fan(packed)
+    spread, near_q = fan(packed)
     own = lax.all_to_all(
         spread, "plane", 0, 0, axis_index_groups=PLANE, tiled=True
     )
+    far_q = lax.ppermute(near_q, "zlo", SWAP)
     other = lax.ppermute(own, "plane", [(i, i ^ 8) for i in range(32)])
     k, v = order_part(info, own)
 
     far_out, k, v = far_part(info, far_q, other, k, v)
     sent = lax.ppermute(far_out, "zlo", SWAP)
-    near_out, mass = near_part(info, packed, k, v)
+    near_out, mass = near_part(info, near_q, k, v)
     out = merge(near_out, mass, sent)
     out = lax.all_to_all(out, "zhi", 0, 0, tiled=True)
     return jnp.transpose(out, (1, 0, 2)).reshape(PIECE, HEADS * HEAD_DIM)

time: 124 us -> 122 us (0.984)
  the two profiles are of different devices: /device:TPU:1 before, /device:TPU:8 now
where the time goes in v5:
time: 122 us; the launch traced here: 121 us
  waiting for transfers between devices  40.3 us (33%)
  starting transfers between devices  30.7 us (25%)
  blocking collectives  26 us (21%)
  Pallas kernels  14.6 us (12%)
  other arithmetic  6.09 us (5%)
  local copies, waits for them, and re-layouts  3.24 us (3%)
    all_to_all x1, blocking collectives, body(): out = lax.all_to_all(out, 'zhi', 0, 0, tiled=True)  26 us
    all_to_all x1, waiting for transfers between devices, body(): packed = lax.all_to_all(packed, 'zhi', 0, 0, tiled=True)  19.6 us
    all_to_all x1, waiting for transfers between devices, body(): lax.all_to_all(spread, 'plane', 0, 0, axis_index_groups=PLANE, tiled=True)  16.9 us
    all_to_all x1, starting transfers between devices, body(): packed = lax.all_to_all(packed, 'zhi', 0, 0, tiled=True)  15.1 us
    all_to_all x1, starting transfers between devices, body(): lax.all_to_all(spread, 'plane', 0, 0, axis_index_groups=PLANE, tiled=True)  7.53 us
    pallas_call x1, Pallas kernels, far_part(): pl.pallas_call(far_kernel, out_shape=(shape(SOURCES, GROUP + 1, PIECE, HE...  5.33 us
    pallas_call x1, Pallas kernels, near_part(): pl.pallas_call(near_kernel, out_shape=(shape(SOURCES, GROUP, PIECE, HEAD_...  4.78 us
    ppermute x1, starting transfers between devices, body(): far_q = lax.ppermute(near_q, 'zlo', SWAP)  3.57 us
  transfers between devices with their start and end apart: 5, of which 4 were waited for; matrix products, arithmetic and copies ran while one was open for 7% of the time, Pallas kernels for 5%

profile of v5, /device:TPU:8, one launch (start us, length us, event | category | flops | bytes accessed | tf_op | source)
XLA Modules:
  0.0 121.1 jit_solution(15177110679084622282)
XLA Ops:
  0.0 1.7 %pack.1 = bf16[8,6,24,128]{3,2,1,0:T(8,128)(2,1)} custom-call(bf16[24,4096]{1,0:T(8,128)(2,1)} %q_ref.1, bf16[24,1024]{1,0:T(8,128)(2,1)} %k_ref.1, bf16[24,1024]{1,0:T(8,128)(2,1)} %v_ref.1), custom_call_target="tpu_custom_call" | custom-call | tf_op jit(solution)/shard_map/pack/pallas_call | solution.py:324
  1.7 15.1 %all-to-all-start = ((bf16[8,6,24,128]{3,2,1,0:T(8,128)(2,1)}), bf16[8,6,24,128]{3,2,1,0:T(8,128)(2,1)S(1)}, u32[]{:S(2)}, u32[]{:S(2)}) async-start(bf16[8,6,24,128]{3,2,1,0:T(8,128)(2,1)} %pack.1), calls=%async_computation | async-start | bytes 589824 | tf_op jit(solution)/shard_map/all_to_all | solution.py:411
  16.8 0.1 pad_add_fusion
  16.9 0.1 add_add_fusion
  17.0 0.1 add.198
  17.1 0.8 select_reduce_fusion.2
  17.9 1.0 convert_reduce_fusion
  18.9 0.1 select_reduce_fusion.3
  19.0 19.6 %all-to-all-done.packed_ref = bf16[8,6,24,128]{3,2,1,0:T(8,128)(2,1)S(1)} async-done(((bf16[8,6,24,128]{3,2,1,0:T(8,128)(2,1)}), bf16[8,6,24,128]{3,2,1,0:T(8,128)(2,1)S(1)}, u32[]{:S(2)}, u32[]{:S(2)}) %all-to-all-start) | async-done | bytes 294944 | tf_op jit(solution)/shard_map/all_to_all | solution.py:411
  38.6 1.4 %fan.1 = (bf16[16,8,2,24,128]{4,3,2,1,0:T(8,128)(2,1)}, bf16[8,4,24,128]{3,2,1,0:T(8,128)(2,1)S(1)}) custom-call(bf16[8,6,24,128]{3,2,1,0:T(8,128)(2,1)S(1)} %all-to-all-done.packed_ref), custom_call_target="tpu_custom_call" | custom-call | tf_op jit(solution)/shard_map/fan/pallas_call | solution.py:334
  40.0 7.5 %all-to-all-start.1 = ((bf16[16,8,2,24,128]{4,3,2,1,0:T(8,128)(2,1)}), bf16[16,8,2,24,128]{4,3,2,1,0:T(8,128)(2,1)S(1)}, u32[]{:S(2)}, u32[]{:S(2)}) async-start(bf16[16,8,2,24,128]{4,3,2,1,0:T(8,128)(2,1)} %get-tuple-element.15), calls=%async_computation.1 | async-start | bytes 3145728 | tf_op jit(solution)/shard_map/all_to_all | solution.py:413
  47.5 0.1 convert_reduce_fusion.1
  47.6 0.2 select_reduce_fusion.1
  47.8 0.1 reduce_sum.124
  47.9 0.1 sub.52
  48.0 0.1 sub.56
  48.1 0.1 le.94
  48.2 0.1 lt.113
  48.3 0.1 lt.114
  48.3 0.1 fusion.6
  48.4 0.6 fusion.9
  49.0 0.1 fusion.4
  49.1 16.9 %all-to-all-done.1.own_ref = bf16[16,8,2,24,128]{4,3,2,1,0:T(8,128)(2,1)S(1)} async-done(((bf16[16,8,2,24,128]{4,3,2,1,0:T(8,128)(2,1)}), bf16[16,8,2,24,128]{4,3,2,1,0:T(8,128)(2,1)S(1)}, u32[]{:S(2)}, u32[]{:S(2)}) %all-to-all-start.1) | async-done | bytes 1572896 | tf_op jit(solution)/shard_map/all_to_all | solution.py:413
  66.1 1.9 %collective-permute-start.1 = (bf16[16,8,2,24,128]{4,3,2,1,0:T(8,128)(2,1)S(1)}, bf16[16,8,2,24,128]{4,3,2,1,0:T(8,128)(2,1)S(1)}, u32[]{:S(2)}, u32[]{:S(2)}) collective-permute-start(bf16[16,8,2,24,128]{4,3,2,1,0:T(8,128)(2,1)S(1)} %all-to-all-done.1.own_ref), channel_id=1, source_target_pairs={{0,8},{1,9},{2,10},{3,11},{4,12},{5,13},{6,14},{7,15},{8,0},{9,1},... | collective-permute-start | bytes 4718600 | tf_op jit(solution)/shard_map/ppermute | solution.py:417
  68.0 0.1 multiply_reduce_fusion.1
  68.1 0.1 multiply_reduce_fusion
  68.2 0.1 add.205
  68.3 0.1 le.91
  68.4 0.1 le.92
  68.5 1.3 %fusion = (s32[2,35]{0,1:T(8,128)S(1)}, s32[2,35]{0,1:T(8,128)S(1)}) fusion(s32[64]{0:T(128)S(1)} %sub.56, s32[2,64]{1,0:T(2,128)S(1)} %compare_select_fusion.4, s32[35]{0:T(128)S(1)} %get-tuple-element.35, s32[35]{0:T(128)S(1)} %get-tuple-element.36), kind=kLoop, calls=%fused_computation.5 | loop fusion | flops 26740 | bytes 1608 | tf_op jit(solution)/shard_map/reduce_sum | solution.py:398
  69.9 0.1 copy.12
  69.9 0.1 copy.13
  70.0 0.1 convert_reduce_fusion.3
  70.1 3.6 %collective-permute-start = (bf16[8,4,24,128]{3,2,1,0:T(8,128)(2,1)S(1)}, bf16[8,4,24,128]{3,2,1,0:T(8,128)(2,1)S(1)}, u32[]{:S(2)}, u32[]{:S(2)}) collective-permute-start(bf16[8,4,24,128]{3,2,1,0:T(8,128)(2,1)S(1)} %get-tuple-element.14.q_ref), channel_id=1, source_target_pairs={{0,32},{32,0},{1,33},{33,1},{2,34},{34,2},{3,35},{35,3},{4,36},{36... | collective-permute-start | bytes 589832 | tf_op jit(solution)/shard_map/ppermute | solution.py:416
  73.7 0.6 minimum_add_fusion
  74.3 0.1 slice.3
  74.3 0.8 add.213
  75.1 0.6 convert_reduce_fusion.2
  75.7 0.7 concatenate.3.info
  76.5 1.0 order.1
  77.4 1.9 %collective-permute-done.q_ref = bf16[8,4,24,128]{3,2,1,0:T(8,128)(2,1)S(1)} collective-permute-done((bf16[8,4,24,128]{3,2,1,0:T(8,128)(2,1)S(1)}, bf16[8,4,24,128]{3,2,1,0:T(8,128)(2,1)S(1)}, u32[]{:S(2)}, u32[]{:S(2)}) %collective-permute-start) | collective-permute-done | bytes 196640 | tf_op jit(solution)/shard_map/ppermute | solution.py:416
  79.3 5.3 %far.1 = (bf16[8,5,24,128]{3,2,1,0:T(8,128)(2,1)S(1)}, bf16[6144,128]{1,0:T(8,128)(2,1)S(1)}, bf16[6144,128]{1,0:T(8,128)(2,1)S(1)}) custom-call(s32[241]{0:T(256)S(1)} %concatenate.3.info, bf16[8,4,24,128]{3,2,1,0:T(8,128)(2,1)S(1)} %collective-permute-done.q_ref, ...), custom_call_target="tpu_custom_call", output_to_operand_aliasing={{1}: (3, {}), {2}: (4, {})} | custom-call | flops 6000000000 | bytes 4000000 | tf_op jit(solution)/shard_map/far/pallas_call | solution.py:279
  84.6 2.6 %collective-permute-start.2 = (bf16[8,5,24,128]{3,2,1,0:T(8,128)(2,1)S(1)}, bf16[8,5,24,128]{3,2,1,0:T(8,128)(2,1)S(1)}, u32[]{:S(2)}, u32[]{:S(2)}) collective-permute-start(bf16[8,5,24,128]{3,2,1,0:T(8,128)(2,1)S(1)} %get-tuple-element.22), channel_id=1, source_target_pairs={{0,32},{32,0},{1,33},{33,1},{2,34},{34,2},{3,35},{35,3},{4,36},{36... | collective-permute-start | bytes 737288 | tf_op jit(solution)/shard_map/ppermute | solution.py:421
  87.3 4.8 %near.1 = (f32[8,4,24,128]{3,2,1,0:T(8,128)S(1)}, f32[8,4,24,128]{3,2,1,0:T(8,128)S(1)}) custom-call(s32[241]{0:T(256)S(1)} %concatenate.3.info, bf16[8,4,24,128]{3,2,1,0:T(8,128)(2,1)S(1)} %get-tuple-element.14.q_ref, bf16[6144,128]{1,0:T(8,128)(2,1)S(1)} %get-tuple-element.18.k_buf, bf16[6144,128]{1,0:T(8,128)(2,1)S(1)} %get-tuple-element.19.v_buf), custom_call_target="tpu_custom_call" | custom-call | flops 6000000000 | bytes 4000000 | tf_op jit(solution)/shard_map/near/pallas_call | solution.py:297
  92.1 1.9 %collective-permute-done.2.far_ref = bf16[8,5,24,128]{3,2,1,0:T(8,128)(2,1)S(1)} collective-permute-done((bf16[8,5,24,128]{3,2,1,0:T(8,128)(2,1)S(1)}, bf16[8,5,24,128]{3,2,1,0:T(8,128)(2,1)S(1)}, u32[]{:S(2)}, u32[]{:S(2)}) %collective-permute-start.2) | collective-permute-done | bytes 245792 | tf_op jit(solution)/shard_map/ppermute | solution.py:421
  94.0 0.5 merge.1
  94.4 26.0 %all_to_all.15 = bf16[8,24,512]{2,1,0:T(8,128)(2,1)S(1)} all-to-all(bf16[8,24,512]{2,1,0:T(8,128)(2,1)S(1)} %merge.1), channel_id=1, replica_groups=mesh['zhi'=8,'zlo'=2,'plane'=32] {'zhi'}, dimensions={0} | all-to-all | bytes 393216 | tf_op jit(solution)/shard_map/all_to_all | solution.py:424
  120.4 0.7 copy.15
  (16 shorter events, 0.1 us)
Async XLA Ops:
  1.7 36.9 %all-to-all-start = ((bf16[8,6,24,128]{3,2,1,0:T(8,128)(2,1)}), bf16[8,6,24,128]{3,2,1,0:T(8,128)(2,1)S(1)}, u32[]{:S(2)}, u32[]{:S(2)}) async-start(bf16[8,6,24,128]{3,2,1,0:T(8,128)(2,1)} %pack.1), calls=%async_computation | async-start | bytes 589824 | tf_op jit(solution)/shard_map/all_to_all | solution.py:411
  40.0 7.5 %copy-start = (s32[64]{0:T(128)S(1)}, s32[64]{0:T(128)}, u32[]{:S(2)}) copy-start(s32[64]{0:T(128)} %param.9) | copy-start | bytes 772
  40.0 26.1 %all-to-all-start.1 = ((bf16[16,8,2,24,128]{4,3,2,1,0:T(8,128)(2,1)}), bf16[16,8,2,24,128]{4,3,2,1,0:T(8,128)(2,1)S(1)}, u32[]{:S(2)}, u32[]{:S(2)}) async-start(bf16[16,8,2,24,128]{4,3,2,1,0:T(8,128)(2,1)} %get-tuple-element.15), calls=%async_computation.1 | async-start | bytes 3145728 | tf_op jit(solution)/shard_map/all_to_all | solution.py:413
  66.1 13.2 %collective-permute-start.1 = (bf16[16,8,2,24,128]{4,3,2,1,0:T(8,128)(2,1)S(1)}, bf16[16,8,2,24,128]{4,3,2,1,0:T(8,128)(2,1)S(1)}, u32[]{:S(2)}, u32[]{:S(2)}) collective-permute-start(bf16[16,8,2,24,128]{4,3,2,1,0:T(8,128)(2,1)S(1)} %all-to-all-done.1.own_ref), channel_id=1, source_target_pairs={{0,8},{1,9},{2,10},{3,11},{4,12},{5,13},{6,14},{7,15},{8,0},{9,1},... | collective-permute-start | bytes 4718600 | tf_op jit(solution)/shard_map/ppermute | solution.py:417
  70.1 9.2 %collective-permute-start = (bf16[8,4,24,128]{3,2,1,0:T(8,128)(2,1)S(1)}, bf16[8,4,24,128]{3,2,1,0:T(8,128)(2,1)S(1)}, u32[]{:S(2)}, u32[]{:S(2)}) collective-permute-start(bf16[8,4,24,128]{3,2,1,0:T(8,128)(2,1)S(1)} %get-tuple-element.14.q_ref), channel_id=1, source_target_pairs={{0,32},{32,0},{1,33},{33,1},{2,34},{34,2},{3,35},{35,3},{4,36},{36... | collective-permute-start | bytes 589832 | tf_op jit(solution)/shard_map/ppermute | solution.py:416
  84.6 9.3 %collective-permute-start.2 = (bf16[8,5,24,128]{3,2,1,0:T(8,128)(2,1)S(1)}, bf16[8,5,24,128]{3,2,1,0:T(8,128)(2,1)S(1)}, u32[]{:S(2)}, u32[]{:S(2)}) collective-permute-start(bf16[8,5,24,128]{3,2,1,0:T(8,128)(2,1)S(1)} %get-tuple-element.22), channel_id=1, source_target_pairs={{0,32},{32,0},{1,33},{33,1},{2,34},{34,2},{3,35},{35,3},{4,36},{36... | collective-permute-start | bytes 737288 | tf_op jit(solution)/shard_map/ppermute | solution.py:421

commit v6 on v5

--- a/solution.py
+++ b/solution.py
@@ -186,19 +186,21 @@
     take_keys(info, other_ref, 1 - info[CORE], k_buf, v_buf)
     lane = lax.broadcasted_iota(jnp.int32, (PIECE, HEAD_DIM), 1)
 
+    packed = [jnp.zeros((PIECE, HEAD_DIM), jnp.float32)]
+
     def put(n, out, mass):
-        o_ref[n, :GROUP] = out.astype(jnp.bfloat16)
+        o_ref[n * GROUP : (n + 1) * GROUP] = out.astype(jnp.bfloat16)
         high = mass.astype(jnp.bfloat16).astype(jnp.float32)
         rest = mass - high
         middle = rest.astype(jnp.bfloat16).astype(jnp.float32)
-        pieces = (high, middle, rest - middle)
-        packed = jnp.zeros((PIECE, HEAD_DIM), jnp.float32)
-        for g in range(GROUP):
-            for i, piece in enumerate(pieces):
-                packed = jnp.where(lane == 3 * g + i, piece[g], packed)
-        o_ref[n, GROUP] = packed.astype(jnp.bfloat16)
+        for i, piece in enumerate((high, middle, rest - middle)):
+            for g in range(GROUP):
+                packed[0] = jnp.where(
+                    lane == (n * GROUP + g) * 3 + i, piece[g], packed[0]
+                )
 
     attend_sources(info, 1 - info[ZLO], q_ref, k_buf, v_buf, scratch, put)
+    o_ref[SOURCES * GROUP] = packed[0].astype(jnp.bfloat16)
 
 
 def near_kernel(info, q_ref, k_buf, v_buf, o_ref, m_ref, *scratch):
@@ -210,18 +212,17 @@
 
 
 def merge_kernel(near_ref, mass_ref, far_ref, o_ref):
+    packed = far_ref[SOURCES * GROUP].astype(jnp.float32)
     for n in range(SOURCES):
-        packed = far_ref[n, GROUP].astype(jnp.float32)
         for g in range(GROUP):
+            c = (n * GROUP + g) * 3
             a = mass_ref[n, g]
             b = (
-                packed[:, 3 * g : 3 * g + 1]
-                + packed[:, 3 * g + 1 : 3 * g + 2]
-                + packed[:, 3 * g + 2 : 3 * g + 3]
+                packed[:, c : c + 1] + packed[:, c + 1 : c + 2] + packed[:, c + 2 : c + 3]
             )
             m = jnp.maximum(a, b)
             wa, wb = jnp.exp2(a - m), jnp.exp2(b - m)
-            out = (wa * near_ref[n, g] + wb * far_ref[n, g].astype(jnp.float32)) / (wa + wb)
+            out = (wa * near_ref[n, g] + wb * far_ref[n * GROUP + g].astype(jnp.float32)) / (wa + wb)
             o_ref[n, :, g * HEAD_DIM : (g + 1) * HEAD_DIM] = out.astype(jnp.bfloat16)
 
 
@@ -279,7 +280,7 @@
     return pl.pallas_call(
         far_kernel,
         out_shape=(
-            shape(SOURCES, GROUP + 1, PIECE, HEAD_DIM),
+            shape(SOURCES * GROUP + 1, PIECE, HEAD_DIM),
             shape(KEYS, HEAD_DIM),
             shape(KEYS, HEAD_DIM),
         ),

time: 122 us -> 121 us (level)
  no operation moved by 1% of the time
where the time goes in v6:
time: 121 us; the launch traced here: 120 us
  waiting for transfers between devices  39.4 us (33%)
  starting transfers between devices  30.7 us (25%)
  blocking collectives  26.3 us (22%)
  Pallas kernels  14.5 us (12%)
  other arithmetic  6.09 us (5%)
  local copies, waits for them, and re-layouts  3.24 us (3%)
    all_to_all x1, blocking collectives, body(): out = lax.all_to_all(out, 'zhi', 0, 0, tiled=True)  26.3 us
    all_to_all x1, waiting for transfers between devices, body(): packed = lax.all_to_all(packed, 'zhi', 0, 0, tiled=True)  19.6 us
    all_to_all x1, waiting for transfers between devices, body(): lax.all_to_all(spread, 'plane', 0, 0, axis_index_groups=PLANE, tiled=True)  16.9 us
    all_to_all x1, starting transfers between devices, body(): packed = lax.all_to_all(packed, 'zhi', 0, 0, tiled=True)  15.1 us
    all_to_all x1, starting transfers between devices, body(): lax.all_to_all(spread, 'plane', 0, 0, axis_index_groups=PLANE, tiled=True)  7.53 us
    pallas_call x1, Pallas kernels, far_part(): pl.pallas_call(far_kernel, out_shape=(shape(SOURCES * GROUP + 1, PIECE, H...  5.32 us
    pallas_call x1, Pallas kernels, near_part(): pl.pallas_call(near_kernel, out_shape=(shape(SOURCES, GROUP, PIECE, HEAD_...  4.78 us
    ppermute x1, starting transfers between devices, body(): far_q = lax.ppermute(near_q, 'zlo', SWAP)  3.57 us
  transfers between devices with their start and end apart: 5, of which 4 were waited for; matrix products, arithmetic and copies ran while one was open for 7% of the time, Pallas kernels for 5%

profile of v6, /device:TPU:8, one launch (start us, length us, event | category | flops | bytes accessed | tf_op | source)
XLA Modules:
  0.0 120.4 jit_solution(6533437063315809416)
XLA Ops:
  0.0 1.7 %pack.1 = bf16[8,6,24,128]{3,2,1,0:T(8,128)(2,1)} custom-call(bf16[24,4096]{1,0:T(8,128)(2,1)} %q_ref.1, bf16[24,1024]{1,0:T(8,128)(2,1)} %k_ref.1, bf16[24,1024]{1,0:T(8,128)(2,1)} %v_ref.1), custom_call_target="tpu_custom_call" | custom-call | tf_op jit(solution)/shard_map/pack/pallas_call | solution.py:325
  1.7 15.1 %all-to-all-start = ((bf16[8,6,24,128]{3,2,1,0:T(8,128)(2,1)}), bf16[8,6,24,128]{3,2,1,0:T(8,128)(2,1)S(1)}, u32[]{:S(2)}, u32[]{:S(2)}) async-start(bf16[8,6,24,128]{3,2,1,0:T(8,128)(2,1)} %pack.1), calls=%async_computation | async-start | bytes 589824 | tf_op jit(solution)/shard_map/all_to_all | solution.py:412
  16.8 0.1 pad_add_fusion
  16.9 0.1 add_add_fusion
  17.0 0.1 add.198
  17.1 0.8 select_reduce_fusion.2
  17.9 1.0 convert_reduce_fusion
  18.9 0.1 select_reduce_fusion.3
  19.0 19.6 %all-to-all-done.packed_ref = bf16[8,6,24,128]{3,2,1,0:T(8,128)(2,1)S(1)} async-done(((bf16[8,6,24,128]{3,2,1,0:T(8,128)(2,1)}), bf16[8,6,24,128]{3,2,1,0:T(8,128)(2,1)S(1)}, u32[]{:S(2)}, u32[]{:S(2)}) %all-to-all-start) | async-done | bytes 294944 | tf_op jit(solution)/shard_map/all_to_all | solution.py:412
  38.6 1.4 %fan.1 = (bf16[16,8,2,24,128]{4,3,2,1,0:T(8,128)(2,1)}, bf16[8,4,24,128]{3,2,1,0:T(8,128)(2,1)S(1)}) custom-call(bf16[8,6,24,128]{3,2,1,0:T(8,128)(2,1)S(1)} %all-to-all-done.packed_ref), custom_call_target="tpu_custom_call" | custom-call | tf_op jit(solution)/shard_map/fan/pallas_call | solution.py:335
  40.0 7.5 %all-to-all-start.1 = ((bf16[16,8,2,24,128]{4,3,2,1,0:T(8,128)(2,1)}), bf16[16,8,2,24,128]{4,3,2,1,0:T(8,128)(2,1)S(1)}, u32[]{:S(2)}, u32[]{:S(2)}) async-start(bf16[16,8,2,24,128]{4,3,2,1,0:T(8,128)(2,1)} %get-tuple-element.15), calls=%async_computation.1 | async-start | bytes 3145728 | tf_op jit(solution)/shard_map/all_to_all | solution.py:414
  47.5 0.1 convert_reduce_fusion.1
  47.6 0.2 select_reduce_fusion.1
  47.8 0.1 reduce_sum.124
  47.9 0.1 sub.52
  48.0 0.1 sub.56
  48.1 0.1 le.94
  48.2 0.1 lt.113
  48.3 0.1 lt.114
  48.3 0.1 fusion.6
  48.4 0.6 fusion.9
  49.0 0.1 fusion.4
  49.1 16.9 %all-to-all-done.1.own_ref = bf16[16,8,2,24,128]{4,3,2,1,0:T(8,128)(2,1)S(1)} async-done(((bf16[16,8,2,24,128]{4,3,2,1,0:T(8,128)(2,1)}), bf16[16,8,2,24,128]{4,3,2,1,0:T(8,128)(2,1)S(1)}, u32[]{:S(2)}, u32[]{:S(2)}) %all-to-all-start.1) | async-done | bytes 1572896 | tf_op jit(solution)/shard_map/all_to_all | solution.py:414
  66.1 1.9 %collective-permute-start.1 = (bf16[16,8,2,24,128]{4,3,2,1,0:T(8,128)(2,1)S(1)}, bf16[16,8,2,24,128]{4,3,2,1,0:T(8,128)(2,1)S(1)}, u32[]{:S(2)}, u32[]{:S(2)}) collective-permute-start(bf16[16,8,2,24,128]{4,3,2,1,0:T(8,128)(2,1)S(1)} %all-to-all-done.1.own_ref), channel_id=1, source_target_pairs={{0,8},{1,9},{2,10},{3,11},{4,12},{5,13},{6,14},{7,15},{8,0},{9,1},... | collective-permute-start | bytes 4718600 | tf_op jit(solution)/shard_map/ppermute | solution.py:418
  68.0 0.1 multiply_reduce_fusion.1
  68.1 0.1 multiply_reduce_fusion
  68.2 0.1 add.205
  68.3 0.1 le.91
  68.4 0.1 le.92
  68.5 1.3 %fusion = (s32[2,35]{0,1:T(8,128)S(1)}, s32[2,35]{0,1:T(8,128)S(1)}) fusion(s32[64]{0:T(128)S(1)} %sub.56, s32[2,64]{1,0:T(2,128)S(1)} %compare_select_fusion.4, s32[35]{0:T(128)S(1)} %get-tuple-element.35, s32[35]{0:T(128)S(1)} %get-tuple-element.36), kind=kLoop, calls=%fused_computation.5 | loop fusion | flops 26740 | bytes 1608 | tf_op jit(solution)/shard_map/reduce_sum | solution.py:399
  69.9 0.1 copy.12
  69.9 0.1 copy.13
  70.0 0.1 convert_reduce_fusion.3
  70.1 3.6 %collective-permute-start = (bf16[8,4,24,128]{3,2,1,0:T(8,128)(2,1)S(1)}, bf16[8,4,24,128]{3,2,1,0:T(8,128)(2,1)S(1)}, u32[]{:S(2)}, u32[]{:S(2)}) collective-permute-start(bf16[8,4,24,128]{3,2,1,0:T(8,128)(2,1)S(1)} %get-tuple-element.14.q_ref), channel_id=1, source_target_pairs={{0,32},{32,0},{1,33},{33,1},{2,34},{34,2},{3,35},{35,3},{4,36},{36... | collective-permute-start | bytes 589832 | tf_op jit(solution)/shard_map/ppermute | solution.py:417
  73.7 0.6 minimum_add_fusion
  74.3 0.1 slice.3
  74.3 0.8 add.213
  75.1 0.6 convert_reduce_fusion.2
  75.7 0.7 concatenate.3.info
  76.5 1.0 order.1
  77.4 1.9 %collective-permute-done.q_ref = bf16[8,4,24,128]{3,2,1,0:T(8,128)(2,1)S(1)} collective-permute-done((bf16[8,4,24,128]{3,2,1,0:T(8,128)(2,1)S(1)}, bf16[8,4,24,128]{3,2,1,0:T(8,128)(2,1)S(1)}, u32[]{:S(2)}, u32[]{:S(2)}) %collective-permute-start) | collective-permute-done | bytes 196640 | tf_op jit(solution)/shard_map/ppermute | solution.py:417
  79.3 5.3 %far.1 = (bf16[33,24,128]{2,1,0:T(8,128)(2,1)S(1)}, bf16[6144,128]{1,0:T(8,128)(2,1)S(1)}, bf16[6144,128]{1,0:T(8,128)(2,1)S(1)}) custom-call(s32[241]{0:T(256)S(1)} %concatenate.3.info, bf16[8,4,24,128]{3,2,1,0:T(8,128)(2,1)S(1)} %collective-permute-done.q_ref, ...), custom_call_target="tpu_custom_call", output_to_operand_aliasing={{1}: (3, {}), {2}: (4, {})} | custom-call | flops 6000000000 | bytes 4000000 | tf_op jit(solution)/shard_map/far/pallas_call | solution.py:280
  84.6 2.6 %collective-permute-start.2 = (bf16[33,24,128]{2,1,0:T(8,128)(2,1)S(1)}, bf16[33,24,128]{2,1,0:T(8,128)(2,1)S(1)}, u32[]{:S(2)}, u32[]{:S(2)}) collective-permute-start(bf16[33,24,128]{2,1,0:T(8,128)(2,1)S(1)} %get-tuple-element.22), channel_id=1, source_target_pairs={{0,32},{32,0},{1,33},{33,1},{2,34},{34,2},{3,35},{35,3},{4,36},{36... | collective-permute-start | bytes 608264 | tf_op jit(solution)/shard_map/ppermute | solution.py:422
  87.3 4.8 %near.1 = (f32[8,4,24,128]{3,2,1,0:T(8,128)S(1)}, f32[8,4,24,128]{3,2,1,0:T(8,128)S(1)}) custom-call(s32[241]{0:T(256)S(1)} %concatenate.3.info, bf16[8,4,24,128]{3,2,1,0:T(8,128)(2,1)S(1)} %get-tuple-element.14.q_ref, bf16[6144,128]{1,0:T(8,128)(2,1)S(1)} %get-tuple-element.18.k_buf, bf16[6144,128]{1,0:T(8,128)(2,1)S(1)} %get-tuple-element.19.v_buf), custom_call_target="tpu_custom_call" | custom-call | flops 6000000000 | bytes 4000000 | tf_op jit(solution)/shard_map/near/pallas_call | solution.py:298
  92.1 1.0 collective-permute-done.2.far_ref
  93.0 0.3 merge.1
  93.4 26.3 %all_to_all.15 = bf16[8,24,512]{2,1,0:T(8,128)(2,1)S(1)} all-to-all(bf16[8,24,512]{2,1,0:T(8,128)(2,1)S(1)} %merge.1), channel_id=1, replica_groups=mesh['zhi'=8,'zlo'=2,'plane'=32] {'zhi'}, dimensions={0} | all-to-all | bytes 393216 | tf_op jit(solution)/shard_map/all_to_all | solution.py:425
  119.7 0.7 copy.15
  (16 shorter events, 0.1 us)
Async XLA Ops:
  1.7 36.9 %all-to-all-start = ((bf16[8,6,24,128]{3,2,1,0:T(8,128)(2,1)}), bf16[8,6,24,128]{3,2,1,0:T(8,128)(2,1)S(1)}, u32[]{:S(2)}, u32[]{:S(2)}) async-start(bf16[8,6,24,128]{3,2,1,0:T(8,128)(2,1)} %pack.1), calls=%async_computation | async-start | bytes 589824 | tf_op jit(solution)/shard_map/all_to_all | solution.py:412
  40.0 7.5 %copy-start = (s32[64]{0:T(128)S(1)}, s32[64]{0:T(128)}, u32[]{:S(2)}) copy-start(s32[64]{0:T(128)} %param.9) | copy-start | bytes 772
  40.0 26.1 %all-to-all-start.1 = ((bf16[16,8,2,24,128]{4,3,2,1,0:T(8,128)(2,1)}), bf16[16,8,2,24,128]{4,3,2,1,0:T(8,128)(2,1)S(1)}, u32[]{:S(2)}, u32[]{:S(2)}) async-start(bf16[16,8,2,24,128]{4,3,2,1,0:T(8,128)(2,1)} %get-tuple-element.15), calls=%async_computation.1 | async-start | bytes 3145728 | tf_op jit(solution)/shard_map/all_to_all | solution.py:414
  66.1 13.2 %collective-permute-start.1 = (bf16[16,8,2,24,128]{4,3,2,1,0:T(8,128)(2,1)S(1)}, bf16[16,8,2,24,128]{4,3,2,1,0:T(8,128)(2,1)S(1)}, u32[]{:S(2)}, u32[]{:S(2)}) collective-permute-start(bf16[16,8,2,24,128]{4,3,2,1,0:T(8,128)(2,1)S(1)} %all-to-all-done.1.own_ref), channel_id=1, source_target_pairs={{0,8},{1,9},{2,10},{3,11},{4,12},{5,13},{6,14},{7,15},{8,0},{9,1},... | collective-permute-start | bytes 4718600 | tf_op jit(solution)/shard_map/ppermute | solution.py:418
  70.1 9.2 %collective-permute-start = (bf16[8,4,24,128]{3,2,1,0:T(8,128)(2,1)S(1)}, bf16[8,4,24,128]{3,2,1,0:T(8,128)(2,1)S(1)}, u32[]{:S(2)}, u32[]{:S(2)}) collective-permute-start(bf16[8,4,24,128]{3,2,1,0:T(8,128)(2,1)S(1)} %get-tuple-element.14.q_ref), channel_id=1, source_target_pairs={{0,32},{32,0},{1,33},{33,1},{2,34},{34,2},{3,35},{35,3},{4,36},{36... | collective-permute-start | bytes 589832 | tf_op jit(solution)/shard_map/ppermute | solution.py:417
  84.6 8.4 %collective-permute-start.2 = (bf16[33,24,128]{2,1,0:T(8,128)(2,1)S(1)}, bf16[33,24,128]{2,1,0:T(8,128)(2,1)S(1)}, u32[]{:S(2)}, u32[]{:S(2)}) collective-permute-start(bf16[33,24,128]{2,1,0:T(8,128)(2,1)S(1)} %get-tuple-element.22), channel_id=1, source_target_pairs={{0,32},{32,0},{1,33},{33,1},{2,34},{34,2},{3,35},{35,3},{4,36},{36... | collective-permute-start | bytes 608264 | tf_op jit(solution)/shard_map/ppermute | solution.py:422

commit v7 on v6

--- a/solution.py
+++ b/solution.py
@@ -235,14 +235,20 @@
             o_ref[h, 2 + g] = q_ref[:, c : c + HEAD_DIM]
 
 
-def fan_kernel(packed_ref, o_ref, q_ref):
-    for i in range(16):
-        o_ref[i] = packed_ref[:, :2]
+def fan_kernel(packed_ref, o_ref, q_ref, sems):
+    copies = [
+        pltpu.make_async_copy(packed_ref.at[:, :2], o_ref.at[i], sems.at[i]) for i in range(16)
+    ]
+    for c in copies:
+        c.start()
     q_ref[...] = packed_ref[:, 2:]
+    for c in copies:
+        c.wait()
 
 
 SMEM = pl.BlockSpec(memory_space=pltpu.SMEM)
 VMEM = pl.BlockSpec(memory_space=pltpu.VMEM)
+ANY = pl.BlockSpec(memory_space=pl.ANY)
 COST = pl.CostEstimate(flops=6_000_000_000, bytes_accessed=4_000_000, transcendentals=4_000_000)
 
 
@@ -339,7 +345,8 @@
             shape(SOURCES, GROUP, PIECE, HEAD_DIM),
         ),
         in_specs=[VMEM],
-        out_specs=(VMEM, VMEM),
+        out_specs=(ANY, VMEM),
+        scratch_shapes=[pltpu.SemaphoreType.DMA((16,))],
         compiler_params=SMALL,
         name="fan",
     )(packed)
@@ -357,7 +364,7 @@
     return jnp.sum(jnp.where(at[:, None] == index[None, :], values[None, :], 0), axis=1)
 
 
-def table(visit_ids, span_order):
+def basics(visit_ids, span_order):
     zlo = lax.axis_index("zlo").astype(jnp.int32)
     block = jnp.arange(SPANS, dtype=jnp.int32)
     mine = (block // 4) % 2 == zlo
@@ -371,6 +378,11 @@
         (visit_ids[None, :] < jnp.arange(VISITS, dtype=jnp.int32)[:, None]).astype(jnp.int32),
         axis=1,
     )
+    return count, ordered, starts
+
+
+def listing(span_order, count, ordered, starts):
+    zlo = lax.axis_index("zlo").astype(jnp.int32)
     at = lax.axis_index("plane")
     place = jnp.stack([at // 16, at // 8 % 2, zlo, at % 8 * PIECE]).astype(jnp.int32)
     side = jnp.stack([zlo, 1 - zlo])[:, None]
@@ -407,10 +419,11 @@
 
 
 def body(queries, key_rows, value_rows, visit_ids, span_order):
-    info = table(visit_ids, span_order)
+    basic = basics(visit_ids, span_order)
     packed = pack(queries, key_rows, value_rows)
     packed = lax.all_to_all(packed, "zhi", 0, 0, tiled=True)
     spread, near_q = fan(packed)
+    info = listing(span_order, *basic)
     own = lax.all_to_all(
         spread, "plane", 0, 0, axis_index_groups=PLANE, tiled=True
     )

time: 121 us -> 121 us (level)
  no operation moved by 1% of the time
where the time goes in v7:
time: 121 us; the launch traced here: 120 us
  waiting for transfers between devices  39.4 us (33%)
  starting transfers between devices  30.6 us (25%)
  blocking collectives  26.3 us (22%)
  Pallas kernels  14.4 us (12%)
  other arithmetic  6.09 us (5%)
  local copies, waits for them, and re-layouts  3.24 us (3%)
    all_to_all x1, blocking collectives, body(): out = lax.all_to_all(out, 'zhi', 0, 0, tiled=True)  26.3 us
    all_to_all x1, waiting for transfers between devices, body(): packed = lax.all_to_all(packed, 'zhi', 0, 0, tiled=True)  19.6 us
    all_to_all x1, waiting for transfers between devices, body(): lax.all_to_all(spread, 'plane', 0, 0, axis_index_groups=PLANE, tiled=True)  16.9 us
    all_to_all x1, starting transfers between devices, body(): packed = lax.all_to_all(packed, 'zhi', 0, 0, tiled=True)  15.1 us
    all_to_all x1, starting transfers between devices, body(): lax.all_to_all(spread, 'plane', 0, 0, axis_index_groups=PLANE, tiled=True)  7.41 us
    pallas_call x1, Pallas kernels, far_part(): pl.pallas_call(far_kernel, out_shape=(shape(SOURCES * GROUP + 1, PIECE, H...  5.33 us
    pallas_call x1, Pallas kernels, near_part(): pl.pallas_call(near_kernel, out_shape=(shape(SOURCES, GROUP, PIECE, HEAD_...  4.78 us
    ppermute x1, starting transfers between devices, body(): far_q = lax.ppermute(near_q, 'zlo', SWAP)  3.57 us
  transfers between devices with their start and end apart: 5, of which 4 were waited for; matrix products, arithmetic and copies ran while one was open for 7% of the time, Pallas kernels for 5%

profile of v7, /device:TPU:8, one launch (start us, length us, event | category | flops | bytes accessed | tf_op | source)
XLA Modules:
  0.0 120.2 jit_solution(14745987441726591833)
XLA Ops:
  0.0 1.7 %pack.1 = bf16[8,6,24,128]{3,2,1,0:T(8,128)(2,1)} custom-call(bf16[24,4096]{1,0:T(8,128)(2,1)} %q_ref.1, bf16[24,1024]{1,0:T(8,128)(2,1)} %k_ref.1, bf16[24,1024]{1,0:T(8,128)(2,1)} %v_ref.1), custom_call_target="tpu_custom_call" | custom-call | tf_op jit(solution)/shard_map/pack/pallas_call | solution.py:331
  1.7 15.1 %all-to-all-start = ((bf16[8,6,24,128]{3,2,1,0:T(8,128)(2,1)}), bf16[8,6,24,128]{3,2,1,0:T(8,128)(2,1)S(1)}, u32[]{:S(2)}, u32[]{:S(2)}) async-start(bf16[8,6,24,128]{3,2,1,0:T(8,128)(2,1)} %pack.1), calls=%async_computation | async-start | bytes 589824 | tf_op jit(solution)/shard_map/all_to_all | solution.py:424
  16.8 0.1 pad_add_fusion
  16.9 0.1 add_add_fusion
  17.0 0.1 add.198
  17.1 0.8 select_reduce_fusion.2
  17.9 1.0 convert_reduce_fusion
  18.9 0.1 select_reduce_fusion.3
  19.0 19.6 %all-to-all-done.packed_ref = bf16[8,6,24,128]{3,2,1,0:T(8,128)(2,1)S(1)} async-done(((bf16[8,6,24,128]{3,2,1,0:T(8,128)(2,1)}), bf16[8,6,24,128]{3,2,1,0:T(8,128)(2,1)S(1)}, u32[]{:S(2)}, u32[]{:S(2)}) %all-to-all-start) | async-done | bytes 294944 | tf_op jit(solution)/shard_map/all_to_all | solution.py:424
  38.6 1.3 %fan.1 = (bf16[16,8,2,24,128]{4,3,2,1,0:T(8,128)(2,1)}, bf16[8,4,24,128]{3,2,1,0:T(8,128)(2,1)S(1)}) custom-call(bf16[8,6,24,128]{3,2,1,0:T(8,128)(2,1)S(1)} %all-to-all-done.packed_ref), custom_call_target="tpu_custom_call" | custom-call | tf_op jit(solution)/shard_map/fan/pallas_call | solution.py:341
  39.9 7.4 %all-to-all-start.1 = ((bf16[16,8,2,24,128]{4,3,2,1,0:T(8,128)(2,1)}), bf16[16,8,2,24,128]{4,3,2,1,0:T(8,128)(2,1)S(1)}, u32[]{:S(2)}, u32[]{:S(2)}) async-start(bf16[16,8,2,24,128]{4,3,2,1,0:T(8,128)(2,1)} %get-tuple-element.15), calls=%async_computation.1 | async-start | bytes 3145728 | tf_op jit(solution)/shard_map/all_to_all | solution.py:427
  47.4 0.1 convert_reduce_fusion.1
  47.5 0.2 select_reduce_fusion.1
  47.6 0.1 reduce_sum.124
  47.7 0.1 sub.52
  47.8 0.1 sub.56
  47.9 0.1 le.94
  48.0 0.1 lt.113
  48.1 0.1 lt.114
  48.2 0.1 fusion.6
  48.3 0.6 fusion.9
  48.9 0.1 fusion.4
  48.9 16.9 %all-to-all-done.1.own_ref = bf16[16,8,2,24,128]{4,3,2,1,0:T(8,128)(2,1)S(1)} async-done(((bf16[16,8,2,24,128]{4,3,2,1,0:T(8,128)(2,1)}), bf16[16,8,2,24,128]{4,3,2,1,0:T(8,128)(2,1)S(1)}, u32[]{:S(2)}, u32[]{:S(2)}) %all-to-all-start.1) | async-done | bytes 1572896 | tf_op jit(solution)/shard_map/all_to_all | solution.py:427
  65.9 1.9 %collective-permute-start.1 = (bf16[16,8,2,24,128]{4,3,2,1,0:T(8,128)(2,1)S(1)}, bf16[16,8,2,24,128]{4,3,2,1,0:T(8,128)(2,1)S(1)}, u32[]{:S(2)}, u32[]{:S(2)}) collective-permute-start(bf16[16,8,2,24,128]{4,3,2,1,0:T(8,128)(2,1)S(1)} %all-to-all-done.1.own_ref), channel_id=1, source_target_pairs={{0,8},{1,9},{2,10},{3,11},{4,12},{5,13},{6,14},{7,15},{8,0},{9,1},... | collective-permute-start | bytes 4718600 | tf_op jit(solution)/shard_map/ppermute | solution.py:431
  67.8 0.1 multiply_reduce_fusion.1
  67.9 0.1 multiply_reduce_fusion
  68.1 0.1 add.205
  68.2 0.1 le.91
  68.2 0.1 le.92
  68.3 1.3 %fusion = (s32[2,35]{0,1:T(8,128)S(1)}, s32[2,35]{0,1:T(8,128)S(1)}) fusion(s32[64]{0:T(128)S(1)} %sub.56, s32[2,64]{1,0:T(2,128)S(1)} %compare_select_fusion.4, s32[35]{0:T(128)S(1)} %get-tuple-element.35, s32[35]{0:T(128)S(1)} %get-tuple-element.36), kind=kLoop, calls=%fused_computation.5 | loop fusion | flops 26740 | bytes 1608 | tf_op jit(solution)/shard_map/reduce_sum | solution.py:411
  69.7 0.1 copy.12
  69.8 0.1 copy.13
  69.9 0.1 convert_reduce_fusion.3
  69.9 3.6 %collective-permute-start = (bf16[8,4,24,128]{3,2,1,0:T(8,128)(2,1)S(1)}, bf16[8,4,24,128]{3,2,1,0:T(8,128)(2,1)S(1)}, u32[]{:S(2)}, u32[]{:S(2)}) collective-permute-start(bf16[8,4,24,128]{3,2,1,0:T(8,128)(2,1)S(1)} %get-tuple-element.14.q_ref), channel_id=1, source_target_pairs={{0,32},{32,0},{1,33},{33,1},{2,34},{34,2},{3,35},{35,3},{4,36},{36... | collective-permute-start | bytes 589832 | tf_op jit(solution)/shard_map/ppermute | solution.py:430
  73.5 0.6 minimum_add_fusion
  74.1 0.1 slice.3
  74.2 0.8 add.213
  74.9 0.6 convert_reduce_fusion.2
  75.5 0.7 concatenate.3.info
  76.3 1.0 order.1
  77.3 1.9 %collective-permute-done.q_ref = bf16[8,4,24,128]{3,2,1,0:T(8,128)(2,1)S(1)} collective-permute-done((bf16[8,4,24,128]{3,2,1,0:T(8,128)(2,1)S(1)}, bf16[8,4,24,128]{3,2,1,0:T(8,128)(2,1)S(1)}, u32[]{:S(2)}, u32[]{:S(2)}) %collective-permute-start) | collective-permute-done | bytes 196640 | tf_op jit(solution)/shard_map/ppermute | solution.py:430
  79.1 5.3 %far.1 = (bf16[33,24,128]{2,1,0:T(8,128)(2,1)S(1)}, bf16[6144,128]{1,0:T(8,128)(2,1)S(1)}, bf16[6144,128]{1,0:T(8,128)(2,1)S(1)}) custom-call(s32[241]{0:T(256)S(1)} %concatenate.3.info, bf16[8,4,24,128]{3,2,1,0:T(8,128)(2,1)S(1)} %collective-permute-done.q_ref, ...), custom_call_target="tpu_custom_call", output_to_operand_aliasing={{1}: (3, {}), {2}: (4, {})} | custom-call | flops 6000000000 | bytes 4000000 | tf_op jit(solution)/shard_map/far/pallas_call | solution.py:286
  84.5 2.6 %collective-permute-start.2 = (bf16[33,24,128]{2,1,0:T(8,128)(2,1)S(1)}, bf16[33,24,128]{2,1,0:T(8,128)(2,1)S(1)}, u32[]{:S(2)}, u32[]{:S(2)}) collective-permute-start(bf16[33,24,128]{2,1,0:T(8,128)(2,1)S(1)} %get-tuple-element.22), channel_id=1, source_target_pairs={{0,32},{32,0},{1,33},{33,1},{2,34},{34,2},{3,35},{35,3},{4,36},{36... | collective-permute-start | bytes 608264 | tf_op jit(solution)/shard_map/ppermute | solution.py:435
  87.1 4.8 %near.1 = (f32[8,4,24,128]{3,2,1,0:T(8,128)S(1)}, f32[8,4,24,128]{3,2,1,0:T(8,128)S(1)}) custom-call(s32[241]{0:T(256)S(1)} %concatenate.3.info, bf16[8,4,24,128]{3,2,1,0:T(8,128)(2,1)S(1)} %get-tuple-element.14.q_ref, bf16[6144,128]{1,0:T(8,128)(2,1)S(1)} %get-tuple-element.18.k_buf, bf16[6144,128]{1,0:T(8,128)(2,1)S(1)} %get-tuple-element.19.v_buf), custom_call_target="tpu_custom_call" | custom-call | flops 6000000000 | bytes 4000000 | tf_op jit(solution)/shard_map/near/pallas_call | solution.py:304
  91.9 1.0 collective-permute-done.2.far_ref
  92.9 0.3 merge.1
  93.2 26.3 %all_to_all.15 = bf16[8,24,512]{2,1,0:T(8,128)(2,1)S(1)} all-to-all(bf16[8,24,512]{2,1,0:T(8,128)(2,1)S(1)} %merge.1), channel_id=1, replica_groups=mesh['zhi'=8,'zlo'=2,'plane'=32] {'zhi'}, dimensions={0} | all-to-all | bytes 393216 | tf_op jit(solution)/shard_map/all_to_all | solution.py:438
  119.5 0.7 copy.15
  (16 shorter events, 0.1 us)
Async XLA Ops:
  1.7 36.9 %all-to-all-start = ((bf16[8,6,24,128]{3,2,1,0:T(8,128)(2,1)}), bf16[8,6,24,128]{3,2,1,0:T(8,128)(2,1)S(1)}, u32[]{:S(2)}, u32[]{:S(2)}) async-start(bf16[8,6,24,128]{3,2,1,0:T(8,128)(2,1)} %pack.1), calls=%async_computation | async-start | bytes 589824 | tf_op jit(solution)/shard_map/all_to_all | solution.py:424
  39.9 7.4 %copy-start = (s32[64]{0:T(128)S(1)}, s32[64]{0:T(128)}, u32[]{:S(2)}) copy-start(s32[64]{0:T(128)} %param.9) | copy-start | bytes 772
  39.9 26.0 %all-to-all-start.1 = ((bf16[16,8,2,24,128]{4,3,2,1,0:T(8,128)(2,1)}), bf16[16,8,2,24,128]{4,3,2,1,0:T(8,128)(2,1)S(1)}, u32[]{:S(2)}, u32[]{:S(2)}) async-start(bf16[16,8,2,24,128]{4,3,2,1,0:T(8,128)(2,1)} %get-tuple-element.15), calls=%async_computation.1 | async-start | bytes 3145728 | tf_op jit(solution)/shard_map/all_to_all | solution.py:427
  65.9 13.2 %collective-permute-start.1 = (bf16[16,8,2,24,128]{4,3,2,1,0:T(8,128)(2,1)S(1)}, bf16[16,8,2,24,128]{4,3,2,1,0:T(8,128)(2,1)S(1)}, u32[]{:S(2)}, u32[]{:S(2)}) collective-permute-start(bf16[16,8,2,24,128]{4,3,2,1,0:T(8,128)(2,1)S(1)} %all-to-all-done.1.own_ref), channel_id=1, source_target_pairs={{0,8},{1,9},{2,10},{3,11},{4,12},{5,13},{6,14},{7,15},{8,0},{9,1},... | collective-permute-start | bytes 4718600 | tf_op jit(solution)/shard_map/ppermute | solution.py:431
  69.9 9.2 %collective-permute-start = (bf16[8,4,24,128]{3,2,1,0:T(8,128)(2,1)S(1)}, bf16[8,4,24,128]{3,2,1,0:T(8,128)(2,1)S(1)}, u32[]{:S(2)}, u32[]{:S(2)}) collective-permute-start(bf16[8,4,24,128]{3,2,1,0:T(8,128)(2,1)S(1)} %get-tuple-element.14.q_ref), channel_id=1, source_target_pairs={{0,32},{32,0},{1,33},{33,1},{2,34},{34,2},{3,35},{35,3},{4,36},{36... | collective-permute-start | bytes 589832 | tf_op jit(solution)/shard_map/ppermute | solution.py:430
  84.5 8.4 %collective-permute-start.2 = (bf16[33,24,128]{2,1,0:T(8,128)(2,1)S(1)}, bf16[33,24,128]{2,1,0:T(8,128)(2,1)S(1)}, u32[]{:S(2)}, u32[]{:S(2)}) collective-permute-start(bf16[33,24,128]{2,1,0:T(8,128)(2,1)S(1)} %get-tuple-element.22), channel_id=1, source_target_pairs={{0,32},{32,0},{1,33},{33,1},{2,34},{34,2},{3,35},{35,3},{4,36},{36... | collective-permute-start | bytes 608264 | tf_op jit(solution)/shard_map/ppermute | solution.py:435

commit v8 on v7

--- a/solution.py
+++ b/solution.py
@@ -18,6 +18,7 @@
 KEYS = HALF * SPAN_ROWS
 PER_TILE = 4
 UNROLL = 3
+DEPTH = 256
 TILE = PER_TILE * SPAN_ROWS
 TILES = KEYS // TILE
 SOURCES = 8
@@ -137,28 +138,29 @@
         for u in range(UNROLL):
             at = i * UNROLL + u
             slots, j = item(at)
-            rows = []
+            tops = []
+            for slot in slots:
+                top = top_buf[jnp.minimum(slot, SOURCES - 1)]
+                tops.append(jnp.where(top > -jnp.inf, top, 0.0))
+            sums = [total[slot] for slot in slots]
+            mixed = jnp.zeros((2 * ROWS, HEAD_DIM), jnp.float32)
+            for d in range(0, TILE, DEPTH):
+                rows = []
+                for e in range(2):
+                    parts = []
+                    for c in range(d, d + DEPTH, HEAD_DIM):
+                        part = s_buf[at, e * ROWS : (e + 1) * ROWS, c : c + HEAD_DIM]
+                        w = jnp.exp2((part - tops[e]) * SCALE_LOG2)
+                        sums[e] = sums[e] + w
+                        parts.append(w.astype(jnp.bfloat16))
+                    rows.append(jnp.concatenate(parts, axis=1))
+                mixed = mixed + jnp.dot(
+                    jnp.concatenate(rows, axis=0),
+                    v_buf[pl.ds(pl.multiple_of(j * TILE + d, DEPTH), DEPTH), :],
+                    preferred_element_type=jnp.float32,
+                )
             for e in range(2):
-                top = top_buf[jnp.minimum(slots[e], SOURCES - 1)]
-                top = jnp.where(top > -jnp.inf, top, 0.0)
-                part_sum = total[slots[e]]
-                parts = []
-                for c in range(TILE // HEAD_DIM):
-                    part = s_buf[
-                        at,
-                        e * ROWS : (e + 1) * ROWS,
-                        c * HEAD_DIM : (c + 1) * HEAD_DIM,
-                    ]
-                    w = jnp.exp2((part - top) * SCALE_LOG2)
-                    part_sum = part_sum + w
-                    parts.append(w.astype(jnp.bfloat16))
-                total[slots[e]] = part_sum
-                rows.append(jnp.concatenate(parts, axis=1))
-            mixed = jnp.dot(
-                jnp.concatenate(rows, axis=0),
-                v_buf[pl.ds(pl.multiple_of(j * TILE, TILE), TILE), :],
-                preferred_element_type=jnp.float32,
-            )
+                total[slots[e]] = sums[e]
             for e in range(2):
                 acc[slots[e]] = acc[slots[e]] + mixed[e * ROWS : (e + 1) * ROWS]
         return carry

time: 121 us -> 120 us (level)
  no operation moved by 1% of the time
where the time goes in v8:
time: 120 us
  waiting for transfers between devices  39.6 us (33%)
  starting transfers between devices  30.7 us (26%)
  blocking collectives  26.1 us (22%)
  Pallas kernels  13.9 us (12%)
  other arithmetic  6.09 us (5%)
  local copies, waits for them, and re-layouts  3.24 us (3%)
    all_to_all x1, blocking collectives, body(): out = lax.all_to_all(out, 'zhi', 0, 0, tiled=True)  26.1 us
    all_to_all x1, waiting for transfers between devices, body(): packed = lax.all_to_all(packed, 'zhi', 0, 0, tiled=True)  19.6 us
    all_to_all x1, waiting for transfers between devices, body(): lax.all_to_all(spread, 'plane', 0, 0, axis_index_groups=PLANE, tiled=True)  16.9 us
    all_to_all x1, starting transfers between devices, body(): packed = lax.all_to_all(packed, 'zhi', 0, 0, tiled=True)  15.1 us
    all_to_all x1, starting transfers between devices, body(): lax.all_to_all(spread, 'plane', 0, 0, axis_index_groups=PLANE, tiled=True)  7.41 us
    pallas_call x1, Pallas kernels, far_part(): pl.pallas_call(far_kernel, out_shape=(shape(SOURCES * GROUP + 1, PIECE, H...  5.08 us
    pallas_call x1, Pallas kernels, near_part(): pl.pallas_call(near_kernel, out_shape=(shape(SOURCES, GROUP, PIECE, HEAD_...  4.55 us
    ppermute x1, starting transfers between devices, body(): far_q = lax.ppermute(near_q, 'zlo', SWAP)  3.57 us
  transfers between devices with their start and end apart: 5, of which 4 were waited for; matrix products, arithmetic and copies ran while one was open for 7% of the time, Pallas kernels for 5%

profile of v8, /device:TPU:8, one launch (start us, length us, event | category | flops | bytes accessed | tf_op | source)
XLA Modules:
  0.0 119.8 jit_solution(10614303325298488774)
XLA Ops:
  0.0 1.7 %pack.1 = bf16[8,6,24,128]{3,2,1,0:T(8,128)(2,1)} custom-call(bf16[24,4096]{1,0:T(8,128)(2,1)} %q_ref.1, bf16[24,1024]{1,0:T(8,128)(2,1)} %k_ref.1, bf16[24,1024]{1,0:T(8,128)(2,1)} %v_ref.1), custom_call_target="tpu_custom_call" | custom-call | tf_op jit(solution)/shard_map/pack/pallas_call | solution.py:333
  1.7 15.1 %all-to-all-start = ((bf16[8,6,24,128]{3,2,1,0:T(8,128)(2,1)}), bf16[8,6,24,128]{3,2,1,0:T(8,128)(2,1)S(1)}, u32[]{:S(2)}, u32[]{:S(2)}) async-start(bf16[8,6,24,128]{3,2,1,0:T(8,128)(2,1)} %pack.1), calls=%async_computation | async-start | bytes 589824 | tf_op jit(solution)/shard_map/all_to_all | solution.py:426
  16.8 0.1 pad_add_fusion
  16.9 0.1 add_add_fusion
  17.0 0.1 add.198
  17.1 0.8 select_reduce_fusion.2
  17.9 1.0 convert_reduce_fusion
  18.9 0.1 select_reduce_fusion.3
  19.0 19.6 %all-to-all-done.packed_ref = bf16[8,6,24,128]{3,2,1,0:T(8,128)(2,1)S(1)} async-done(((bf16[8,6,24,128]{3,2,1,0:T(8,128)(2,1)}), bf16[8,6,24,128]{3,2,1,0:T(8,128)(2,1)S(1)}, u32[]{:S(2)}, u32[]{:S(2)}) %all-to-all-start) | async-done | bytes 294944 | tf_op jit(solution)/shard_map/all_to_all | solution.py:426
  38.6 1.3 %fan.1 = (bf16[16,8,2,24,128]{4,3,2,1,0:T(8,128)(2,1)}, bf16[8,4,24,128]{3,2,1,0:T(8,128)(2,1)S(1)}) custom-call(bf16[8,6,24,128]{3,2,1,0:T(8,128)(2,1)S(1)} %all-to-all-done.packed_ref), custom_call_target="tpu_custom_call" | custom-call | tf_op jit(solution)/shard_map/fan/pallas_call | solution.py:343
  39.9 7.4 %all-to-all-start.1 = ((bf16[16,8,2,24,128]{4,3,2,1,0:T(8,128)(2,1)}), bf16[16,8,2,24,128]{4,3,2,1,0:T(8,128)(2,1)S(1)}, u32[]{:S(2)}, u32[]{:S(2)}) async-start(bf16[16,8,2,24,128]{4,3,2,1,0:T(8,128)(2,1)} %get-tuple-element.15), calls=%async_computation.1 | async-start | bytes 3145728 | tf_op jit(solution)/shard_map/all_to_all | solution.py:429
  47.4 0.1 convert_reduce_fusion.1
  47.5 0.2 select_reduce_fusion.1
  47.6 0.1 reduce_sum.124
  47.7 0.1 sub.52
  47.8 0.1 sub.56
  47.9 0.1 le.94
  48.0 0.1 lt.113
  48.1 0.1 lt.114
  48.2 0.1 fusion.6
  48.3 0.6 fusion.9
  48.9 0.1 fusion.4
  48.9 16.9 %all-to-all-done.1.own_ref = bf16[16,8,2,24,128]{4,3,2,1,0:T(8,128)(2,1)S(1)} async-done(((bf16[16,8,2,24,128]{4,3,2,1,0:T(8,128)(2,1)}), bf16[16,8,2,24,128]{4,3,2,1,0:T(8,128)(2,1)S(1)}, u32[]{:S(2)}, u32[]{:S(2)}) %all-to-all-start.1) | async-done | bytes 1572896 | tf_op jit(solution)/shard_map/all_to_all | solution.py:429
  65.9 1.9 %collective-permute-start.1 = (bf16[16,8,2,24,128]{4,3,2,1,0:T(8,128)(2,1)S(1)}, bf16[16,8,2,24,128]{4,3,2,1,0:T(8,128)(2,1)S(1)}, u32[]{:S(2)}, u32[]{:S(2)}) collective-permute-start(bf16[16,8,2,24,128]{4,3,2,1,0:T(8,128)(2,1)S(1)} %all-to-all-done.1.own_ref), channel_id=1, source_target_pairs={{0,8},{1,9},{2,10},{3,11},{4,12},{5,13},{6,14},{7,15},{8,0},{9,1},... | collective-permute-start | bytes 4718600 | tf_op jit(solution)/shard_map/ppermute | solution.py:433
  67.8 0.1 multiply_reduce_fusion.1
  67.9 0.1 multiply_reduce_fusion
  68.1 0.1 add.205
  68.2 0.1 le.91
  68.2 0.1 le.92
  68.3 1.3 %fusion = (s32[2,35]{0,1:T(8,128)S(1)}, s32[2,35]{0,1:T(8,128)S(1)}) fusion(s32[64]{0:T(128)S(1)} %sub.56, s32[2,64]{1,0:T(2,128)S(1)} %compare_select_fusion.4, s32[35]{0:T(128)S(1)} %get-tuple-element.35, s32[35]{0:T(128)S(1)} %get-tuple-element.36), kind=kLoop, calls=%fused_computation.5 | loop fusion | flops 26740 | bytes 1608 | tf_op jit(solution)/shard_map/reduce_sum | solution.py:413
  69.7 0.1 copy.12
  69.8 0.1 copy.13
  69.9 0.1 convert_reduce_fusion.3
  69.9 3.6 %collective-permute-start = (bf16[8,4,24,128]{3,2,1,0:T(8,128)(2,1)S(1)}, bf16[8,4,24,128]{3,2,1,0:T(8,128)(2,1)S(1)}, u32[]{:S(2)}, u32[]{:S(2)}) collective-permute-start(bf16[8,4,24,128]{3,2,1,0:T(8,128)(2,1)S(1)} %get-tuple-element.14.q_ref), channel_id=1, source_target_pairs={{0,32},{32,0},{1,33},{33,1},{2,34},{34,2},{3,35},{35,3},{4,36},{36... | collective-permute-start | bytes 589832 | tf_op jit(solution)/shard_map/ppermute | solution.py:432
  73.5 0.6 minimum_add_fusion
  74.1 0.1 slice.3
  74.2 0.8 add.213
  74.9 0.6 convert_reduce_fusion.2
  75.5 0.7 concatenate.3.info
  76.3 1.0 order.1
  77.3 1.9 %collective-permute-done.q_ref = bf16[8,4,24,128]{3,2,1,0:T(8,128)(2,1)S(1)} collective-permute-done((bf16[8,4,24,128]{3,2,1,0:T(8,128)(2,1)S(1)}, bf16[8,4,24,128]{3,2,1,0:T(8,128)(2,1)S(1)}, u32[]{:S(2)}, u32[]{:S(2)}) %collective-permute-start) | collective-permute-done | bytes 196640 | tf_op jit(solution)/shard_map/ppermute | solution.py:432
  79.1 5.1 %far.1 = (bf16[33,24,128]{2,1,0:T(8,128)(2,1)S(1)}, bf16[6144,128]{1,0:T(8,128)(2,1)S(1)}, bf16[6144,128]{1,0:T(8,128)(2,1)S(1)}) custom-call(s32[241]{0:T(256)S(1)} %concatenate.3.info, bf16[8,4,24,128]{3,2,1,0:T(8,128)(2,1)S(1)} %collective-permute-done.q_ref, ...), custom_call_target="tpu_custom_call", output_to_operand_aliasing={{1}: (3, {}), {2}: (4, {})} | custom-call | flops 6000000000 | bytes 4000000 | tf_op jit(solution)/shard_map/far/pallas_call | solution.py:288
  84.2 2.7 %collective-permute-start.2 = (bf16[33,24,128]{2,1,0:T(8,128)(2,1)S(1)}, bf16[33,24,128]{2,1,0:T(8,128)(2,1)S(1)}, u32[]{:S(2)}, u32[]{:S(2)}) collective-permute-start(bf16[33,24,128]{2,1,0:T(8,128)(2,1)S(1)} %get-tuple-element.22), channel_id=1, source_target_pairs={{0,32},{32,0},{1,33},{33,1},{2,34},{34,2},{3,35},{35,3},{4,36},{36... | collective-permute-start | bytes 608264 | tf_op jit(solution)/shard_map/ppermute | solution.py:437
  86.9 4.5 %near.1 = (f32[8,4,24,128]{3,2,1,0:T(8,128)S(1)}, f32[8,4,24,128]{3,2,1,0:T(8,128)S(1)}) custom-call(s32[241]{0:T(256)S(1)} %concatenate.3.info, bf16[8,4,24,128]{3,2,1,0:T(8,128)(2,1)S(1)} %get-tuple-element.14.q_ref, bf16[6144,128]{1,0:T(8,128)(2,1)S(1)} %get-tuple-element.18.k_buf, bf16[6144,128]{1,0:T(8,128)(2,1)S(1)} %get-tuple-element.19.v_buf), custom_call_target="tpu_custom_call" | custom-call | flops 6000000000 | bytes 4000000 | tf_op jit(solution)/shard_map/near/pallas_call | solution.py:306
  91.5 1.2 collective-permute-done.2.far_ref
  92.6 0.3 merge.1
  93.0 26.1 %all_to_all.15 = bf16[8,24,512]{2,1,0:T(8,128)(2,1)S(1)} all-to-all(bf16[8,24,512]{2,1,0:T(8,128)(2,1)S(1)} %merge.1), channel_id=1, replica_groups=mesh['zhi'=8,'zlo'=2,'plane'=32] {'zhi'}, dimensions={0} | all-to-all | bytes 393216 | tf_op jit(solution)/shard_map/all_to_all | solution.py:440
  119.1 0.7 copy.15
  (16 shorter events, 0.1 us)
Async XLA Ops:
  1.7 36.9 %all-to-all-start = ((bf16[8,6,24,128]{3,2,1,0:T(8,128)(2,1)}), bf16[8,6,24,128]{3,2,1,0:T(8,128)(2,1)S(1)}, u32[]{:S(2)}, u32[]{:S(2)}) async-start(bf16[8,6,24,128]{3,2,1,0:T(8,128)(2,1)} %pack.1), calls=%async_computation | async-start | bytes 589824 | tf_op jit(solution)/shard_map/all_to_all | solution.py:426
  39.9 7.4 %copy-start = (s32[64]{0:T(128)S(1)}, s32[64]{0:T(128)}, u32[]{:S(2)}) copy-start(s32[64]{0:T(128)} %param.9) | copy-start | bytes 772
  39.9 26.0 %all-to-all-start.1 = ((bf16[16,8,2,24,128]{4,3,2,1,0:T(8,128)(2,1)}), bf16[16,8,2,24,128]{4,3,2,1,0:T(8,128)(2,1)S(1)}, u32[]{:S(2)}, u32[]{:S(2)}) async-start(bf16[16,8,2,24,128]{4,3,2,1,0:T(8,128)(2,1)} %get-tuple-element.15), calls=%async_computation.1 | async-start | bytes 3145728 | tf_op jit(solution)/shard_map/all_to_all | solution.py:429
  65.9 13.2 %collective-permute-start.1 = (bf16[16,8,2,24,128]{4,3,2,1,0:T(8,128)(2,1)S(1)}, bf16[16,8,2,24,128]{4,3,2,1,0:T(8,128)(2,1)S(1)}, u32[]{:S(2)}, u32[]{:S(2)}) collective-permute-start(bf16[16,8,2,24,128]{4,3,2,1,0:T(8,128)(2,1)S(1)} %all-to-all-done.1.own_ref), channel_id=1, source_target_pairs={{0,8},{1,9},{2,10},{3,11},{4,12},{5,13},{6,14},{7,15},{8,0},{9,1},... | collective-permute-start | bytes 4718600 | tf_op jit(solution)/shard_map/ppermute | solution.py:433
  69.9 9.2 %collective-permute-start = (bf16[8,4,24,128]{3,2,1,0:T(8,128)(2,1)S(1)}, bf16[8,4,24,128]{3,2,1,0:T(8,128)(2,1)S(1)}, u32[]{:S(2)}, u32[]{:S(2)}) collective-permute-start(bf16[8,4,24,128]{3,2,1,0:T(8,128)(2,1)S(1)} %get-tuple-element.14.q_ref), channel_id=1, source_target_pairs={{0,32},{32,0},{1,33},{33,1},{2,34},{34,2},{3,35},{35,3},{4,36},{36... | collective-permute-start | bytes 589832 | tf_op jit(solution)/shard_map/ppermute | solution.py:432
  84.2 8.4 %collective-permute-start.2 = (bf16[33,24,128]{2,1,0:T(8,128)(2,1)S(1)}, bf16[33,24,128]{2,1,0:T(8,128)(2,1)S(1)}, u32[]{:S(2)}, u32[]{:S(2)}) collective-permute-start(bf16[33,24,128]{2,1,0:T(8,128)(2,1)S(1)} %get-tuple-element.22), channel_id=1, source_target_pairs={{0,32},{32,0},{1,33},{33,1},{2,34},{34,2},{3,35},{35,3},{4,36},{36... | collective-permute-start | bytes 608264 | tf_op jit(solution)/shard_map/ppermute | solution.py:437
